TPU v7x, 256 devices: a whole 4x4x8 slice. The times are simulated.
256 devices in a mesh: dp: 4 (over x), tm: 32 (over z, y), height: 2 (over core).
Axes of the slice: x: 4, y: 4, z: 8, core: 2. Of those that a mesh axis runs over, the one named last changes fastest.
Arguments:
- clip_frames: bfloat16 [128, 64, 160, 256], P(('dp', 'tm'), 'height'), parts along dimension 0
- frame_of_slot: int32 [128], P('dp'), parts along dimension 0, may hold values from -1 to 16, as said below
- w_spatial: bfloat16 [3, 3, 256, 512], replicated, may hold values from -0.125 to 0.125
- norm_gain: float32 [512], replicated, may hold values from 0.1 to 1.9
- norm_shift: float32 [512], replicated, may hold values from -3 to 3
- w_time: bfloat16 [3, 512, 512], replicated, may hold values from -0.15625 to 0.15625
- time_bias: float32 [512], replicated, may hold values from -3 to 3
Outputs:
- latent: bfloat16 [36, 2, 32, 160, 512], P('dp', 'height', 'tm'), parts along dimension 0
There are 4 independent parts, one for each index of `dp`. A program takes and returns all parts, laid end to end along the dimension named above; an argument that names none is the same for every part. Nothing has to cross between parts.
Inputs may be any that keep to these rules, and one draw needn't show every extreme that they name: `frame_of_slot`: each frame 0 to 16 stands in exactly one slot; every other slot holds -1.
All inputs are finite; a program needn't handle non-finite values.
Results may differ from a plain program's by a relative error of at most 0.0053.
Values may be sent and summed in bfloat16 or wider, within the bound.
A program may use at most 192 MiB of HBM per device.

v0:
```python
import jax
import jax.numpy as jnp
import numpy as np
from jax import lax
from jax.sharding import PartitionSpec as P

GROUPS = 32


def with_halo(block, sides, width):
    for axis, dim in sides:
        count = lax.axis_size(axis)
        forward = [(i, i + 1) for i in range(count - 1)]
        backward = [(target, source) for source, target in forward]
        low = lax.ppermute(
            lax.slice_in_dim(block, block.shape[dim] - width, None, axis=dim), axis, forward
        )
        high = lax.ppermute(lax.slice_in_dim(block, 0, width, axis=dim), axis, backward)
        block = jnp.concatenate([low, block, high], axis=dim)
    return block


def slot_lookup(frame_of_slot, live_frames):
    wanted = jnp.arange(live_frames, dtype=jnp.int32)[:, None]
    places = jnp.arange(frame_of_slot.shape[0], dtype=jnp.int32)[None, :]
    matches = frame_of_slot[None, :] == wanted
    return jnp.sum(jnp.where(matches, places, 0), axis=1)


def spatial_conv(row_padded, w_spatial):
    padded = jnp.pad(row_padded, ((0, 0), (0, 0), (1, 1), (0, 0)))
    row_count = padded.shape[1] - 2
    col_count = padded.shape[2] - 2
    running = None
    for row_tap in range(3):
        for col_tap in range(3):
            window = padded[:, row_tap : row_tap + row_count, col_tap : col_tap + col_count]
            product = jnp.einsum(
                "nrwc,cd->nrwd",
                window,
                w_spatial[row_tap, col_tap],
                preferred_element_type=jnp.float32,
            )
            running = product if running is None else running + product
    return running.astype(jnp.bfloat16)


def normalize(conv_out, weight, all_rows, live_frames, norm_gain, norm_shift):
    cout_width = conv_out.shape[-1]
    per_group = cout_width // GROUPS
    values = conv_out.astype(jnp.float32)
    grouped = values.reshape(conv_out.shape[:-1] + (GROUPS, per_group))
    reduce_axes = tuple(range(grouped.ndim - 2)) + (grouped.ndim - 1,)
    sums = jnp.sum(grouped, axis=reduce_axes) * weight
    squares = jnp.sum(grouped * grouped, axis=reduce_axes) * weight
    sums, squares = lax.psum((sums, squares), ("tm", "height"))
    cell_count = float(live_frames * all_rows * conv_out.shape[2] * per_group)
    group_mean = sums / cell_count
    group_var = squares / cell_count - group_mean * group_mean
    inv_scale = lax.rsqrt(group_var + 1e-06)
    mean_chan = jnp.repeat(group_mean, per_group)
    scale_chan = jnp.repeat(inv_scale, per_group)
    return jax.nn.silu((values - mean_chan) * scale_chan * norm_gain + norm_shift).astype(
        jnp.bfloat16
    )


def time_conv(activated, w_time, time_bias, out_frames):
    running = None
    for time_tap in range(3):
        sources = np.array(
            [max(2 * out_step + time_tap - 2, 0) for out_step in range(out_frames)], np.int32
        )
        picked = jnp.take(activated, jnp.asarray(sources), axis=0)
        product = jnp.einsum(
            "trwc,cd->trwd", picked, w_time[time_tap], preferred_element_type=jnp.float32
        )
        running = product if running is None else running + product
    return (running + time_bias).astype(jnp.bfloat16)


def shards(clip_frames, frame_of_slot, w_spatial, norm_gain, norm_shift, w_time, time_bias):
    tm_count = lax.axis_size("tm")
    height_count = lax.axis_size("height")
    live_frames = tm_count // 2 + 1
    out_frames = (live_frames - 1) // 2 + 1
    frame_slots = slot_lookup(frame_of_slot, live_frames)
    padded = with_halo(clip_frames, (("height", 1),), 1)
    conv_out = spatial_conv(padded, w_spatial)
    own_frame = lax.dynamic_index_in_dim(frame_of_slot, lax.axis_index("tm"), 0, keepdims=False)
    weight = jnp.where(own_frame >= 0, 1.0, 0.0).astype(jnp.float32)
    activated = normalize(
        conv_out, weight, clip_frames.shape[1] * height_count, live_frames, norm_gain, norm_shift
    )
    latent = time_conv(
        jnp.take(
            lax.all_to_all(activated, "tm", split_axis=1, concat_axis=0, tiled=True),
            frame_slots,
            axis=0,
        ),
        w_time,
        time_bias,
        out_frames,
    )
    return latent.reshape(out_frames, 1, latent.shape[1], latent.shape[2], latent.shape[3])


def solution(mesh):
    return jax.shard_map(
        shards,
        mesh=mesh,
        in_specs=(P(("dp", "tm"), "height", None, None), P("dp"), P(), P(), P(), P(), P()),
        out_specs=P("dp", "height", "tm", None, None),
        check_vma=False,
    )
```

profile of v0, /device:TPU:1, one launch (start us, length us, event | category | flops | bytes accessed | tf_op | source)
XLA Modules:
  0.0 364.3 jit_solution(2229044250089898196)
XLA Ops:
  0.0 0.9 fusion.69
  0.9 1.3 collective-permute-start
  2.2 0.0 copy-start.8
  2.3 0.0 copy-start
  2.3 5.4 %collective-permute-start.1 = (bf16[1,1,160,256]{3,2,1,0:T(8,128)(2,1)S(1)}, bf16[1,1,160,256]{3,2,1,0:T(8,128)(2,1)S(1)}, u32[]{:S(2)}, u32[]{:S(2)}) collective-permute-start(bf16[1,1,160,256]{3,2,1,0:T(8,128)(2,1)S(1)} %get-tuple-element.11), channel_id=1, source_target_pairs={{1,0},{3,2},{5,4},{7,6},{9,8},{11,10},{13,12},{15,14},{17,16},{19,... | collective-permute-start | bytes 245768 | tf_op jit(solution)/shard_map/ppermute | solution.py:18
  7.6 7.1 %fusion.31 = f32[32,160,512]{2,1,0:T(8,128)} fusion(bf16[1,32,160,256]{3,2,1,0:T(8,128)(2,1)} %param.12, bf16[3,3,256,512]{3,2,1,0:T(8,128)(2,1)} %param.14), kind=kOutput, calls=%fused_computation.49 | convolution fusion | flops 1342177280 | bytes 13369344 | tf_op jit(solution)/shard_map/nrwc,cd->nrwd/dot_general | solution.py:38
  14.8 0.0 copy-done.8
  14.8 0.0 copy-start.2
  14.8 0.6 dynamic_slice.4
  16.1 0.0 collective-permute-done
  16.1 0.0 collective-permute-done.1
  16.1 0.0 copy-done
  16.2 1.2 fusion.16
  17.4 0.0 copy-done.2
  17.4 5.5 %fusion.18 = f32[32,160,512]{2,1,0:T(8,128)} fusion(bf16[1,34,162,256]{3,2,1,0:T(8,128)(2,1)S(1)} %fusion.16, bf16[3,3,256,512]{3,2,1,0:T(8,128)(2,1)S(1)} %copy-done.2), kind=kOutput, calls=%fused_computation.31 | convolution fusion | flops 1342177280 | bytes 13369344 | tf_op jit(solution)/shard_map/nrwc,cd->nrwd/dot_general | solution.py:38
  22.9 5.3 %fusion.22 = f32[32,160,512]{2,1,0:T(8,128)} fusion(bf16[1,34,162,256]{3,2,1,0:T(8,128)(2,1)S(1)} %fusion.16, bf16[3,3,256,512]{3,2,1,0:T(8,128)(2,1)S(1)} %copy-done.2), kind=kOutput, calls=%fused_computation.36 | convolution fusion | flops 1342177280 | bytes 13369344 | tf_op jit(solution)/shard_map/nrwc,cd->nrwd/dot_general | solution.py:38
  28.3 5.5 %fusion.23 = f32[32,160,512]{2,1,0:T(8,128)} fusion(bf16[1,34,162,256]{3,2,1,0:T(8,128)(2,1)S(1)} %fusion.16, bf16[3,3,256,512]{3,2,1,0:T(8,128)(2,1)S(1)} %copy-done.2), kind=kOutput, calls=%fused_computation.38 | convolution fusion | flops 1342177280 | bytes 13369344 | tf_op jit(solution)/shard_map/nrwc,cd->nrwd/dot_general | solution.py:38
  33.8 5.5 %fusion.24 = f32[32,160,512]{2,1,0:T(8,128)} fusion(bf16[1,34,162,256]{3,2,1,0:T(8,128)(2,1)S(1)} %fusion.16, bf16[3,3,256,512]{3,2,1,0:T(8,128)(2,1)S(1)} %copy-done.2), kind=kOutput, calls=%fused_computation.40 | convolution fusion | flops 1342177280 | bytes 13369344 | tf_op jit(solution)/shard_map/nrwc,cd->nrwd/dot_general | solution.py:38
  39.2 5.4 %fusion.25 = f32[32,160,512]{2,1,0:T(8,128)} fusion(bf16[1,34,162,256]{3,2,1,0:T(8,128)(2,1)S(1)} %fusion.16, bf16[3,3,256,512]{3,2,1,0:T(8,128)(2,1)S(1)} %copy-done.2), kind=kOutput, calls=%fused_computation.42 | convolution fusion | flops 1342177280 | bytes 13369344 | tf_op jit(solution)/shard_map/nrwc,cd->nrwd/dot_general | solution.py:38
  44.6 5.5 %fusion.30 = f32[32,160,512]{2,1,0:T(8,128)} fusion(bf16[1,34,162,256]{3,2,1,0:T(8,128)(2,1)S(1)} %fusion.16, bf16[3,3,256,512]{3,2,1,0:T(8,128)(2,1)S(1)} %copy-done.2), kind=kOutput, calls=%fused_computation.48 | convolution fusion | flops 1342177280 | bytes 13369344 | tf_op jit(solution)/shard_map/nrwc,cd->nrwd/dot_general | solution.py:38
  50.1 5.5 %fusion.27 = f32[32,160,512]{2,1,0:T(8,128)} fusion(bf16[1,32,160,256]{3,2,1,0:T(8,128)(2,1)S(1)} %copy-done, bf16[1,1,160,256]{3,2,1,0:T(8,128)(2,1)S(1)} %collective-permute-done, bf16[3,3,256,512]{3,2,1,0:T(8,128)(2,1)S(1)} %copy-done.2), kind=kOutput, calls=%fused_computation.45 | convolution fusion | flops 1343488000 | bytes 13451264 | tf_op jit(solution)/shard_map/nrwc,cd->nrwd/dot_general | solution.py:38
  55.5 0.0 copy-start.3
  55.5 0.0 copy-start.4
  55.5 29.1 %convert_reduce_fusion = (f32[512]{0:T(512)S(1)}, f32[512]{0:T(512)S(1)}, bf16[32,160,512]{2,1,0:T(8,128)(2,1)}) fusion(f32[32,160,512]{2,1,0:T(8,128)} %fusion.18, bf16[3,3,256,512]{3,2,1,0:T(8,128)(2,1)S(1)} %copy-done.2, bf16[1,1,160,256]{3,2,1,0:T(8,128)(2,1)S(1)} %collective-permute-done.1, bf16[1,32,160,256]{3,2,1,0:T(8,128)(2,1)S(1)} %copy-done, ...), kind=kOutput, calls=%fused_computation.6 | convolution fusion | flops 1377565696 | bytes 92098560 | tf_op jit(solution)/shard_map/nrwc,cd->nrwd/dot_general | solution.py:38
  84.6 0.1 reduce_sum.37
  84.7 0.1 reduce_sum.48
  84.8 0.1 reduce_sum.46
  84.9 0.1 reduce_sum.49
  85.0 125.7 %all-reduce.1 = (f32[32]{0:T(128)S(1)}, f32[32]{0:T(128)S(1)}) all-reduce(f32[32]{0:T(128)S(1)} %get-tuple-element.15, f32[32]{0:T(128)S(1)} %get-tuple-element.16), channel_id=1, replica_groups=mesh['dp'=4,'tm'=32,'height'=2] {'tm','height'}, use_global_device_ids=true, to_apply=%region_6.7 | all-reduce | flops 64 | bytes 512 | tf_op jit(solution)/shard_map/psum | solution.py:56
  210.8 0.1 broadcast_in_dim.47
  210.8 0.1 mul.50
  210.9 0.1 broadcast_in_dim.46
  211.0 0.1 sub.14
  211.1 0.0 copy-done.3
  211.1 0.0 copy-done.4
  211.1 7.3 %fusion.11 = bf16[1,32,160,512]{3,2,0,1:T(8,128)(2,1)} fusion(bf16[32,160,512]{2,1,0:T(8,128)(2,1)} %get-tuple-element.14, f32[512]{0:T(512)S(1)} %copy-done.3, f32[512]{0:T(512)S(1)} %copy-done.4, f32[512]{0:T(512)S(1)} %mul.50, f32[512]{0:T(512)S(1)} %sub.14), kind=kLoop, calls=%fused_computation.21 | loop fusion | flops 26214400 | bytes 10493952 | tf_op jit(solution)/shard_map/convert_element_type | solution.py:63
  218.4 0.0 copy-start.7
  218.4 0.0 copy-start.6
  218.4 6.5 %all-to-all-start = ((bf16[1,32,160,512]{3,2,0,1:T(8,128)(2,1)}), bf16[1,32,160,512]{3,2,0,1:T(8,128)(2,1)}, u32[]{:S(2)}, u32[]{:S(2)}) async-start(bf16[1,32,160,512]{3,2,0,1:T(8,128)(2,1)} %fusion.11), calls=%async_computation | async-start | bytes 10485760 | tf_op jit(solution)/shard_map/all_to_all | solution.py:97
  224.9 0.1 select_reduce_fusion
  225.0 0.0 copy-done.7
  225.1 0.0 copy-done.6
  225.1 113.2 %all-to-all-done = bf16[1,32,160,512]{3,2,0,1:T(8,128)(2,1)} async-done(((bf16[1,32,160,512]{3,2,0,1:T(8,128)(2,1)}), bf16[1,32,160,512]{3,2,0,1:T(8,128)(2,1)}, u32[]{:S(2)}, u32[]{:S(2)}) %all-to-all-start) | async-done | bytes 5242912 | tf_op jit(solution)/shard_map/all_to_all | solution.py:97
  338.3 5.0 %gather_fusion = bf16[17,160,512]{2,1,0:T(8,128)(2,1)} fusion(bf16[32,160,512]{2,1,0:T(8,128)(2,1)} %bitcast.30, s32[1024]{0:T(1024)S(1)} %pad_clamp_fusion.3), kind=kCustom, calls=%fused_computation.3 | custom fusion | bytes 5570628 | tf_op jit(solution)/shard_map/jit(_take)/gather | solution.py:96
  343.3 2.1 fusion.17
  345.4 1.9 gather_fusion.2
  347.3 1.9 gather_fusion.1
  349.2 0.0 copy-start.1
  349.2 4.1 %fusion.40 = f32[9,160,512]{2,1,0:T(8,128)} fusion(bf16[9,160,512]{2,1,0:T(8,128)(2,1)} %gather_fusion.2, bf16[3,512,512]{2,1,0:T(8,128)(2,1)} %param.17), kind=kOutput, calls=%fused_computation.57 | convolution fusion | flops 754974720 | bytes 4947968 | tf_op jit(solution)/shard_map/trwc,cd->trwd/dot_general | solution.py:75
  353.3 0.0 copy-done.1
  353.3 0.0 copy-start.5
  353.3 3.6 fusion.42
  356.9 1.9 gather_fusion.3
  358.8 0.0 copy-done.5
  358.8 5.5 %fusion.35 = bf16[9,1,1,160,512]{4,3,2,1,0:T(8,128)(2,1)} fusion(f32[512]{0:T(512)S(1)} %copy-done.5, bf16[9,160,512]{2,1,0:T(8,128)(2,1)} %gather_fusion.3, pred[9]{0:T(512)(128)(4,1)S(1)} %compare_and_fusion, f32[9,160,512]{2,1,0:T(8,128)} %fusion.42, f32[9,160,512]{2,1,0:T(8,128)} %fusion.40, bf16[3,512,512]{2,1,0:T(8,128)(2,1)} %param.17), kind=kOutput, calls=%fused_computation.54 | convolution fusion | flops 758661120 | bytes 9373705 | tf_op jit(solution)/shard_map/trwc,cd->trwd/dot_general | solution.py:75
  (10 shorter events, 0.1 us)
Async XLA Ops:
  0.9 15.2 %collective-permute-start = (bf16[1,1,160,256]{3,2,1,0:T(8,128)(2,1)S(1)}, bf16[1,1,160,256]{3,2,1,0:T(8,128)(2,1)S(1)}, u32[]{:S(2)}, u32[]{:S(2)}) collective-permute-start(bf16[1,1,160,256]{3,2,1,0:T(8,128)(2,1)S(1)} %get-tuple-element.10), channel_id=1, source_target_pairs={{0,1},{2,3},{4,5},{6,7},{8,9},{10,11},{12,13},{14,15},{16,17},{18,... | collective-permute-start | bytes 245768 | tf_op jit(solution)/shard_map/ppermute | solution.py:15
  2.2 12.5 %copy-start.8 = (s32[32]{0:T(128)S(1)}, s32[32]{0:T(128)}, u32[]{:S(2)}) copy-start(s32[32]{0:T(128)} %param.13) | copy-start | bytes 388
  2.3 13.9 %copy-start = (bf16[1,32,160,256]{3,2,1,0:T(8,128)(2,1)S(1)}, bf16[1,32,160,256]{3,2,1,0:T(8,128)(2,1)}, u32[]{:S(2)}) copy-start(bf16[1,32,160,256]{3,2,1,0:T(8,128)(2,1)} %param.12) | copy-start | bytes 7864324
  2.3 13.9 %collective-permute-start.1 = (bf16[1,1,160,256]{3,2,1,0:T(8,128)(2,1)S(1)}, bf16[1,1,160,256]{3,2,1,0:T(8,128)(2,1)S(1)}, u32[]{:S(2)}, u32[]{:S(2)}) collective-permute-start(bf16[1,1,160,256]{3,2,1,0:T(8,128)(2,1)S(1)} %get-tuple-element.11), channel_id=1, source_target_pairs={{1,0},{3,2},{5,4},{7,6},{9,8},{11,10},{13,12},{15,14},{17,16},{19,... | collective-permute-start | bytes 245768 | tf_op jit(solution)/shard_map/ppermute | solution.py:18
  14.8 2.6 copy-start.2
  55.5 155.5 %copy-start.3 = (f32[512]{0:T(512)S(1)}, f32[512]{0:T(512)}, u32[]{:S(2)}) copy-start(f32[512]{0:T(512)} %param.16) | copy-start | bytes 6148
  55.5 155.6 %copy-start.4 = (f32[512]{0:T(512)S(1)}, f32[512]{0:T(512)}, u32[]{:S(2)}) copy-start(f32[512]{0:T(512)} %param.15) | copy-start | bytes 6148
  218.4 6.7 %copy-start.7 = (s32[9]{0:T(128)S(1)}, s32[9]{0:T(128)}, u32[]{:S(2)}) copy-start(s32[9]{0:T(128)} %constant.89) | copy-start | bytes 112
  218.4 6.7 %copy-start.6 = (s32[9]{0:T(128)S(1)}, s32[9]{0:T(128)}, u32[]{:S(2)}) copy-start(s32[9]{0:T(128)} %constant.88) | copy-start | bytes 112
  218.4 119.9 %all-to-all-start = ((bf16[1,32,160,512]{3,2,0,1:T(8,128)(2,1)}), bf16[1,32,160,512]{3,2,0,1:T(8,128)(2,1)}, u32[]{:S(2)}, u32[]{:S(2)}) async-start(bf16[1,32,160,512]{3,2,0,1:T(8,128)(2,1)} %fusion.11), calls=%async_computation | async-start | bytes 10485760 | tf_op jit(solution)/shard_map/all_to_all | solution.py:97
  349.2 4.1 %copy-start.1 = (bf16[9,160,512]{2,1,0:T(8,128)(2,1)S(1)}, bf16[9,160,512]{2,1,0:T(8,128)(2,1)}, u32[]{:S(2)}) copy-start(bf16[9,160,512]{2,1,0:T(8,128)(2,1)} %gather_fusion.1) | copy-start | bytes 4423684
  353.3 5.5 %copy-start.5 = (f32[512]{0:T(512)S(1)}, f32[512]{0:T(512)}, u32[]{:S(2)}) copy-start(f32[512]{0:T(512)} %param.18) | copy-start | bytes 6148
where the time goes:
time: 368 us; the launch traced here: 364 us
  blocking collectives  126 us (34%)
  waiting for transfers between devices  113 us (31%)
  matrix products  87.5 us (24%)
  starting transfers between devices  13.2 us (4%)
  local copies, waits for them, and re-layouts  12.7 us (3%)
  other arithmetic  11 us (3%)
    psum x1, blocking collectives, normalize(): sums, squares = lax.psum((sums, squares), ('tm', 'height'))  126 us
    all_to_all x1, waiting for transfers between devices, shards(): lax.all_to_all(activated, 'tm', split_axis=1, concat_axis=0, tiled=True)  113 us
    dot_general x9, matrix products, spatial_conv(): jnp.einsum('nrwc,cd->nrwd', window, w_spatial[row_tap, col_tap], preferre...  74.3 us
    dot_general x3, matrix products, time_conv(): jnp.einsum('trwc,cd->trwd', picked, w_time[time_tap], preferred_element_t...  13.2 us
  transfers between devices with their start and end apart: 3, of which 1 were waited for; matrix products, arithmetic and copies ran while one was open for 2% of the time, Pallas kernels for 0%

commit v1 on v0

--- a/solution.py
+++ b/solution.py
@@ -28,38 +28,34 @@
 
 
 def spatial_conv(row_padded, w_spatial):
-    padded = jnp.pad(row_padded, ((0, 0), (0, 0), (1, 1), (0, 0)))
-    row_count = padded.shape[1] - 2
-    col_count = padded.shape[2] - 2
-    running = None
-    for row_tap in range(3):
-        for col_tap in range(3):
-            window = padded[:, row_tap : row_tap + row_count, col_tap : col_tap + col_count]
-            product = jnp.einsum(
-                "nrwc,cd->nrwd",
-                window,
-                w_spatial[row_tap, col_tap],
-                preferred_element_type=jnp.float32,
-            )
-            running = product if running is None else running + product
-    return running.astype(jnp.bfloat16)
+    out = lax.conv_general_dilated(
+        row_padded,
+        w_spatial,
+        window_strides=(1, 1),
+        padding=((0, 0), (1, 1)),
+        dimension_numbers=("NHWC", "HWIO", "NHWC"),
+        preferred_element_type=jnp.float32,
+    )
+    return out.astype(jnp.bfloat16)
 
 
-def normalize(conv_out, weight, all_rows, live_frames, norm_gain, norm_shift):
+def group_stats(conv_out, weight):
     cout_width = conv_out.shape[-1]
     per_group = cout_width // GROUPS
-    values = conv_out.astype(jnp.float32)
-    grouped = values.reshape(conv_out.shape[:-1] + (GROUPS, per_group))
-    reduce_axes = tuple(range(grouped.ndim - 2)) + (grouped.ndim - 1,)
-    sums = jnp.sum(grouped, axis=reduce_axes) * weight
-    squares = jnp.sum(grouped * grouped, axis=reduce_axes) * weight
-    sums, squares = lax.psum((sums, squares), ("tm", "height"))
-    cell_count = float(live_frames * all_rows * conv_out.shape[2] * per_group)
+    values = conv_out.astype(jnp.float32).reshape(-1, cout_width)
+    sums = jnp.sum(values, axis=0).reshape(GROUPS, per_group).sum(axis=1) * weight
+    squares = jnp.sum(values * values, axis=0).reshape(GROUPS, per_group).sum(axis=1) * weight
+    return sums, squares
+
+
+def normalize(conv_out, sums, squares, cell_count, norm_gain, norm_shift):
+    per_group = conv_out.shape[-1] // GROUPS
     group_mean = sums / cell_count
     group_var = squares / cell_count - group_mean * group_mean
     inv_scale = lax.rsqrt(group_var + 1e-06)
     mean_chan = jnp.repeat(group_mean, per_group)
     scale_chan = jnp.repeat(inv_scale, per_group)
+    values = conv_out.astype(jnp.float32)
     return jax.nn.silu((values - mean_chan) * scale_chan * norm_gain + norm_shift).astype(
         jnp.bfloat16
     )
@@ -87,21 +83,18 @@
     frame_slots = slot_lookup(frame_of_slot, live_frames)
     padded = with_halo(clip_frames, (("height", 1),), 1)
     conv_out = spatial_conv(padded, w_spatial)
+    exchanged = lax.all_to_all(conv_out, "tm", split_axis=1, concat_axis=0, tiled=True)
     own_frame = lax.dynamic_index_in_dim(frame_of_slot, lax.axis_index("tm"), 0, keepdims=False)
     weight = jnp.where(own_frame >= 0, 1.0, 0.0).astype(jnp.float32)
-    activated = normalize(
-        conv_out, weight, clip_frames.shape[1] * height_count, live_frames, norm_gain, norm_shift
+    sums, squares = group_stats(conv_out, weight)
+    sums, squares = lax.psum((sums, squares), ("tm", "height"))
+    per_group = conv_out.shape[-1] // GROUPS
+    cell_count = float(
+        live_frames * clip_frames.shape[1] * height_count * conv_out.shape[2] * per_group
     )
-    latent = time_conv(
-        jnp.take(
-            lax.all_to_all(activated, "tm", split_axis=1, concat_axis=0, tiled=True),
-            frame_slots,
-            axis=0,
-        ),
-        w_time,
-        time_bias,
-        out_frames,
-    )
+    live = jnp.take(exchanged, frame_slots, axis=0)
+    activated = normalize(live, sums, squares, cell_count, norm_gain, norm_shift)
+    latent = time_conv(activated, w_time, time_bias, out_frames)
     return latent.reshape(out_frames, 1, latent.shape[1], latent.shape[2], latent.shape[3])
 
 

time: 368 us -> 322 us (0.88)
  waiting for transfers between devices: 113 us -> 0.9 us
  blocking collectives: 126 us -> 227 us
  matrix products: 87.5 us -> 28.4 us
  local copies, waits for them, and re-layouts: 12.7 us -> 38.3 us
  other arithmetic: 11 us -> 7.27 us
    all_to_all x1, waiting for transfers between devices: 113 us -> 0.01 us  [shards(): lax.all_to_all(conv_out, 'tm', split_axis=1, concat_axis=0, tiled=True)]
    psum x1, blocking collectives: 126 us -> 227 us  [shards(): sums, squares = lax.psum((sums, squares), ('tm', 'height'))]
    dot_general x9 -> x0, matrix products: 74.3 us -> none  [spatial_conv(): jnp.einsum('nrwc,cd->nrwd', window, w_spatial[row_tap, col_tap], preferre...]
    conv_general_dilated x0 -> x1, matrix products: none -> 15.2 us  [spatial_conv(): lax.conv_general_dilated(row_padded, w_spatial, window_strides=(1, 1), pa...]
    conv_general_dilated x0 -> x3, local copies, waits for them, and re-layouts: none -> 8.44 us  [spatial_conv(): lax.conv_general_dilated(row_padded, w_spatial, window_strides=(1, 1), pa...]
    convert_element_type x0 -> x3, local copies, waits for them, and re-layouts: none -> 8.14 us  [spatial_conv(): return out.astype(jnp.bfloat16)]
    convert_element_type x1 -> x0, other arithmetic: 7.29 us -> none  [normalize(): jax.nn.silu((values - mean_chan) * scale_chan * norm_gain + norm_shift)]
    gather x3, local copies, waits for them, and re-layouts: 5.65 us -> 11 us  [time_conv(): picked = jnp.take(activated, jnp.asarray(sources), axis=0)]
  transfers between devices with their start and end apart: 3 -> 3, of which waited for: 1 -> 1; matrix products, arithmetic and copies ran while one was open for 2% -> 0% of each run, Pallas kernels for 0% -> 0%
where the time goes in v1:
time: 322 us; the launch traced here: 319 us
  blocking collectives  227 us (70%)
  local copies, waits for them, and re-layouts  38.3 us (12%)
  matrix products  28.4 us (9%)
  starting transfers between devices  16.6 us (5%)
  other arithmetic  7.27 us (2%)
    psum x1, blocking collectives, shards(): sums, squares = lax.psum((sums, squares), ('tm', 'height'))  227 us
    conv_general_dilated x1, matrix products, spatial_conv(): lax.conv_general_dilated(row_padded, w_spatial, window_strides=(1, 1), pa...  15.2 us
    dot_general x3, matrix products, time_conv(): jnp.einsum('trwc,cd->trwd', picked, w_time[time_tap], preferred_element_t...  13.2 us
    gather x3, local copies, waits for them, and re-layouts, time_conv(): picked = jnp.take(activated, jnp.asarray(sources), axis=0)  11 us
    all_to_all x1, starting transfers between devices, shards(): lax.all_to_all(conv_out, 'tm', split_axis=1, concat_axis=0, tiled=True)  10.2 us
    conv_general_dilated x3, local copies, waits for them, and re-layouts, spatial_conv(): lax.conv_general_dilated(row_padded, w_spatial, window_strides=(1, 1), pa...  8.44 us
    convert_element_type x3, local copies, waits for them, and re-layouts, spatial_conv(): return out.astype(jnp.bfloat16)  8.14 us
  transfers between devices with their start and end apart: 3, of which 1 were waited for; matrix products, arithmetic and copies ran while one was open for 0% of the time, Pallas kernels for 0%

profile of v1, /device:TPU:1, one launch (start us, length us, event | category | flops | bytes accessed | tf_op | source)
XLA Modules:
  0.0 319.4 jit_solution(5733083394259424839)
XLA Ops:
  0.0 0.0 copy-start
  0.0 1.1 fusion.31
  1.1 1.3 collective-permute-start
  2.4 5.1 %collective-permute-start.1 = (bf16[1,1,160,256]{3,2,1,0:T(8,128)(2,1)S(1)}, bf16[1,1,160,256]{3,2,1,0:T(8,128)(2,1)S(1)}, u32[]{:S(2)}, u32[]{:S(2)}) collective-permute-start(bf16[1,1,160,256]{3,2,1,0:T(8,128)(2,1)S(1)} %get-tuple-element.11), channel_id=1, source_target_pairs={{1,0},{3,2},{5,4},{7,6},{9,8},{11,10},{13,12},{15,14},{17,16},{19,... | collective-permute-start | bytes 245768 | tf_op jit(solution)/shard_map/ppermute | solution.py:18
  7.5 0.0 collective-permute-done
  7.5 0.9 collective-permute-done.1
  8.4 2.1 maximum_bitcast_fusion
  10.5 3.5 %pad = bf16[34,1,168,256]{3,2,0,1:T(8,128)(2,1)} pad(bf16[34,1,160,256]{3,2,0,1:T(8,128)(2,1)S(1)} %maximum_bitcast_fusion, bf16[]{:T(256)} %constant.66), padding=0_0x0_0x1_7x0_0 | pad | bytes 5709826 | tf_op jit(solution)/shard_map/concatenate | solution.py:19
  14.0 5.6 %reshape.142 = bf16[34,1,8,21,256]{4,3,2,0,1:T(8,128)(2,1)} reshape(bf16[34,1,168,256]{3,2,0,1:T(8,128)(2,1)} %pad) | data formatting | bytes 5849088 | tf_op jit(solution)/shard_map/conv_general_dilated | solution.py:31
  19.6 0.0 copy-start.8
  19.6 2.8 copy.30
  22.4 0.1 slice.30
  22.5 0.0 copy-done
  22.5 0.0 copy-done.8
  22.5 15.2 %fusion = (f32[512]{0:T(512)S(1)}, f32[512]{0:T(512)S(1)}, bf16[32,8,21,512]{3,1,2,0:T(8,128)(2,1)S(1)}) fusion(pred[8,21]{0,1:T(8,128)(4,1)S(1)} %copy-done.8, bf16[3,3,256,512]{3,2,1,0:T(8,128)(2,1)S(1)} %copy-done, bf16[34,1,7,2,256]{4,2,3,0,1:T(8,128)(2,1)S(1)} %slice.30, bf16[34,1,8,21,256]{4,2,3,0,1:T(8,128)(2,1)S(1)} %copy.30), kind=kOutput, calls=%fused_computation.6 | convolution fusion | flops 12715204608 | bytes 11036840 | tf_op jit(solution)/shard_map/conv_general_dilated | solution.py:31
  37.7 2.0 copy.31
  39.7 0.8 slice_bitcast_fusion
  40.5 5.3 %copy.32 = bf16[1,32,160,512]{3,2,0,1:T(8,128)(2,1)} copy(bf16[1,32,160,512]{3,1,2,0:T(8,128)(2,1)S(1)} %slice_bitcast_fusion) | data formatting | bytes 10485760 | tf_op jit(solution)/shard_map/convert_element_type | solution.py:39
  45.9 0.0 copy-start.7
  45.9 0.0 copy-start.6
  45.9 0.0 copy-start.5
  45.9 10.2 %all-to-all-start = ((bf16[1,32,160,512]{3,2,0,1:T(8,128)(2,1)}), bf16[1,32,160,512]{3,2,0,1:T(8,128)(2,1)}, u32[]{:S(2)}, u32[]{:S(2)}) async-start(bf16[1,32,160,512]{3,2,0,1:T(8,128)(2,1)} %copy.32), calls=%async_computation | async-start | bytes 10485760 | tf_op jit(solution)/shard_map/all_to_all | solution.py:86
  56.1 0.0 copy-done.7
  56.1 0.6 dynamic_slice.4
  57.3 0.1 select_reduce_fusion
  57.5 0.0 copy-done.6
  57.5 0.0 copy-done.5
  57.6 0.1 reshape.134
  57.6 0.1 reshape.135
  57.7 0.1 reduce_sum.50
  57.8 0.1 reduce_sum.52
  58.0 227.0 %all-reduce = (f32[32]{0:T(128)S(1)}, f32[32]{0:T(128)S(1)}) all-reduce(f32[32]{0:T(128)S(1)} %get-tuple-element.15, f32[32]{0:T(128)S(1)} %get-tuple-element.16), channel_id=1, replica_groups=mesh['dp'=4,'tm'=32,'height'=2] {'tm','height'}, use_global_device_ids=true, to_apply=%region_6.7 | all-reduce | flops 64 | bytes 512 | tf_op jit(solution)/shard_map/psum | solution.py:90
  285.0 0.1 broadcast_in_dim.48
  285.1 0.1 mul.68
  285.2 0.1 broadcast_in_dim.47
  285.2 0.1 sub.21
  285.3 0.0 all-to-all-done
  285.3 0.0 copy-start.2
  285.3 0.0 copy-start.3
  285.3 5.0 %gather_fusion = bf16[17,160,512]{2,1,0:T(8,128)(2,1)} fusion(bf16[32,160,512]{2,1,0:T(8,128)(2,1)} %bitcast.4, s32[1024]{0:T(1024)S(1)} %pad_clamp_fusion.3), kind=kCustom, calls=%fused_computation.3 | custom fusion | bytes 5570628 | tf_op jit(solution)/shard_map/jit(_take)/gather | solution.py:95
  290.4 0.0 copy-done.2
  290.4 0.0 copy-done.3
  290.4 4.8 %fusion.10 = bf16[17,160,512]{2,1,0:T(8,128)(2,1)} fusion(bf16[17,160,512]{2,1,0:T(8,128)(2,1)} %gather_fusion, f32[512]{0:T(512)S(1)} %copy-done.2, f32[512]{0:T(512)S(1)} %copy-done.3, f32[512]{0:T(512)S(1)} %mul.68, f32[512]{0:T(512)S(1)} %sub.21, pred[17]{0:T(512)(128)(4,1)S(1)} %compare_and_fusion.1), kind=kLoop, calls=%fused_computation.20 | loop fusion | flops 15319040 | bytes 5578769 | tf_op jit(solution)/shard_map/jit(_take)/Arg_0.15 | solution.py:70
  295.1 3.7 %gather_fusion.2 = bf16[9,160,512]{2,1,0:T(8,128)(2,1)} fusion(bf16[17,160,512]{2,1,0:T(8,128)(2,1)} %fusion.10, s32[1024]{0:T(1024)S(1)} %pad_clamp_fusion.1), kind=kCustom, calls=%fused_computation.1.clone | custom fusion | bytes 2949156 | tf_op jit(solution)/shard_map/jit(_take)/gather | solution.py:70
  298.8 3.6 %gather_fusion.1 = bf16[9,160,512]{2,1,0:T(8,128)(2,1)} fusion(bf16[17,160,512]{2,1,0:T(8,128)(2,1)} %fusion.10, s32[1024]{0:T(1024)S(1)} %pad_clamp_fusion.2), kind=kCustom, calls=%fused_computation.clone | custom fusion | bytes 2949156 | tf_op jit(solution)/shard_map/jit(_take)/gather | solution.py:70
  302.5 0.0 copy-start.1
  302.5 4.1 %fusion.19 = f32[9,160,512]{2,1,0:T(8,128)} fusion(bf16[9,160,512]{2,1,0:T(8,128)(2,1)} %gather_fusion.2, bf16[3,512,512]{2,1,0:T(8,128)(2,1)} %param.17), kind=kOutput, calls=%fused_computation.30 | convolution fusion | flops 754974720 | bytes 4947968 | tf_op jit(solution)/shard_map/trwc,cd->trwd/dot_general | solution.py:71
  306.6 0.0 copy-done.1
  306.6 0.0 copy-start.4
  306.6 3.6 %fusion.21 = f32[9,160,512]{2,1,0:T(8,128)} fusion(bf16[9,160,512]{2,1,0:T(8,128)(2,1)S(1)} %copy-done.1, bf16[3,512,512]{2,1,0:T(8,128)(2,1)} %param.17), kind=kOutput, calls=%fused_computation.32 | convolution fusion | flops 754974720 | bytes 4947968 | tf_op jit(solution)/shard_map/trwc,cd->trwd/dot_general | solution.py:71
  310.2 3.7 %gather_fusion.3 = bf16[9,160,512]{2,1,0:T(8,128)(2,1)} fusion(bf16[17,160,512]{2,1,0:T(8,128)(2,1)} %fusion.10, s32[1024]{0:T(1024)S(1)} %pad_clamp_fusion), kind=kCustom, calls=%fused_computation.2.clone | custom fusion | bytes 2949156 | tf_op jit(solution)/shard_map/jit(_take)/gather | solution.py:70
  313.9 0.0 copy-done.4
  313.9 5.5 %fusion.14 = bf16[9,1,1,160,512]{4,3,2,1,0:T(8,128)(2,1)} fusion(f32[512]{0:T(512)S(1)} %copy-done.4, bf16[9,160,512]{2,1,0:T(8,128)(2,1)} %gather_fusion.3, pred[9]{0:T(512)(128)(4,1)S(1)} %compare_and_fusion, f32[9,160,512]{2,1,0:T(8,128)} %fusion.21, f32[9,160,512]{2,1,0:T(8,128)} %fusion.19, bf16[3,512,512]{2,1,0:T(8,128)(2,1)} %param.17), kind=kOutput, calls=%fused_computation.27 | convolution fusion | flops 758661120 | bytes 9373705 | tf_op jit(solution)/shard_map/trwc,cd->trwd/dot_general | solution.py:71
  (10 shorter events, 0.1 us)
Async XLA Ops:
  0.0 22.5 %copy-start = (bf16[3,3,256,512]{3,2,1,0:T(8,128)(2,1)S(1)}, bf16[3,3,256,512]{3,2,1,0:T(8,128)(2,1)}, u32[]{:S(2)}) copy-start(bf16[3,3,256,512]{3,2,1,0:T(8,128)(2,1)} %param.14) | copy-start | bytes 7077892
  1.1 6.4 %collective-permute-start = (bf16[1,1,160,256]{3,2,1,0:T(8,128)(2,1)S(1)}, bf16[1,1,160,256]{3,2,1,0:T(8,128)(2,1)S(1)}, u32[]{:S(2)}, u32[]{:S(2)}) collective-permute-start(bf16[1,1,160,256]{3,2,1,0:T(8,128)(2,1)S(1)} %get-tuple-element.10), channel_id=1, source_target_pairs={{0,1},{2,3},{4,5},{6,7},{8,9},{10,11},{12,13},{14,15},{16,17},{18,... | collective-permute-start | bytes 245768 | tf_op jit(solution)/shard_map/ppermute | solution.py:15
  2.4 6.0 %collective-permute-start.1 = (bf16[1,1,160,256]{3,2,1,0:T(8,128)(2,1)S(1)}, bf16[1,1,160,256]{3,2,1,0:T(8,128)(2,1)S(1)}, u32[]{:S(2)}, u32[]{:S(2)}) collective-permute-start(bf16[1,1,160,256]{3,2,1,0:T(8,128)(2,1)S(1)} %get-tuple-element.11), channel_id=1, source_target_pairs={{1,0},{3,2},{5,4},{7,6},{9,8},{11,10},{13,12},{15,14},{17,16},{19,... | collective-permute-start | bytes 245768 | tf_op jit(solution)/shard_map/ppermute | solution.py:18
  19.6 2.9 copy-start.8
  45.9 10.2 %copy-start.7 = (s32[32]{0:T(128)S(1)}, s32[32]{0:T(128)}, u32[]{:S(2)}) copy-start(s32[32]{0:T(128)} %param.13) | copy-start | bytes 388
  45.9 11.6 %copy-start.6 = (s32[9]{0:T(128)S(1)}, s32[9]{0:T(128)}, u32[]{:S(2)}) copy-start(s32[9]{0:T(128)} %constant.94) | copy-start | bytes 112
  45.9 11.6 %copy-start.5 = (s32[9]{0:T(128)S(1)}, s32[9]{0:T(128)}, u32[]{:S(2)}) copy-start(s32[9]{0:T(128)} %constant.93) | copy-start | bytes 112
  45.9 239.5 %all-to-all-start = ((bf16[1,32,160,512]{3,2,0,1:T(8,128)(2,1)}), bf16[1,32,160,512]{3,2,0,1:T(8,128)(2,1)}, u32[]{:S(2)}, u32[]{:S(2)}) async-start(bf16[1,32,160,512]{3,2,0,1:T(8,128)(2,1)} %copy.32), calls=%async_computation | async-start | bytes 10485760 | tf_op jit(solution)/shard_map/all_to_all | solution.py:86
  285.3 5.1 %copy-start.2 = (f32[512]{0:T(512)S(1)}, f32[512]{0:T(512)}, u32[]{:S(2)}) copy-start(f32[512]{0:T(512)} %param.16) | copy-start | bytes 6148
  285.3 5.0 %copy-start.3 = (f32[512]{0:T(512)S(1)}, f32[512]{0:T(512)}, u32[]{:S(2)}) copy-start(f32[512]{0:T(512)} %param.15) | copy-start | bytes 6148
  302.5 4.1 %copy-start.1 = (bf16[9,160,512]{2,1,0:T(8,128)(2,1)S(1)}, bf16[9,160,512]{2,1,0:T(8,128)(2,1)}, u32[]{:S(2)}) copy-start(bf16[9,160,512]{2,1,0:T(8,128)(2,1)} %gather_fusion.1) | copy-start | bytes 4423684
  306.6 7.3 %copy-start.4 = (f32[512]{0:T(512)S(1)}, f32[512]{0:T(512)}, u32[]{:S(2)}) copy-start(f32[512]{0:T(512)} %param.18) | copy-start | bytes 6148

commit v2 on v1

--- a/solution.py
+++ b/solution.py
@@ -62,17 +62,29 @@
 
 
 def time_conv(activated, w_time, time_bias, out_frames):
-    running = None
-    for time_tap in range(3):
-        sources = np.array(
-            [max(2 * out_step + time_tap - 2, 0) for out_step in range(out_frames)], np.int32
-        )
-        picked = jnp.take(activated, jnp.asarray(sources), axis=0)
-        product = jnp.einsum(
-            "trwc,cd->trwd", picked, w_time[time_tap], preferred_element_type=jnp.float32
-        )
-        running = product if running is None else running + product
-    return (running + time_bias).astype(jnp.bfloat16)
+    first = activated[0:1]
+    even = activated[0::2][:out_frames]
+    odd = activated[1::2][: out_frames - 1]
+    taps = [
+        jnp.concatenate([first, even[: out_frames - 1]], axis=0),
+        jnp.concatenate([first, odd], axis=0),
+        even,
+    ]
+    stacked = jnp.concatenate(taps, axis=-1)
+    weights = w_time.reshape(-1, w_time.shape[-1])
+    product = jnp.einsum("trwc,cd->trwd", stacked, weights, preferred_element_type=jnp.float32)
+    return (product + time_bias).astype(jnp.bfloat16)
+
+
+def encode_stats(stats):
+    high = stats.astype(jnp.bfloat16)
+    low = (stats - high.astype(jnp.float32)).astype(jnp.bfloat16)
+    return jnp.concatenate([high, low])
+
+
+def decode_stats(coded, width):
+    values = coded.astype(jnp.float32)
+    return jnp.sum(values[:, :width], axis=0) + jnp.sum(values[:, width : 2 * width], axis=0)
 
 
 def shards(clip_frames, frame_of_slot, w_spatial, norm_gain, norm_shift, w_time, time_bias):
@@ -83,11 +95,19 @@
     frame_slots = slot_lookup(frame_of_slot, live_frames)
     padded = with_halo(clip_frames, (("height", 1),), 1)
     conv_out = spatial_conv(padded, w_spatial)
-    exchanged = lax.all_to_all(conv_out, "tm", split_axis=1, concat_axis=0, tiled=True)
     own_frame = lax.dynamic_index_in_dim(frame_of_slot, lax.axis_index("tm"), 0, keepdims=False)
     weight = jnp.where(own_frame >= 0, 1.0, 0.0).astype(jnp.float32)
     sums, squares = group_stats(conv_out, weight)
-    sums, squares = lax.psum((sums, squares), ("tm", "height"))
+    coded = encode_stats(jnp.concatenate([sums, squares]))
+    column = jnp.zeros((conv_out.shape[-1],), jnp.bfloat16).at[: coded.shape[0]].set(coded)
+    column = jnp.broadcast_to(column, (1, conv_out.shape[1], 1, conv_out.shape[-1]))
+    payload = jnp.concatenate([conv_out, column], axis=2)
+    received = lax.all_to_all(payload, "tm", split_axis=1, concat_axis=0, tiled=True)
+    exchanged = received[:, :, : conv_out.shape[2]]
+    partial = decode_stats(received[:, 0, conv_out.shape[2], : coded.shape[0]], 2 * GROUPS)
+    other = lax.ppermute(partial, "height", [(0, 1), (1, 0)])
+    totals = partial + other
+    sums, squares = totals[:GROUPS], totals[GROUPS:]
     per_group = conv_out.shape[-1] // GROUPS
     cell_count = float(
         live_frames * clip_frames.shape[1] * height_count * conv_out.shape[2] * per_group

time: 322 us -> 213 us (0.66)
  blocking collectives: 227 us -> 0 us
  waiting for transfers between devices: 0.9 us -> 123 us
  matrix products: 28.4 us -> 19.8 us
  starting transfers between devices: 16.6 us -> 20.5 us
    psum x1 -> x0, blocking collectives: 227 us -> none  [shards(): sums, squares = lax.psum((sums, squares), ('tm', 'height'))]
    all_to_all x1, waiting for transfers between devices: 0.01 us -> 123 us  [shards(): lax.all_to_all(payload, 'tm', split_axis=1, concat_axis=0, tiled=True)]
    gather x3 -> x0, local copies, waits for them, and re-layouts: 11 us -> none  [time_conv(): picked = jnp.take(activated, jnp.asarray(sources), axis=0)]
    dot_general x3 -> x1, matrix products: 13.2 us -> 3.68 us  [time_conv(): jnp.einsum('trwc,cd->trwd', stacked, weights, preferred_element_type=jnp....]
    slice x0 -> x5, local copies, waits for them, and re-layouts: none -> 5.66 us  [the longest x1 5.38 us: shards(): exchanged = received[:, :, :conv_out.shape[2]]]
    concatenate x0 -> x1, local copies, waits for them, and re-layouts: none -> 5.42 us  [shards(): payload = jnp.concatenate([conv_out, column], axis=2)]
    another operation x1 -> x0, other arithmetic: 4.76 us -> none  [time_conv(): picked = jnp.take(activated, jnp.asarray(sources), axis=0)]
    convert_element_type x0 -> x4, other arithmetic: none -> 4.63 us  [the longest x1 3.62 us: normalize(): jax.nn.silu((values - mean_chan) * scale_chan * norm_gain + norm_shift)]
  transfers between devices with their start and end apart: 3 -> 4, of which waited for: 1 -> 1; matrix products, arithmetic and copies ran while one was open for 0% -> 6% of each run, Pallas kernels for 0% -> 0%
where the time goes in v2:
time: 213 us; the launch traced here: 209 us
  waiting for transfers between devices  123 us (58%)
  local copies, waits for them, and re-layouts  37.3 us (18%)
  starting transfers between devices  20.5 us (10%)
  matrix products  19.8 us (9%)
  other arithmetic  7.81 us (4%)
    all_to_all x1, waiting for transfers between devices, shards(): lax.all_to_all(payload, 'tm', split_axis=1, concat_axis=0, tiled=True)  123 us
    conv_general_dilated x1, matrix products, spatial_conv(): lax.conv_general_dilated(row_padded, w_spatial, window_strides=(1, 1), pa...  16.2 us
    all_to_all x1, starting transfers between devices, shards(): lax.all_to_all(payload, 'tm', split_axis=1, concat_axis=0, tiled=True)  10.2 us
    conv_general_dilated x3, local copies, waits for them, and re-layouts, spatial_conv(): lax.conv_general_dilated(row_padded, w_spatial, window_strides=(1, 1), pa...  8.43 us
    concatenate x1, local copies, waits for them, and re-layouts, shards(): payload = jnp.concatenate([conv_out, column], axis=2)  5.42 us
    slice x1, local copies, waits for them, and re-layouts, shards(): exchanged = received[:, :, :conv_out.shape[2]]  5.38 us
    convert_element_type x2, local copies, waits for them, and re-layouts, spatial_conv(): return out.astype(jnp.bfloat16)  5.28 us
    ppermute x1, starting transfers between devices, with_halo(): lax.ppermute(lax.slice_in_dim(block, 0, width, axis=dim), axis, backward)  5.11 us
  transfers between devices with their start and end apart: 4, of which 1 were waited for; matrix products, arithmetic and copies ran while one was open for 6% of the time, Pallas kernels for 0%

profile of v2, /device:TPU:1, one launch (start us, length us, event | category | flops | bytes accessed | tf_op | source)
XLA Modules:
  0.0 209.4 jit_solution(7737448832690738982)
XLA Ops:
  0.0 0.0 copy-start
  0.0 1.1 fusion.30
  1.1 1.3 collective-permute-start
  2.4 5.1 %collective-permute-start.1 = (bf16[1,1,160,256]{3,2,1,0:T(8,128)(2,1)S(1)}, bf16[1,1,160,256]{3,2,1,0:T(8,128)(2,1)S(1)}, u32[]{:S(2)}, u32[]{:S(2)}) collective-permute-start(bf16[1,1,160,256]{3,2,1,0:T(8,128)(2,1)S(1)} %get-tuple-element.22), channel_id=1, source_target_pairs={{1,0},{3,2},{5,4},{7,6},{9,8},{11,10},{13,12},{15,14},{17,16},{19,... | collective-permute-start | bytes 245768 | tf_op jit(solution)/shard_map/ppermute | solution.py:18
  7.5 1.2 dynamic_slice.4
  9.4 0.0 collective-permute-done
  9.4 0.0 collective-permute-done.1
  9.4 2.1 %maximum_bitcast_fusion.2 = bf16[34,1,160,256]{3,2,0,1:T(8,128)(2,1)S(1)} fusion(bf16[1,1,160,256]{3,2,1,0:T(8,128)(2,1)S(1)} %collective-permute-done.1, bf16[1,32,160,256]{3,2,1,0:T(8,128)(2,1)} %param.9, bf16[1,1,160,256]{3,2,1,0:T(8,128)(2,1)S(1)} %collective-permute-done), kind=kLoop, calls=%fused_computation.29 | loop fusion | flops 2785280 | bytes 5570560 | tf_op jit(solution)/shard_map/concatenate | solution.py:19
  11.5 3.5 %pad.3 = bf16[34,1,168,256]{3,2,0,1:T(8,128)(2,1)} pad(bf16[34,1,160,256]{3,2,0,1:T(8,128)(2,1)S(1)} %maximum_bitcast_fusion.2, bf16[]{:T(256)} %constant.65.clone.1), padding=0_0x0_0x1_7x0_0 | pad | bytes 5709826 | tf_op jit(solution)/shard_map/concatenate | solution.py:19
  15.1 5.6 %reshape.145 = bf16[34,1,8,21,256]{4,3,2,0,1:T(8,128)(2,1)} reshape(bf16[34,1,168,256]{3,2,0,1:T(8,128)(2,1)} %pad.3) | data formatting | bytes 5849088 | tf_op jit(solution)/shard_map/conv_general_dilated | solution.py:31
  20.6 0.0 copy-start.7
  20.6 2.8 %copy.24 = bf16[34,1,8,21,256]{4,2,3,0,1:T(8,128)(2,1)S(1)} copy(bf16[34,1,8,21,256]{4,3,2,0,1:T(8,128)(2,1)} %reshape.145) | data formatting | bytes 5849088 | tf_op jit(solution)/shard_map/conv_general_dilated | solution.py:31
  23.4 0.1 slice.63
  23.5 0.0 copy-done
  23.5 0.0 copy-done.7
  23.5 16.2 %fusion = (f32[512]{0:T(512)S(1)}, f32[512]{0:T(512)S(1)}, bf16[32,8,21,512]{3,1,2,0:T(8,128)(2,1)}) fusion(pred[8,21]{0,1:T(8,128)(4,1)S(1)} %copy-done.7, bf16[3,3,256,512]{3,2,1,0:T(8,128)(2,1)S(1)} %copy-done, bf16[34,1,7,2,256]{4,2,3,0,1:T(8,128)(2,1)S(1)} %slice.63, bf16[34,1,8,21,256]{4,2,3,0,1:T(8,128)(2,1)S(1)} %copy.24), kind=kOutput, calls=%fused_computation.3 | convolution fusion | flops 12715204608 | bytes 11036840 | tf_op jit(solution)/shard_map/conv_general_dilated | solution.py:31
  39.7 0.1 reshape.138
  39.8 0.1 reshape.139
  39.8 0.1 reduce_sum.67
  40.0 0.1 reduce_sum.69
  40.1 0.1 fusion.29
  40.2 0.1 subtract_convert_fusion
  40.3 4.4 %copy.25 = bf16[32,8,21,512]{3,0,2,1:T(8,128)(2,1)S(1)} copy(bf16[32,8,21,512]{3,1,2,0:T(8,128)(2,1)} %get-tuple-element.25) | data formatting | bytes 11010048 | tf_op jit(solution)/shard_map/convert_element_type | solution.py:39
  44.7 0.8 slice_bitcast_fusion.1
  45.5 0.1 fusion.23
  45.6 0.5 pad_maximum_fusion
  46.1 5.4 %copy.26 = bf16[1,32,161,512]{3,2,0,1:T(8,128)(2,1)} copy(bf16[1,32,161,512]{3,1,2,0:T(8,128)(2,1)S(1)} %pad_maximum_fusion) | data formatting | bytes 10551296 | tf_op jit(solution)/shard_map/concatenate | solution.py:104
  51.5 0.0 copy-start.6
  51.5 10.2 %all-to-all-start = ((bf16[1,32,161,512]{3,2,0,1:T(8,128)(2,1)}), bf16[1,32,161,512]{3,2,0,1:T(8,128)(2,1)}, u32[]{:S(2)}, u32[]{:S(2)}) async-start(bf16[1,32,161,512]{3,2,0,1:T(8,128)(2,1)} %copy.26), calls=%async_computation | async-start | bytes 11010048 | tf_op jit(solution)/shard_map/all_to_all | solution.py:105
  61.7 0.0 copy-done.6
  61.7 0.1 select_reduce_fusion
  61.9 123.1 %all-to-all-done = bf16[1,32,161,512]{3,2,0,1:T(8,128)(2,1)} async-done(((bf16[1,32,161,512]{3,2,0,1:T(8,128)(2,1)}), bf16[1,32,161,512]{3,2,0,1:T(8,128)(2,1)}, u32[]{:S(2)}, u32[]{:S(2)}) %all-to-all-start) | async-done | bytes 5275680 | tf_op jit(solution)/shard_map/all_to_all | solution.py:105
  184.9 0.8 slice_convert_fusion
  185.8 0.1 slice_reduce_fusion
  185.9 3.9 %collective-permute-start.2 = (f32[64]{0:T(128)S(1)}, f32[64]{0:T(128)S(1)}, u32[]{:S(2)}, u32[]{:S(2)}) collective-permute-start(f32[64]{0:T(128)S(1)} %add.75), channel_id=1, source_target_pairs={{0,1},{1,0},{2,3},{3,2},{4,5},{5,4},{6,7},{7,6},{8,9},{9,8},{10,11... | collective-permute-start | bytes 776 | tf_op jit(solution)/shard_map/ppermute | solution.py:108
  189.8 5.4 %slice_bitcast_fusion = bf16[32,160,512]{2,1,0:T(8,128)(2,1)} fusion(bf16[32,1,161,512]{3,2,0,1:T(8,128)(2,1)} %bitcast.5), kind=kLoop, calls=%fused_computation.11 | loop fusion | bytes 10485760 | tf_op jit(solution)/shard_map/slice | solution.py:106
  195.2 0.0 copy-start.2
  195.2 0.0 copy-start.3
  195.2 5.0 %gather_fusion = bf16[17,160,512]{2,1,0:T(8,128)(2,1)} fusion(bf16[32,160,512]{2,1,0:T(8,128)(2,1)} %slice_bitcast_fusion, s32[1024]{0:T(1024)S(1)} %pad_clamp_fusion), kind=kCustom, calls=%fused_computation | custom fusion | bytes 5570628 | tf_op jit(solution)/shard_map/jit(_take)/gather | solution.py:115
  200.2 0.0 collective-permute-done.2
  200.2 0.1 slice_multiply_fusion
  200.3 0.1 broadcast_in_dim.44
  200.4 0.1 mul.68
  200.5 0.1 broadcast_in_dim.43
  200.6 0.1 sub.25
  200.6 0.0 copy-done.2
  200.6 0.0 copy-done.3
  200.7 3.6 %multiply_convert_fusion = bf16[17,1,160,512]{3,2,0,1:T(8,128)(2,1)S(1)} fusion(bf16[17,160,512]{2,1,0:T(8,128)(2,1)} %gather_fusion, f32[512]{0:T(512)S(1)} %copy-done.2, f32[512]{0:T(512)S(1)} %copy-done.3, f32[512]{0:T(512)S(1)} %mul.68, f32[512]{0:T(512)S(1)} %sub.25, pred[17]{0:T(512)(128)(4,1)S(1)} %compare_and_fusion), kind=kLoop, calls=%fused_computation.9 | loop fusion | flops 15319040 | bytes 5578769 | tf_op jit(solution)/shard_map/convert_element_type | solution.py:59
  204.3 0.0 copy-start.4
  204.3 0.0 copy-start.5
  204.3 0.1 slice.56
  204.4 0.1 slice.58
  204.5 0.1 slice.70
  204.6 1.1 copy-done.4
  205.7 0.0 copy-done.5
  205.7 0.0 copy-start.1
  205.7 3.7 %fusion.20 = bf16[9,1,1,160,512]{4,3,2,1,0:T(8,128)(2,1)} fusion(f32[512]{0:T(512)S(1)} %copy-done.5, bf16[1536,512,1]{1,0,2:T(8,128)(2,1)S(1)} %bitcast.45, bf16[9,1,160,512]{3,2,0,1:T(8,128)(2,1)S(1)} %slice.56, bf16[8,1,160,512]{3,2,0,1:T(8,128)(2,1)S(1)} %slice.58, bf16[1,1,160,512]{3,2,0,1:T(8,128)(2,1)S(1)} %slice.69, ...), kind=kOutput, calls=%fused_computation.32 | convolution fusion | flops 2288517120 | bytes 7309312 | tf_op jit(solution)/shard_map/trwc,cd->trwd/dot_general | solution.py:75
  209.4 0.0 copy-done.1
  (8 shorter events, 0.1 us)
Async XLA Ops:
  0.0 23.5 %copy-start = (bf16[3,3,256,512]{3,2,1,0:T(8,128)(2,1)S(1)}, bf16[3,3,256,512]{3,2,1,0:T(8,128)(2,1)}, u32[]{:S(2)}) copy-start(bf16[3,3,256,512]{3,2,1,0:T(8,128)(2,1)} %param.11) | copy-start | bytes 7077892
  1.1 8.3 %collective-permute-start = (bf16[1,1,160,256]{3,2,1,0:T(8,128)(2,1)S(1)}, bf16[1,1,160,256]{3,2,1,0:T(8,128)(2,1)S(1)}, u32[]{:S(2)}, u32[]{:S(2)}) collective-permute-start(bf16[1,1,160,256]{3,2,1,0:T(8,128)(2,1)S(1)} %get-tuple-element.21), channel_id=1, source_target_pairs={{0,1},{2,3},{4,5},{6,7},{8,9},{10,11},{12,13},{14,15},{16,17},{18,... | collective-permute-start | bytes 245768 | tf_op jit(solution)/shard_map/ppermute | solution.py:15
  2.4 7.0 %collective-permute-start.1 = (bf16[1,1,160,256]{3,2,1,0:T(8,128)(2,1)S(1)}, bf16[1,1,160,256]{3,2,1,0:T(8,128)(2,1)S(1)}, u32[]{:S(2)}, u32[]{:S(2)}) collective-permute-start(bf16[1,1,160,256]{3,2,1,0:T(8,128)(2,1)S(1)} %get-tuple-element.22), channel_id=1, source_target_pairs={{1,0},{3,2},{5,4},{7,6},{9,8},{11,10},{13,12},{15,14},{17,16},{19,... | collective-permute-start | bytes 245768 | tf_op jit(solution)/shard_map/ppermute | solution.py:18
  20.6 2.9 %copy-start.7 = (pred[8,21]{0,1:T(8,128)(4,1)S(1)}, pred[8,21]{0,1:T(8,128)(4,1)}, u32[]{:S(2)}) copy-start(pred[8,21]{0,1:T(8,128)(4,1)} %constant.79) | copy-start | bytes 508
  51.5 10.2 %copy-start.6 = (s32[32]{0:T(128)S(1)}, s32[32]{0:T(128)}, u32[]{:S(2)}) copy-start(s32[32]{0:T(128)} %param.10) | copy-start | bytes 388
  51.5 133.4 %all-to-all-start = ((bf16[1,32,161,512]{3,2,0,1:T(8,128)(2,1)}), bf16[1,32,161,512]{3,2,0,1:T(8,128)(2,1)}, u32[]{:S(2)}, u32[]{:S(2)}) async-start(bf16[1,32,161,512]{3,2,0,1:T(8,128)(2,1)} %copy.26), calls=%async_computation | async-start | bytes 11010048 | tf_op jit(solution)/shard_map/all_to_all | solution.py:105
  185.9 14.4 %collective-permute-start.2 = (f32[64]{0:T(128)S(1)}, f32[64]{0:T(128)S(1)}, u32[]{:S(2)}, u32[]{:S(2)}) collective-permute-start(f32[64]{0:T(128)S(1)} %add.75), channel_id=1, source_target_pairs={{0,1},{1,0},{2,3},{3,2},{4,5},{5,4},{6,7},{7,6},{8,9},{9,8},{10,11... | collective-permute-start | bytes 776 | tf_op jit(solution)/shard_map/ppermute | solution.py:108
  195.2 5.4 %copy-start.2 = (f32[512]{0:T(512)S(1)}, f32[512]{0:T(512)}, u32[]{:S(2)}) copy-start(f32[512]{0:T(512)} %param.13) | copy-start | bytes 6148
  195.2 5.4 %copy-start.3 = (f32[512]{0:T(512)S(1)}, f32[512]{0:T(512)}, u32[]{:S(2)}) copy-start(f32[512]{0:T(512)} %param.12) | copy-start | bytes 6148
  204.3 1.4 copy-start.4
  204.3 1.4 copy-start.5
  205.7 3.7 %copy-start.1 = (bf16[3,3,256,512]{3,2,1,0:T(8,128)(2,1)S(1)}, bf16[3,3,256,512]{3,2,1,0:T(8,128)(2,1)}, u32[]{:S(2)}) copy-start(bf16[3,3,256,512]{3,2,1,0:T(8,128)(2,1)} %param.11) | copy-start | bytes 7077892

commit v3 on v2

--- a/solution.py
+++ b/solution.py
@@ -99,12 +99,15 @@
     weight = jnp.where(own_frame >= 0, 1.0, 0.0).astype(jnp.float32)
     sums, squares = group_stats(conv_out, weight)
     coded = encode_stats(jnp.concatenate([sums, squares]))
-    column = jnp.zeros((conv_out.shape[-1],), jnp.bfloat16).at[: coded.shape[0]].set(coded)
-    column = jnp.broadcast_to(column, (1, conv_out.shape[1], 1, conv_out.shape[-1]))
-    payload = jnp.concatenate([conv_out, column], axis=2)
+    lanes = 128
+    rows, cols, chans = conv_out.shape[1], conv_out.shape[2], conv_out.shape[3]
+    column = jnp.zeros((lanes,), jnp.bfloat16).at[: coded.shape[0]].set(coded)
+    column = jnp.broadcast_to(column, (1, rows, 1, lanes))
+    flat = conv_out.reshape(1, rows, cols * chans // lanes, lanes)
+    payload = jnp.concatenate([flat, column], axis=2)
     received = lax.all_to_all(payload, "tm", split_axis=1, concat_axis=0, tiled=True)
-    exchanged = received[:, :, : conv_out.shape[2]]
-    partial = decode_stats(received[:, 0, conv_out.shape[2], : coded.shape[0]], 2 * GROUPS)
+    exchanged = received[:, :, : cols * chans // lanes].reshape(received.shape[0], 1, cols, chans)
+    partial = decode_stats(received[:, 0, cols * chans // lanes, : coded.shape[0]], 2 * GROUPS)
     other = lax.ppermute(partial, "height", [(0, 1), (1, 0)])
     totals = partial + other
     sums, squares = totals[:GROUPS], totals[GROUPS:]

time: 213 us -> 232 us (1.089)
  local copies, waits for them, and re-layouts: 37.3 us -> 55.4 us
  other arithmetic: 7.81 us -> 12.6 us
  starting transfers between devices: 20.5 us -> 17.2 us
    reshape x0 -> x2, local copies, waits for them, and re-layouts: none -> 18.3 us  [the longest x1 9.14 us: shards(): flat = conv_out.reshape(1, rows, cols * chans // lanes, lanes)]
    concatenate x1 -> x0, local copies, waits for them, and re-layouts: 5.42 us -> none  [shards(): payload = jnp.concatenate([conv_out, column], axis=2)]
    convert_element_type x2 -> x3, local copies, waits for them, and re-layouts: 5.28 us -> 10.6 us  [spatial_conv(): return out.astype(jnp.bfloat16)]
    concatenate x1, other arithmetic: 0.45 us -> 5.25 us  [shards(): payload = jnp.concatenate([flat, column], axis=2)]
    ppermute x1, starting transfers between devices: 3.93 us -> 0.63 us  [shards(): other = lax.ppermute(partial, 'height', [(0, 1), (1, 0)])]
  transfers between devices with their start and end apart: 4 -> 4, of which waited for: 1 -> 1; matrix products, arithmetic and copies ran while one was open for 6% -> 9% of each run, Pallas kernels for 0% -> 0%
where the time goes in v3:
time: 232 us; the launch traced here: 228 us
  waiting for transfers between devices  122 us (53%)
  local copies, waits for them, and re-layouts  55.4 us (24%)
  matrix products  19.8 us (9%)
  starting transfers between devices  17.2 us (7%)
  other arithmetic  12.6 us (5%)
    all_to_all x1, waiting for transfers between devices, shards(): lax.all_to_all(payload, 'tm', split_axis=1, concat_axis=0, tiled=True)  122 us
    conv_general_dilated x1, matrix products, spatial_conv(): lax.conv_general_dilated(row_padded, w_spatial, window_strides=(1, 1), pa...  16.2 us
    convert_element_type x3, local copies, waits for them, and re-layouts, spatial_conv(): return out.astype(jnp.bfloat16)  10.6 us
    all_to_all x1, starting transfers between devices, shards(): lax.all_to_all(payload, 'tm', split_axis=1, concat_axis=0, tiled=True)  10.2 us
    reshape x1, local copies, waits for them, and re-layouts, shards(): flat = conv_out.reshape(1, rows, cols * chans // lanes, lanes)  9.14 us
    reshape x1, local copies, waits for them, and re-layouts, shards(): received[:, :, :cols * chans // lanes]  9.14 us
    conv_general_dilated x3, local copies, waits for them, and re-layouts, spatial_conv(): lax.conv_general_dilated(row_padded, w_spatial, window_strides=(1, 1), pa...  8.43 us
    slice x1, local copies, waits for them, and re-layouts, shards(): received[:, :, :cols * chans // lanes]  5.38 us
  transfers between devices with their start and end apart: 4, of which 1 were waited for; matrix products, arithmetic and copies ran while one was open for 9% of the time, Pallas kernels for 0%

profile of v3, /device:TPU:1, one launch (start us, length us, event | category | flops | bytes accessed | tf_op | source)
XLA Modules:
  0.0 228.1 jit_solution(9944124585271844727)
XLA Ops:
  0.0 0.0 copy-start
  0.0 1.1 fusion.27
  1.1 1.3 collective-permute-start
  2.4 5.1 %collective-permute-start.1 = (bf16[1,1,160,256]{3,2,1,0:T(8,128)(2,1)S(1)}, bf16[1,1,160,256]{3,2,1,0:T(8,128)(2,1)S(1)}, u32[]{:S(2)}, u32[]{:S(2)}) collective-permute-start(bf16[1,1,160,256]{3,2,1,0:T(8,128)(2,1)S(1)} %get-tuple-element.30), channel_id=1, source_target_pairs={{1,0},{3,2},{5,4},{7,6},{9,8},{11,10},{13,12},{15,14},{17,16},{19,... | collective-permute-start | bytes 245768 | tf_op jit(solution)/shard_map/ppermute | solution.py:18
  7.5 1.2 dynamic_slice.4
  9.4 0.0 collective-permute-done
  9.4 0.0 collective-permute-done.1
  9.4 2.1 maximum_bitcast_fusion.3
  11.5 3.5 %pad.3 = bf16[34,1,168,256]{3,2,0,1:T(8,128)(2,1)} pad(bf16[34,1,160,256]{3,2,0,1:T(8,128)(2,1)S(1)} %maximum_bitcast_fusion.3, bf16[]{:T(256)} %constant.79), padding=0_0x0_0x1_7x0_0 | pad | bytes 5709826 | tf_op jit(solution)/shard_map/concatenate | solution.py:19
  15.1 5.6 %reshape.155 = bf16[34,1,8,21,256]{4,3,2,0,1:T(8,128)(2,1)} reshape(bf16[34,1,168,256]{3,2,0,1:T(8,128)(2,1)} %pad.3) | data formatting | bytes 5849088 | tf_op jit(solution)/shard_map/conv_general_dilated | solution.py:31
  20.6 0.0 copy-start.7
  20.6 2.8 %copy.25 = bf16[34,1,8,21,256]{4,2,3,0,1:T(8,128)(2,1)S(1)} copy(bf16[34,1,8,21,256]{4,3,2,0,1:T(8,128)(2,1)} %reshape.155) | data formatting | bytes 5849088 | tf_op jit(solution)/shard_map/conv_general_dilated | solution.py:31
  23.4 0.1 slice.61
  23.5 0.0 copy-done
  23.5 0.0 copy-done.7
  23.5 16.2 %fusion = (f32[512]{0:T(512)S(1)}, f32[512]{0:T(512)S(1)}, bf16[32,8,21,512]{3,1,2,0:T(8,128)(2,1)}) fusion(pred[8,21]{0,1:T(8,128)(4,1)S(1)} %copy-done.7, bf16[3,3,256,512]{3,2,1,0:T(8,128)(2,1)S(1)} %copy-done, bf16[34,1,7,2,256]{4,2,3,0,1:T(8,128)(2,1)S(1)} %slice.61, bf16[34,1,8,21,256]{4,2,3,0,1:T(8,128)(2,1)S(1)} %copy.25), kind=kOutput, calls=%fused_computation.3 | convolution fusion | flops 12715204608 | bytes 11036840 | tf_op jit(solution)/shard_map/conv_general_dilated | solution.py:31
  39.7 0.1 reshape.147
  39.8 0.1 reshape.148
  39.8 0.1 reduce_sum.67
  40.0 0.1 reduce_sum.69
  40.1 0.1 fusion.26
  40.2 0.1 subtract_convert_fusion
  40.3 4.4 %copy.26 = bf16[32,8,21,512]{3,0,2,1:T(8,128)(2,1)S(1)} copy(bf16[32,8,21,512]{3,1,2,0:T(8,128)(2,1)} %get-tuple-element.33) | data formatting | bytes 11010048 | tf_op jit(solution)/shard_map/convert_element_type | solution.py:39
  44.7 0.8 slice.62
  45.5 5.3 %copy.27 = bf16[32,1,160,512]{3,2,0,1:T(8,128)(2,1)} copy(bf16[32,1,160,512]{3,0,2,1:T(8,128)(2,1)S(1)} %slice.62) | data formatting | bytes 10485760 | tf_op jit(solution)/shard_map/convert_element_type | solution.py:39
  50.9 9.1 %reshape.146 = bf16[1,32,640,128]{3,2,1,0:T(8,128)(2,1)} reshape(bf16[32,1,160,512]{3,2,0,1:T(8,128)(2,1)} %copy.27) | data formatting | bytes 10485760 | tf_op jit(solution)/shard_map/reshape | solution.py:106
  60.0 0.1 pad_maximum_fusion.1
  60.1 5.2 %maximum_bitcast_fusion = bf16[1,32,641,128]{3,2,0,1:T(8,128)(2,1)} fusion(bf16[1,32,1,128]{3,2,1,0:T(2,128)(2,1)S(1)} %broadcast_in_dim.41, bf16[1,32,640,128]{3,2,1,0:T(8,128)(2,1)} %reshape.146), kind=kLoop, calls=%fused_computation.10 | loop fusion | flops 10502144 | bytes 10502144 | tf_op jit(solution)/shard_map/concatenate | solution.py:107
  65.4 0.0 copy-start.6
  65.4 10.2 %all-to-all-start = ((bf16[1,32,641,128]{3,2,0,1:T(8,128)(2,1)}), bf16[1,32,641,128]{3,2,0,1:T(8,128)(2,1)}, u32[]{:S(2)}, u32[]{:S(2)}) async-start(bf16[1,32,641,128]{3,2,0,1:T(8,128)(2,1)} %maximum_bitcast_fusion), calls=%async_computation | async-start | bytes 10616832 | tf_op jit(solution)/shard_map/all_to_all | solution.py:108
  75.6 0.0 copy-done.6
  75.6 0.1 select_reduce_fusion
  75.7 122.1 %all-to-all-done = bf16[1,32,641,128]{3,2,0,1:T(8,128)(2,1)} async-done(((bf16[1,32,641,128]{3,2,0,1:T(8,128)(2,1)}), bf16[1,32,641,128]{3,2,0,1:T(8,128)(2,1)}, u32[]{:S(2)}, u32[]{:S(2)}) %all-to-all-start) | async-done | bytes 5251104 | tf_op jit(solution)/shard_map/all_to_all | solution.py:108
  197.8 0.8 slice_convert_fusion
  198.7 0.1 slice_reduce_fusion
  198.8 0.6 collective-permute-start.2
  199.4 5.4 %slice.63 = bf16[32,1,640,128]{3,2,0,1:T(8,128)(2,1)} slice(bf16[32,1,641,128]{3,2,0,1:T(8,128)(2,1)} %bitcast.5), slice={[0:32], [0:1], [0:640], [0:128]} | slice | bytes 10485760 | tf_op jit(solution)/shard_map/slice | solution.py:109
  204.8 9.1 %reshape.169 = bf16[32,160,512]{2,1,0:T(8,128)(2,1)} reshape(bf16[32,1,640,128]{3,2,0,1:T(8,128)(2,1)} %slice.63) | data formatting | bytes 10485760 | tf_op jit(solution)/shard_map/reshape | solution.py:109
  213.9 0.0 copy-start.2
  213.9 0.0 copy-start.3
  213.9 5.0 %gather_fusion = bf16[17,160,512]{2,1,0:T(8,128)(2,1)} fusion(bf16[32,160,512]{2,1,0:T(8,128)(2,1)} %reshape.169, s32[1024]{0:T(1024)S(1)} %pad_clamp_fusion), kind=kCustom, calls=%fused_computation | custom fusion | bytes 5570628 | tf_op jit(solution)/shard_map/jit(_take)/gather | solution.py:118
  219.0 0.0 collective-permute-done.2
  219.0 0.1 slice_multiply_fusion
  219.0 0.1 broadcast_in_dim.44
  219.1 0.1 mul.68
  219.2 0.1 broadcast_in_dim.43
  219.3 0.1 sub.25
  219.3 0.0 copy-done.2
  219.4 0.0 copy-done.3
  219.4 3.6 %multiply_convert_fusion = bf16[17,1,160,512]{3,2,0,1:T(8,128)(2,1)S(1)} fusion(bf16[17,160,512]{2,1,0:T(8,128)(2,1)} %gather_fusion, f32[512]{0:T(512)S(1)} %copy-done.2, f32[512]{0:T(512)S(1)} %copy-done.3, f32[512]{0:T(512)S(1)} %mul.68, f32[512]{0:T(512)S(1)} %sub.25, pred[17]{0:T(512)(128)(4,1)S(1)} %compare_and_fusion), kind=kLoop, calls=%fused_computation.9 | loop fusion | flops 15319040 | bytes 5578769 | tf_op jit(solution)/shard_map/convert_element_type | solution.py:59
  223.0 0.0 copy-start.4
  223.0 0.0 copy-start.5
  223.0 0.1 slice.54
  223.1 0.1 slice.56
  223.2 0.1 slice.68
  223.3 1.1 copy-done.4
  224.4 0.0 copy-done.5
  224.4 0.0 copy-start.1
  224.4 3.7 %fusion.20 = bf16[9,1,1,160,512]{4,3,2,1,0:T(8,128)(2,1)} fusion(f32[512]{0:T(512)S(1)} %copy-done.5, bf16[1536,512,1]{1,0,2:T(8,128)(2,1)S(1)} %bitcast.51, bf16[9,1,160,512]{3,2,0,1:T(8,128)(2,1)S(1)} %slice.54, bf16[8,1,160,512]{3,2,0,1:T(8,128)(2,1)S(1)} %slice.56, bf16[1,1,160,512]{3,2,0,1:T(8,128)(2,1)S(1)} %slice.67, ...), kind=kOutput, calls=%fused_computation.30 | convolution fusion | flops 2288517120 | bytes 7309312 | tf_op jit(solution)/shard_map/trwc,cd->trwd/dot_general | solution.py:75
  228.1 0.0 copy-done.1
  (8 shorter events, 0.1 us)
Async XLA Ops:
  0.0 23.5 %copy-start = (bf16[3,3,256,512]{3,2,1,0:T(8,128)(2,1)S(1)}, bf16[3,3,256,512]{3,2,1,0:T(8,128)(2,1)}, u32[]{:S(2)}) copy-start(bf16[3,3,256,512]{3,2,1,0:T(8,128)(2,1)} %param.13) | copy-start | bytes 7077892
  1.1 8.3 %collective-permute-start = (bf16[1,1,160,256]{3,2,1,0:T(8,128)(2,1)S(1)}, bf16[1,1,160,256]{3,2,1,0:T(8,128)(2,1)S(1)}, u32[]{:S(2)}, u32[]{:S(2)}) collective-permute-start(bf16[1,1,160,256]{3,2,1,0:T(8,128)(2,1)S(1)} %get-tuple-element.29), channel_id=1, source_target_pairs={{0,1},{2,3},{4,5},{6,7},{8,9},{10,11},{12,13},{14,15},{16,17},{18,... | collective-permute-start | bytes 245768 | tf_op jit(solution)/shard_map/ppermute | solution.py:15
  2.4 7.0 %collective-permute-start.1 = (bf16[1,1,160,256]{3,2,1,0:T(8,128)(2,1)S(1)}, bf16[1,1,160,256]{3,2,1,0:T(8,128)(2,1)S(1)}, u32[]{:S(2)}, u32[]{:S(2)}) collective-permute-start(bf16[1,1,160,256]{3,2,1,0:T(8,128)(2,1)S(1)} %get-tuple-element.30), channel_id=1, source_target_pairs={{1,0},{3,2},{5,4},{7,6},{9,8},{11,10},{13,12},{15,14},{17,16},{19,... | collective-permute-start | bytes 245768 | tf_op jit(solution)/shard_map/ppermute | solution.py:18
  20.6 2.9 %copy-start.7 = (pred[8,21]{0,1:T(8,128)(4,1)S(1)}, pred[8,21]{0,1:T(8,128)(4,1)}, u32[]{:S(2)}) copy-start(pred[8,21]{0,1:T(8,128)(4,1)} %constant.85) | copy-start | bytes 508
  65.4 10.2 %copy-start.6 = (s32[32]{0:T(128)S(1)}, s32[32]{0:T(128)}, u32[]{:S(2)}) copy-start(s32[32]{0:T(128)} %param.12) | copy-start | bytes 388
  65.4 132.5 %all-to-all-start = ((bf16[1,32,641,128]{3,2,0,1:T(8,128)(2,1)}), bf16[1,32,641,128]{3,2,0,1:T(8,128)(2,1)}, u32[]{:S(2)}, u32[]{:S(2)}) async-start(bf16[1,32,641,128]{3,2,0,1:T(8,128)(2,1)} %maximum_bitcast_fusion), calls=%async_computation | async-start | bytes 10616832 | tf_op jit(solution)/shard_map/all_to_all | solution.py:108
  198.8 20.2 %collective-permute-start.2 = (f32[64]{0:T(128)S(1)}, f32[64]{0:T(128)S(1)}, u32[]{:S(2)}, u32[]{:S(2)}) collective-permute-start(f32[64]{0:T(128)S(1)} %add.74), channel_id=1, source_target_pairs={{0,1},{1,0},{2,3},{3,2},{4,5},{5,4},{6,7},{7,6},{8,9},{9,8},{10,11... | collective-permute-start | bytes 776 | tf_op jit(solution)/shard_map/ppermute | solution.py:111
  213.9 5.4 %copy-start.2 = (f32[512]{0:T(512)S(1)}, f32[512]{0:T(512)}, u32[]{:S(2)}) copy-start(f32[512]{0:T(512)} %param.15) | copy-start | bytes 6148
  213.9 5.4 %copy-start.3 = (f32[512]{0:T(512)S(1)}, f32[512]{0:T(512)}, u32[]{:S(2)}) copy-start(f32[512]{0:T(512)} %param.14) | copy-start | bytes 6148
  223.0 1.4 copy-start.4
  223.0 1.4 copy-start.5
  224.4 3.7 %copy-start.1 = (bf16[3,3,256,512]{3,2,1,0:T(8,128)(2,1)S(1)}, bf16[3,3,256,512]{3,2,1,0:T(8,128)(2,1)}, u32[]{:S(2)}) copy-start(bf16[3,3,256,512]{3,2,1,0:T(8,128)(2,1)} %param.13) | copy-start | bytes 7077892

commit v4 on v2

--- a/solution.py
+++ b/solution.py
@@ -1,7 +1,11 @@
+import functools
+
 import jax
 import jax.numpy as jnp
 import numpy as np
 from jax import lax
+from jax.experimental import pallas as pl
+from jax.experimental.pallas import tpu as pltpu
 from jax.sharding import PartitionSpec as P
 
 GROUPS = 32
@@ -25,6 +29,61 @@
     places = jnp.arange(frame_of_slot.shape[0], dtype=jnp.int32)[None, :]
     matches = frame_of_slot[None, :] == wanted
     return jnp.sum(jnp.where(matches, places, 0), axis=1)
+
+
+def conv_kernel(x_ref, w_ref, out_ref, sum_ref, sq_ref, *, chunk, cols):
+    step = pl.program_id(0)
+    base = step * chunk
+    m = chunk * cols
+    parts = []
+    for col_tap in range(3):
+        acc = None
+        for row_tap in range(3):
+            xs = x_ref[pl.ds(base + row_tap, chunk), :, :].reshape(m, x_ref.shape[-1])
+            p = jnp.dot(xs, w_ref[row_tap, col_tap], preferred_element_type=jnp.float32)
+            acc = p if acc is None else acc + p
+        parts.append(acc)
+    col = lax.broadcasted_iota(jnp.int32, (m, 1), 0) % cols
+    left = jnp.where(col == 0, 0.0, pltpu.roll(parts[0], 1, 0))
+    right = jnp.where(col == cols - 1, 0.0, pltpu.roll(parts[2], m - 1, 0))
+    total = (left + parts[1]) + right
+    rounded = total.astype(jnp.bfloat16)
+    out_ref[:, 0:cols, :] = rounded.reshape(chunk, cols, -1)
+    out_ref[:, cols:cols + 1, :] = jnp.zeros((chunk, 1, out_ref.shape[-1]), jnp.bfloat16)
+    values = rounded.astype(jnp.float32)
+
+    @pl.when(step == 0)
+    def _():
+        sum_ref[...] = jnp.zeros_like(sum_ref)
+        sq_ref[...] = jnp.zeros_like(sq_ref)
+
+    sum_ref[...] += jnp.sum(values, axis=0, keepdims=True)
+    sq_ref[...] += jnp.sum(values * values, axis=0, keepdims=True)
+
+def conv_call(x, w, chunk=8):
+    rows = x.shape[0] - 2
+    cols = x.shape[1]
+    cin = x.shape[2]
+    cout = w.shape[-1]
+    return pl.pallas_call(
+        functools.partial(conv_kernel, chunk=chunk, cols=cols),
+        grid=(rows // chunk,),
+        in_specs=[
+            pl.BlockSpec((rows + 2, cols, cin), lambda i: (0, 0, 0)),
+            pl.BlockSpec((3, 3, cin, cout), lambda i: (0, 0, 0, 0)),
+        ],
+        out_specs=[
+            pl.BlockSpec((chunk, cols + 1, cout), lambda i: (i, 0, 0)),
+            pl.BlockSpec((1, cout), lambda i: (0, 0)),
+            pl.BlockSpec((1, cout), lambda i: (0, 0)),
+        ],
+        out_shape=[
+            jax.ShapeDtypeStruct((rows, cols + 1, cout), jnp.bfloat16),
+            jax.ShapeDtypeStruct((1, cout), jnp.float32),
+            jax.ShapeDtypeStruct((1, cout), jnp.float32),
+        ],
+        compiler_params=pltpu.CompilerParams(dimension_semantics=("arbitrary",)),
+    )(x, w)
 
 
 def spatial_conv(row_padded, w_spatial):
@@ -94,24 +153,23 @@
     out_frames = (live_frames - 1) // 2 + 1
     frame_slots = slot_lookup(frame_of_slot, live_frames)
     padded = with_halo(clip_frames, (("height", 1),), 1)
-    conv_out = spatial_conv(padded, w_spatial)
+    staged, chan_sums, chan_squares = conv_call(padded[0], w_spatial)
+    cols = staged.shape[1] - 1
     own_frame = lax.dynamic_index_in_dim(frame_of_slot, lax.axis_index("tm"), 0, keepdims=False)
     weight = jnp.where(own_frame >= 0, 1.0, 0.0).astype(jnp.float32)
-    sums, squares = group_stats(conv_out, weight)
+    per_group = staged.shape[-1] // GROUPS
+    sums = chan_sums.reshape(GROUPS, per_group).sum(axis=1) * weight
+    squares = chan_squares.reshape(GROUPS, per_group).sum(axis=1) * weight
     coded = encode_stats(jnp.concatenate([sums, squares]))
-    column = jnp.zeros((conv_out.shape[-1],), jnp.bfloat16).at[: coded.shape[0]].set(coded)
-    column = jnp.broadcast_to(column, (1, conv_out.shape[1], 1, conv_out.shape[-1]))
-    payload = jnp.concatenate([conv_out, column], axis=2)
-    received = lax.all_to_all(payload, "tm", split_axis=1, concat_axis=0, tiled=True)
-    exchanged = received[:, :, : conv_out.shape[2]]
-    partial = decode_stats(received[:, 0, conv_out.shape[2], : coded.shape[0]], 2 * GROUPS)
+    column = jnp.zeros((staged.shape[-1],), jnp.bfloat16).at[: coded.shape[0]].set(coded)
+    payload = staged.at[:, cols, :].set(jnp.broadcast_to(column, (staged.shape[0], column.shape[0])))
+    received = lax.all_to_all(payload[None], "tm", split_axis=1, concat_axis=0, tiled=True)
+    exchanged = received[:, :, :cols]
+    partial = decode_stats(received[:, 0, cols, : coded.shape[0]], 2 * GROUPS)
     other = lax.ppermute(partial, "height", [(0, 1), (1, 0)])
     totals = partial + other
     sums, squares = totals[:GROUPS], totals[GROUPS:]
-    per_group = conv_out.shape[-1] // GROUPS
-    cell_count = float(
-        live_frames * clip_frames.shape[1] * height_count * conv_out.shape[2] * per_group
-    )
+    cell_count = float(live_frames * clip_frames.shape[1] * height_count * cols * per_group)
     live = jnp.take(exchanged, frame_slots, axis=0)
     activated = normalize(live, sums, squares, cell_count, norm_gain, norm_shift)
     latent = time_conv(activated, w_time, time_bias, out_frames)

time: 213 us -> 197 us (0.925)
  local copies, waits for them, and re-layouts: 37.3 us -> 14.9 us
  Pallas kernels: 0 us -> 19 us
  matrix products: 19.8 us -> 3.68 us
  other arithmetic: 7.81 us -> 11.4 us
  starting transfers between devices: 20.5 us -> 17.2 us
  waiting for transfers between devices: 123 us -> 126 us
    pallas_call x0 -> x1, Pallas kernels: none -> 19 us  [conv_call(): pl.pallas_call(functools.partial(conv_kernel, chunk=chunk, cols=cols), gr...]
    conv_general_dilated x1 -> x0, matrix products: 16.2 us -> none  [spatial_conv(): lax.conv_general_dilated(row_padded, w_spatial, window_strides=(1, 1), pa...]
    concatenate x2 -> x0, local copies, waits for them, and re-layouts: 8.96 us -> none  [the longest x1 5.42 us: shards(): payload = jnp.concatenate([conv_out, column], axis=2)]
    conv_general_dilated x3 -> x0, local copies, waits for them, and re-layouts: 8.43 us -> none  [spatial_conv(): lax.conv_general_dilated(row_padded, w_spatial, window_strides=(1, 1), pa...]
    convert_element_type x2 -> x0, local copies, waits for them, and re-layouts: 5.28 us -> none  [spatial_conv(): return out.astype(jnp.bfloat16)]
    squeeze x0 -> x1, other arithmetic: none -> 3.64 us  [shards(): staged, chan_sums, chan_squares = conv_call(padded[0], w_spatial)]
    all_to_all x1, waiting for transfers between devices: 123 us -> 126 us  [shards(): lax.all_to_all(payload[None], 'tm', split_axis=1, concat_axis=0, tiled=True)]
    ppermute x1, starting transfers between devices: 3.93 us -> 0.6 us  [shards(): other = lax.ppermute(partial, 'height', [(0, 1), (1, 0)])]
where the time goes in v4:
time: 197 us; the launch traced here: 193 us
  waiting for transfers between devices  126 us (64%)
  Pallas kernels  19 us (10%)
  starting transfers between devices  17.2 us (9%)
  local copies, waits for them, and re-layouts  14.9 us (8%)
  other arithmetic  11.4 us (6%)
  matrix products  3.68 us (2%)
    all_to_all x1, waiting for transfers between devices, shards(): lax.all_to_all(payload[None], 'tm', split_axis=1, concat_axis=0, tiled=True)  126 us
    pallas_call x1, Pallas kernels, conv_call(): pl.pallas_call(functools.partial(conv_kernel, chunk=chunk, cols=cols), gr...  19 us
    all_to_all x1, starting transfers between devices, shards(): lax.all_to_all(payload[None], 'tm', split_axis=1, concat_axis=0, tiled=True)  10.2 us
    slice x1, local copies, waits for them, and re-layouts, shards(): exchanged = received[:, :, :cols]  5.35 us
    ppermute x1, starting transfers between devices, with_halo(): lax.ppermute(lax.slice_in_dim(block, 0, width, axis=dim), axis, backward)  5.11 us
    gather x1, local copies, waits for them, and re-layouts, shards(): live = jnp.take(exchanged, frame_slots, axis=0)  5 us
  transfers between devices with their start and end apart: 4, of which 1 were waited for; matrix products, arithmetic and copies ran while one was open for 6% of the time, Pallas kernels for 0%

profile of v4, /device:TPU:1, one launch (start us, length us, event | category | flops | bytes accessed | tf_op | source)
XLA Modules:
  0.0 193.4 jit_solution(16208680177846765607)
XLA Ops:
  0.0 0.0 copy-start
  0.0 1.1 fusion.16
  1.1 1.3 collective-permute-start
  2.4 5.1 %collective-permute-start.1 = (bf16[1,1,160,256]{3,2,1,0:T(8,128)(2,1)S(1)}, bf16[1,1,160,256]{3,2,1,0:T(8,128)(2,1)S(1)}, u32[]{:S(2)}, u32[]{:S(2)}) collective-permute-start(bf16[1,1,160,256]{3,2,1,0:T(8,128)(2,1)S(1)} %get-tuple-element.38), channel_id=1, source_target_pairs={{1,0},{3,2},{5,4},{7,6},{9,8},{11,10},{13,12},{15,14},{17,16},{19,... | collective-permute-start | bytes 245768 | tf_op jit(solution)/shard_map/ppermute | solution.py:22
  7.5 1.2 dynamic_slice.4
  9.4 0.0 collective-permute-done
  9.4 0.0 collective-permute-done.1
  9.4 3.6 %maximum_bitcast_fusion.2.x_ref = bf16[34,160,256]{2,1,0:T(8,128)(2,1)} fusion(bf16[1,1,160,256]{3,2,1,0:T(8,128)(2,1)S(1)} %collective-permute-done.1, bf16[1,32,160,256]{3,2,1,0:T(8,128)(2,1)} %param.11, bf16[1,1,160,256]{3,2,1,0:T(8,128)(2,1)S(1)} %collective-permute-done), kind=kLoop, calls=%fused_computation.14 | loop fusion | flops 2785280 | bytes 5570560 | tf_op jit(solution)/shard_map/squeeze | solution.py:156
  13.0 19.0 %shard_map.73 = (bf16[32,161,512]{2,1,0:T(8,128)(2,1)}, f32[1,512]{1,0:T(1,128)}, f32[1,512]{1,0:T(1,128)}) custom-call(bf16[34,160,256]{2,1,0:T(8,128)(2,1)} %maximum_bitcast_fusion.2.x_ref, bf16[3,3,256,512]{3,2,1,0:T(8,128)(2,1)} %w_ref.1), custom_call_target="tpu_custom_call" | custom-call | tf_op jit(solution)/shard_map/pallas_call | solution.py:68
  32.0 0.5 broadcast.170
  32.5 1.2 reduce.11
  33.8 0.1 reshape.164
  33.8 1.2 reduce.10
  35.1 0.1 reshape.165
  35.2 0.1 reduce_sum.48
  35.3 0.1 reduce_sum.49
  35.4 0.1 fusion.15
  35.5 0.1 subtract_convert_fusion
  35.6 0.1 fusion.12
  35.6 0.7 broadcast_dynamic-update-slice_fusion
  36.3 0.0 copy-start.4
  36.3 10.2 %all-to-all-start = ((bf16[1,32,161,512]{3,2,0,1:T(8,128)(2,1)}), bf16[1,32,161,512]{3,2,0,1:T(8,128)(2,1)}, u32[]{:S(2)}, u32[]{:S(2)}) async-start(bf16[1,32,161,512]{3,2,0,1:T(8,128)(2,1)} %bitcast.34), calls=%async_computation | async-start | bytes 11010048 | tf_op jit(solution)/shard_map/all_to_all | solution.py:166
  46.5 0.0 copy-done.4
  46.5 0.1 select_reduce_fusion
  46.7 126.4 %all-to-all-done = bf16[1,32,161,512]{3,2,0,1:T(8,128)(2,1)} async-done(((bf16[1,32,161,512]{3,2,0,1:T(8,128)(2,1)}), bf16[1,32,161,512]{3,2,0,1:T(8,128)(2,1)}, u32[]{:S(2)}, u32[]{:S(2)}) %all-to-all-start) | async-done | bytes 5275680 | tf_op jit(solution)/shard_map/all_to_all | solution.py:166
  173.1 0.8 slice_convert_fusion
  173.9 0.1 slice_reduce_fusion
  174.0 0.6 collective-permute-start.2
  174.6 5.3 %slice_bitcast_fusion = bf16[32,160,512]{2,1,0:T(8,128)(2,1)} fusion(bf16[32,1,161,512]{3,2,0,1:T(8,128)(2,1)} %bitcast.4), kind=kLoop, calls=%fused_computation.2 | loop fusion | bytes 10485760 | tf_op jit(solution)/shard_map/slice | solution.py:167
  180.0 0.0 copy-start.1
  180.0 0.0 copy-start.2
  180.0 5.0 %gather_fusion = bf16[17,160,512]{2,1,0:T(8,128)(2,1)} fusion(bf16[32,160,512]{2,1,0:T(8,128)(2,1)} %slice_bitcast_fusion, s32[1024]{0:T(1024)S(1)} %pad_clamp_fusion), kind=kCustom, calls=%fused_computation | custom fusion | bytes 5570628 | tf_op jit(solution)/shard_map/jit(_take)/gather | solution.py:173
  185.0 0.0 collective-permute-done.2
  185.0 0.1 slice_multiply_fusion
  185.1 0.1 broadcast_in_dim.48
  185.2 0.1 mul.63
  185.2 0.1 broadcast_in_dim.47
  185.3 0.1 sub.25
  185.4 0.0 copy-done.1
  185.4 0.0 copy-done.2
  185.4 3.6 %multiply_convert_fusion = bf16[17,1,160,512]{3,2,0,1:T(8,128)(2,1)S(1)} fusion(bf16[17,160,512]{2,1,0:T(8,128)(2,1)} %gather_fusion, f32[512]{0:T(512)S(1)} %copy-done.1, f32[512]{0:T(512)S(1)} %copy-done.2, f32[512]{0:T(512)S(1)} %mul.63, f32[512]{0:T(512)S(1)} %sub.25, pred[17]{0:T(512)(128)(4,1)S(1)} %compare_and_fusion), kind=kLoop, calls=%fused_computation.1 | loop fusion | flops 15319040 | bytes 5578769 | tf_op jit(solution)/shard_map/convert_element_type | solution.py:118
  189.0 0.0 copy-start.3
  189.1 0.1 slice.76
  189.2 0.1 slice.78
  189.3 0.1 slice.86
  189.4 0.0 copy-done
  189.4 0.3 copy-done.3
  189.7 3.7 %fusion.9 = bf16[9,1,1,160,512]{4,3,2,1,0:T(8,128)(2,1)} fusion(f32[512]{0:T(512)S(1)} %copy-done.3, bf16[1536,512,1]{1,0,2:T(8,128)(2,1)S(1)} %bitcast.32, bf16[9,1,160,512]{3,2,0,1:T(8,128)(2,1)S(1)} %slice.76, bf16[8,1,160,512]{3,2,0,1:T(8,128)(2,1)S(1)} %slice.78, bf16[1,1,160,512]{3,2,0,1:T(8,128)(2,1)S(1)} %slice.85, ...), kind=kOutput, calls=%fused_computation.16 | convolution fusion | flops 2288517120 | bytes 7309312 | tf_op jit(solution)/shard_map/trwc,cd->trwd/dot_general | solution.py:134
  (7 shorter events, 0.1 us)
Async XLA Ops:
  0.0 189.4 %copy-start = (bf16[3,512,512]{2,1,0:T(8,128)(2,1)S(1)}, bf16[3,512,512]{2,1,0:T(8,128)(2,1)}, u32[]{:S(2)}) copy-start(bf16[3,512,512]{2,1,0:T(8,128)(2,1)} %param.16) | copy-start | bytes 4718596
  1.1 8.3 %collective-permute-start = (bf16[1,1,160,256]{3,2,1,0:T(8,128)(2,1)S(1)}, bf16[1,1,160,256]{3,2,1,0:T(8,128)(2,1)S(1)}, u32[]{:S(2)}, u32[]{:S(2)}) collective-permute-start(bf16[1,1,160,256]{3,2,1,0:T(8,128)(2,1)S(1)} %get-tuple-element.37), channel_id=1, source_target_pairs={{0,1},{2,3},{4,5},{6,7},{8,9},{10,11},{12,13},{14,15},{16,17},{18,... | collective-permute-start | bytes 245768 | tf_op jit(solution)/shard_map/ppermute | solution.py:19
  2.4 7.0 %collective-permute-start.1 = (bf16[1,1,160,256]{3,2,1,0:T(8,128)(2,1)S(1)}, bf16[1,1,160,256]{3,2,1,0:T(8,128)(2,1)S(1)}, u32[]{:S(2)}, u32[]{:S(2)}) collective-permute-start(bf16[1,1,160,256]{3,2,1,0:T(8,128)(2,1)S(1)} %get-tuple-element.38), channel_id=1, source_target_pairs={{1,0},{3,2},{5,4},{7,6},{9,8},{11,10},{13,12},{15,14},{17,16},{19,... | collective-permute-start | bytes 245768 | tf_op jit(solution)/shard_map/ppermute | solution.py:22
  36.3 10.2 %copy-start.4 = (s32[32]{0:T(128)S(1)}, s32[32]{0:T(128)}, u32[]{:S(2)}) copy-start(s32[32]{0:T(128)} %param.12) | copy-start | bytes 388
  36.3 136.8 %all-to-all-start = ((bf16[1,32,161,512]{3,2,0,1:T(8,128)(2,1)}), bf16[1,32,161,512]{3,2,0,1:T(8,128)(2,1)}, u32[]{:S(2)}, u32[]{:S(2)}) async-start(bf16[1,32,161,512]{3,2,0,1:T(8,128)(2,1)} %bitcast.34), calls=%async_computation | async-start | bytes 11010048 | tf_op jit(solution)/shard_map/all_to_all | solution.py:166
  174.0 11.0 %collective-permute-start.2 = (f32[64]{0:T(128)S(1)}, f32[64]{0:T(128)S(1)}, u32[]{:S(2)}, u32[]{:S(2)}) collective-permute-start(f32[64]{0:T(128)S(1)} %add.77), channel_id=1, source_target_pairs={{0,1},{1,0},{2,3},{3,2},{4,5},{5,4},{6,7},{7,6},{8,9},{9,8},{10,11... | collective-permute-start | bytes 776 | tf_op jit(solution)/shard_map/ppermute | solution.py:169
  180.0 5.4 %copy-start.1 = (f32[512]{0:T(512)S(1)}, f32[512]{0:T(512)}, u32[]{:S(2)}) copy-start(f32[512]{0:T(512)} %param.15) | copy-start | bytes 6148
  180.0 5.4 %copy-start.2 = (f32[512]{0:T(512)S(1)}, f32[512]{0:T(512)}, u32[]{:S(2)}) copy-start(f32[512]{0:T(512)} %param.14) | copy-start | bytes 6148
  189.0 0.7 copy-start.3

commit v5 on v4

--- a/solution.py
+++ b/solution.py
@@ -86,6 +86,50 @@
     )(x, w)
 
 
+def latent_kernel(slots_ref, x0_ref, x1_ref, x2_ref, w_ref, mean_ref, scale_ref, gain_ref, shift_ref, bias_ref, out_ref):
+    running = bias_ref[...]
+    for time_tap, x_ref in enumerate((x0_ref, x1_ref, x2_ref)):
+        values = x_ref[0].astype(jnp.float32)
+        normed = (values - mean_ref[...]) * scale_ref[...] * gain_ref[...] + shift_ref[...]
+        activated = jax.nn.silu(normed).astype(jnp.bfloat16)
+        running = running + jnp.dot(activated, w_ref[time_tap], preferred_element_type=jnp.float32)
+    out_ref[0] = running.astype(jnp.bfloat16)
+
+
+def tap_spec(time_tap, cols, chans):
+    def index(step, slots):
+        return (slots[jnp.maximum(2 * step + time_tap - 2, 0)], 0, 0)
+
+    return pl.BlockSpec((1, cols, chans), index)
+
+
+def latent_call(frame_slots, received, w_time, mean_chan, scale_chan, norm_gain, norm_shift, time_bias, out_frames, cols):
+    chans = received.shape[-1]
+    vec = pl.BlockSpec((1, chans), lambda step, slots: (0, 0))
+    grid_spec = pltpu.PrefetchScalarGridSpec(
+        num_scalar_prefetch=1,
+        grid=(out_frames,),
+        in_specs=[
+            tap_spec(0, cols, chans),
+            tap_spec(1, cols, chans),
+            tap_spec(2, cols, chans),
+            pl.BlockSpec(w_time.shape, lambda step, slots: (0, 0, 0)),
+            vec, vec, vec, vec, vec,
+        ],
+        out_specs=pl.BlockSpec((1, cols, chans), lambda step, slots: (step, 0, 0)),
+    )
+    row = lambda v: v.reshape(1, chans).astype(jnp.float32)
+    return pl.pallas_call(
+        latent_kernel,
+        grid_spec=grid_spec,
+        out_shape=jax.ShapeDtypeStruct((out_frames, cols, chans), jnp.bfloat16),
+        compiler_params=pltpu.CompilerParams(dimension_semantics=("arbitrary",)),
+    )(
+        frame_slots, received, received, received, w_time,
+        row(mean_chan), row(scale_chan), row(norm_gain), row(norm_shift), row(time_bias),
+    )
+
+
 def spatial_conv(row_padded, w_spatial):
     out = lax.conv_general_dilated(
         row_padded,
@@ -164,15 +208,27 @@
     column = jnp.zeros((staged.shape[-1],), jnp.bfloat16).at[: coded.shape[0]].set(coded)
     payload = staged.at[:, cols, :].set(jnp.broadcast_to(column, (staged.shape[0], column.shape[0])))
     received = lax.all_to_all(payload[None], "tm", split_axis=1, concat_axis=0, tiled=True)
-    exchanged = received[:, :, :cols]
     partial = decode_stats(received[:, 0, cols, : coded.shape[0]], 2 * GROUPS)
     other = lax.ppermute(partial, "height", [(0, 1), (1, 0)])
     totals = partial + other
     sums, squares = totals[:GROUPS], totals[GROUPS:]
     cell_count = float(live_frames * clip_frames.shape[1] * height_count * cols * per_group)
-    live = jnp.take(exchanged, frame_slots, axis=0)
-    activated = normalize(live, sums, squares, cell_count, norm_gain, norm_shift)
-    latent = time_conv(activated, w_time, time_bias, out_frames)
+    group_mean = sums / cell_count
+    group_var = squares / cell_count - group_mean * group_mean
+    inv_scale = lax.rsqrt(group_var + 1e-06)
+    latent = latent_call(
+        frame_slots.astype(jnp.int32),
+        received[0] if received.ndim == 3 else received.reshape(received.shape[0], cols + 1, -1),
+        w_time,
+        jnp.repeat(group_mean, per_group),
+        jnp.repeat(inv_scale, per_group),
+        norm_gain,
+        norm_shift,
+        time_bias,
+        out_frames,
+        cols,
+    )
+    latent = latent.reshape(out_frames, 1, cols, latent.shape[-1])
     return latent.reshape(out_frames, 1, latent.shape[1], latent.shape[2], latent.shape[3])
 
 

time: 197 us -> 188 us (0.954); the launches traced: 193 us -> 188 us
  blocking collectives: 0 us -> 136 us
  waiting for transfers between devices: 126 us -> 0.18 us
  starting transfers between devices: 17.2 us -> 7.06 us
  Pallas kernels: 19 us -> 29.1 us
  local copies, waits for them, and re-layouts: 14.9 us -> 7.38 us
  other arithmetic: 11.4 us -> 7.4 us
  matrix products: 3.68 us -> 0 us
    all_to_all x0 -> x1, blocking collectives: none -> 136 us  [shards(): lax.all_to_all(payload[None], 'tm', split_axis=1, concat_axis=0, tiled=True)]
    all_to_all x1 -> x0, waiting for transfers between devices: 126 us -> none  [shards(): lax.all_to_all(payload[None], 'tm', split_axis=1, concat_axis=0, tiled=True)]
    all_to_all x1 -> x0, starting transfers between devices: 10.2 us -> none  [shards(): lax.all_to_all(payload[None], 'tm', split_axis=1, concat_axis=0, tiled=True)]
    pallas_call x0 -> x1, Pallas kernels: none -> 10.1 us  [latent_call(): pl.pallas_call(latent_kernel, grid_spec=grid_spec, out_shape=jax.ShapeDty...]
    slice x5 -> x0, local copies, waits for them, and re-layouts: 5.63 us -> none  [the longest x1 5.35 us: shards(): exchanged = received[:, :, :cols]]
    gather x1 -> x0, local copies, waits for them, and re-layouts: 5 us -> none  [shards(): live = jnp.take(exchanged, frame_slots, axis=0)]
    dot_general x1 -> x0, matrix products: 3.68 us -> none  [time_conv(): jnp.einsum('trwc,cd->trwd', stacked, weights, preferred_element_type=jnp....]
    convert_element_type x1 -> x0, other arithmetic: 3.62 us -> none  [normalize(): jax.nn.silu((values - mean_chan) * scale_chan * norm_gain + norm_shift)]
  transfers between devices with their start and end apart: 4 -> 3, of which waited for: 1 -> 1; matrix products, arithmetic and copies ran while one was open for 6% -> 1% of each run, Pallas kernels for 0% -> 0%
where the time goes in v5:
time: 188 us
  blocking collectives  136 us (72%)
  Pallas kernels  29.1 us (15%)
  other arithmetic  7.4 us (4%)
  local copies, waits for them, and re-layouts  7.38 us (4%)
  starting transfers between devices  7.06 us (4%)
    all_to_all x1, blocking collectives, shards(): lax.all_to_all(payload[None], 'tm', split_axis=1, concat_axis=0, tiled=True)  136 us
    pallas_call x1, Pallas kernels, conv_call(): pl.pallas_call(functools.partial(conv_kernel, chunk=chunk, cols=cols), gr...  19 us
    pallas_call x1, Pallas kernels, latent_call(): pl.pallas_call(latent_kernel, grid_spec=grid_spec, out_shape=jax.ShapeDty...  10.1 us
    ppermute x1, starting transfers between devices, with_halo(): lax.ppermute(lax.slice_in_dim(block, 0, width, axis=dim), axis, backward)  5.11 us
  transfers between devices with their start and end apart: 3, of which 1 were waited for; matrix products, arithmetic and copies ran while one was open for 1% of the time, Pallas kernels for 0%

profile of v5, /device:TPU:1, one launch (start us, length us, event | category | flops | bytes accessed | tf_op | source)
XLA Modules:
  0.0 187.8 jit_solution(8995069645843906036)
XLA Ops:
  0.0 0.9 fusion.4
  0.9 1.3 collective-permute-start
  2.2 5.1 %collective-permute-start.1 = (bf16[1,1,160,256]{3,2,1,0:T(8,128)(2,1)S(1)}, bf16[1,1,160,256]{3,2,1,0:T(8,128)(2,1)S(1)}, u32[]{:S(2)}, u32[]{:S(2)}) collective-permute-start(bf16[1,1,160,256]{3,2,1,0:T(8,128)(2,1)S(1)} %get-tuple-element.38), channel_id=1, source_target_pairs={{1,0},{3,2},{5,4},{7,6},{9,8},{11,10},{13,12},{15,14},{17,16},{19,... | collective-permute-start | bytes 245768 | tf_op jit(solution)/shard_map/ppermute | solution.py:22
  7.4 1.2 dynamic_slice.4
  9.3 0.0 collective-permute-done
  9.3 0.0 collective-permute-done.1
  9.3 3.6 %maximum_bitcast_fusion.x_ref = bf16[34,160,256]{2,1,0:T(8,128)(2,1)} fusion(bf16[1,1,160,256]{3,2,1,0:T(8,128)(2,1)S(1)} %collective-permute-done.1, bf16[1,32,160,256]{3,2,1,0:T(8,128)(2,1)} %param.11, bf16[1,1,160,256]{3,2,1,0:T(8,128)(2,1)S(1)} %collective-permute-done), kind=kLoop, calls=%fused_computation | loop fusion | flops 2785280 | bytes 5570560 | tf_op jit(solution)/shard_map/squeeze | solution.py:200
  12.9 19.0 %shard_map.73 = (bf16[32,161,512]{2,1,0:T(8,128)(2,1)}, f32[1,512]{1,0:T(1,128)}, f32[1,512]{1,0:T(1,128)}) custom-call(bf16[34,160,256]{2,1,0:T(8,128)(2,1)} %maximum_bitcast_fusion.x_ref, bf16[3,3,256,512]{3,2,1,0:T(8,128)(2,1)} %w_ref.2), custom_call_target="tpu_custom_call" | custom-call | tf_op jit(solution)/shard_map/pallas_call | solution.py:68
  31.9 0.5 broadcast.59
  32.4 1.2 reduce.11
  33.6 0.1 reshape.80
  33.7 1.2 reduce.10
  35.0 0.1 reshape.81
  35.0 0.1 reduce_sum.46
  35.1 0.1 reduce_sum.47
  35.3 0.1 fusion.3
  35.4 0.1 subtract_convert_fusion
  35.4 0.1 fusion.2
  35.5 0.7 broadcast_dynamic-update-slice_fusion
  36.2 0.0 copy-start.1
  36.2 135.9 %all_to_all.12 = bf16[1,32,161,512]{3,2,0,1:T(8,128)(2,1)S(1)} all-to-all(bf16[1,32,161,512]{3,2,0,1:T(8,128)(2,1)} %bitcast.19), channel_id=1, replica_groups=mesh['dp'=4,'tm'=32,'height'=2] {'tm'}, dimensions={1} | all-to-all | bytes 10551296 | tf_op jit(solution)/shard_map/all_to_all | solution.py:210
  172.1 0.0 copy-start
  172.1 2.4 %copy-done = bf16[1,32,161,512]{3,2,0,1:T(8,128)(2,1)} copy-done((bf16[1,32,161,512]{3,2,0,1:T(8,128)(2,1)}, bf16[1,32,161,512]{3,2,0,1:T(8,128)(2,1)S(1)}, u32[]{:S(2)}) %copy-start) | copy-done | bytes 5275672
  174.5 0.1 slice_reduce_fusion
  174.6 0.7 collective-permute-start.2
  175.3 0.0 copy-done.1
  175.3 0.6 select_reduce_fusion.slots_ref
  175.9 0.2 collective-permute-done.2
  176.1 0.1 add_rsqrt_fusion
  176.2 0.1 broadcast_in_dim.33
  176.3 0.7 reshape_reshape.10.scale_ref
  176.9 0.1 broadcast_in_dim.32
  177.0 0.7 reshape_reshape.9.mean_ref
  177.7 10.1 %shard_map.74 = bf16[9,160,512]{2,1,0:T(8,128)(2,1)} custom-call(s32[17]{0:T(128)} %select_reduce_fusion.slots_ref, bf16[32,161,512]{2,1,0:T(8,128)(2,1)} %bitcast.15, bf16[32,161,512]{2,1,0:T(8,128)(2,1)} %bitcast.16, bf16[32,161,512]{2,1,0:T(8,128)(2,1)} %bitcast.17, bf16[3,512,512]{2,1,0:T(8,128)(2,1)} %w_ref.3, f32[1,512]{1,0:T(1,128)} %reshape_reshape.9.mean_ref, ...), custom_call_target="tpu_custom_call" | custom-call | tf_op jit(solution)/shard_map/pallas_call | solution.py:122
  (4 shorter events, 0.0 us)
Async XLA Ops:
  0.9 8.3 %collective-permute-start = (bf16[1,1,160,256]{3,2,1,0:T(8,128)(2,1)S(1)}, bf16[1,1,160,256]{3,2,1,0:T(8,128)(2,1)S(1)}, u32[]{:S(2)}, u32[]{:S(2)}) collective-permute-start(bf16[1,1,160,256]{3,2,1,0:T(8,128)(2,1)S(1)} %get-tuple-element.37), channel_id=1, source_target_pairs={{0,1},{2,3},{4,5},{6,7},{8,9},{10,11},{12,13},{14,15},{16,17},{18,... | collective-permute-start | bytes 245768 | tf_op jit(solution)/shard_map/ppermute | solution.py:19
  2.2 7.0 %collective-permute-start.1 = (bf16[1,1,160,256]{3,2,1,0:T(8,128)(2,1)S(1)}, bf16[1,1,160,256]{3,2,1,0:T(8,128)(2,1)S(1)}, u32[]{:S(2)}, u32[]{:S(2)}) collective-permute-start(bf16[1,1,160,256]{3,2,1,0:T(8,128)(2,1)S(1)} %get-tuple-element.38), channel_id=1, source_target_pairs={{1,0},{3,2},{5,4},{7,6},{9,8},{11,10},{13,12},{15,14},{17,16},{19,... | collective-permute-start | bytes 245768 | tf_op jit(solution)/shard_map/ppermute | solution.py:22
  36.2 139.1 %copy-start.1 = (s32[32]{0:T(128)S(1)}, s32[32]{0:T(128)}, u32[]{:S(2)}) copy-start(s32[32]{0:T(128)} %param.12) | copy-start | bytes 388
  172.1 2.4 %copy-start = (bf16[1,32,161,512]{3,2,0,1:T(8,128)(2,1)}, bf16[1,32,161,512]{3,2,0,1:T(8,128)(2,1)S(1)}, u32[]{:S(2)}) copy-start(bf16[1,32,161,512]{3,2,0,1:T(8,128)(2,1)S(1)} %all_to_all.12) | copy-start | bytes 15826948
  174.6 1.5 collective-permute-start.2

commit v6 on v5

--- a/solution.py
+++ b/solution.py
@@ -86,14 +86,25 @@
     )(x, w)
 
 
-def latent_kernel(slots_ref, x0_ref, x1_ref, x2_ref, w_ref, mean_ref, scale_ref, gain_ref, shift_ref, bias_ref, out_ref):
-    running = bias_ref[...]
-    for time_tap, x_ref in enumerate((x0_ref, x1_ref, x2_ref)):
+def latent_kernel(slots_ref, x1_ref, x2_ref, w_ref, mean_ref, scale_ref, gain_ref, shift_ref, bias_ref, out_ref, prev_ref):
+    def activate(x_ref):
         values = x_ref[0].astype(jnp.float32)
         normed = (values - mean_ref[...]) * scale_ref[...] * gain_ref[...] + shift_ref[...]
-        activated = jax.nn.silu(normed).astype(jnp.bfloat16)
-        running = running + jnp.dot(activated, w_ref[time_tap], preferred_element_type=jnp.float32)
+        return jax.nn.silu(normed).astype(jnp.bfloat16)
+
+    odd = activate(x1_ref)
+    even = activate(x2_ref)
+
+    @pl.when(pl.program_id(0) == 0)
+    def _():
+        prev_ref[...] = even
+
+    running = bias_ref[...]
+    running = running + jnp.dot(prev_ref[...], w_ref[0], preferred_element_type=jnp.float32)
+    running = running + jnp.dot(odd, w_ref[1], preferred_element_type=jnp.float32)
+    running = running + jnp.dot(even, w_ref[2], preferred_element_type=jnp.float32)
     out_ref[0] = running.astype(jnp.bfloat16)
+    prev_ref[...] = even
 
 
 def tap_spec(time_tap, cols, chans):
@@ -110,13 +121,13 @@
         num_scalar_prefetch=1,
         grid=(out_frames,),
         in_specs=[
-            tap_spec(0, cols, chans),
             tap_spec(1, cols, chans),
             tap_spec(2, cols, chans),
             pl.BlockSpec(w_time.shape, lambda step, slots: (0, 0, 0)),
             vec, vec, vec, vec, vec,
         ],
         out_specs=pl.BlockSpec((1, cols, chans), lambda step, slots: (step, 0, 0)),
+        scratch_shapes=[pltpu.VMEM((cols, chans), jnp.bfloat16)],
     )
     row = lambda v: v.reshape(1, chans).astype(jnp.float32)
     return pl.pallas_call(
@@ -125,7 +136,7 @@
         out_shape=jax.ShapeDtypeStruct((out_frames, cols, chans), jnp.bfloat16),
         compiler_params=pltpu.CompilerParams(dimension_semantics=("arbitrary",)),
     )(
-        frame_slots, received, received, received, w_time,
+        frame_slots, received, received, w_time,
         row(mean_chan), row(scale_chan), row(norm_gain), row(norm_shift), row(time_bias),
     )
 

time: 188 us -> 189 us (level)
  no operation moved by 1% of the time
where the time goes in v6:
time: 189 us; the launch traced here: 188 us
  blocking collectives  136 us (72%)
  Pallas kernels  29.6 us (16%)
  other arithmetic  7.4 us (4%)
  local copies, waits for them, and re-layouts  7.38 us (4%)
  starting transfers between devices  7.06 us (4%)
    all_to_all x1, blocking collectives, shards(): lax.all_to_all(payload[None], 'tm', split_axis=1, concat_axis=0, tiled=True)  136 us
    pallas_call x1, Pallas kernels, conv_call(): pl.pallas_call(functools.partial(conv_kernel, chunk=chunk, cols=cols), gr...  19 us
    pallas_call x1, Pallas kernels, latent_call(): pl.pallas_call(latent_kernel, grid_spec=grid_spec, out_shape=jax.ShapeDty...  10.6 us
    ppermute x1, starting transfers between devices, with_halo(): lax.ppermute(lax.slice_in_dim(block, 0, width, axis=dim), axis, backward)  5.11 us
  transfers between devices with their start and end apart: 3, of which 1 were waited for; matrix products, arithmetic and copies ran while one was open for 1% of the time, Pallas kernels for 0%

profile of v6, /device:TPU:1, one launch (start us, length us, event | category | flops | bytes accessed | tf_op | source)
XLA Modules:
  0.0 188.3 jit_solution(9034482947147085373)
XLA Ops:
  0.0 0.9 fusion.4
  0.9 1.3 collective-permute-start
  2.2 5.1 %collective-permute-start.1 = (bf16[1,1,160,256]{3,2,1,0:T(8,128)(2,1)S(1)}, bf16[1,1,160,256]{3,2,1,0:T(8,128)(2,1)S(1)}, u32[]{:S(2)}, u32[]{:S(2)}) collective-permute-start(bf16[1,1,160,256]{3,2,1,0:T(8,128)(2,1)S(1)} %get-tuple-element.38), channel_id=1, source_target_pairs={{1,0},{3,2},{5,4},{7,6},{9,8},{11,10},{13,12},{15,14},{17,16},{19,... | collective-permute-start | bytes 245768 | tf_op jit(solution)/shard_map/ppermute | solution.py:22
  7.4 1.2 dynamic_slice.4
  9.3 0.0 collective-permute-done
  9.3 0.0 collective-permute-done.1
  9.3 3.6 %maximum_bitcast_fusion.x_ref = bf16[34,160,256]{2,1,0:T(8,128)(2,1)} fusion(bf16[1,1,160,256]{3,2,1,0:T(8,128)(2,1)S(1)} %collective-permute-done.1, bf16[1,32,160,256]{3,2,1,0:T(8,128)(2,1)} %param.11, bf16[1,1,160,256]{3,2,1,0:T(8,128)(2,1)S(1)} %collective-permute-done), kind=kLoop, calls=%fused_computation | loop fusion | flops 2785280 | bytes 5570560 | tf_op jit(solution)/shard_map/squeeze | solution.py:211
  12.9 19.0 %shard_map.73 = (bf16[32,161,512]{2,1,0:T(8,128)(2,1)}, f32[1,512]{1,0:T(1,128)}, f32[1,512]{1,0:T(1,128)}) custom-call(bf16[34,160,256]{2,1,0:T(8,128)(2,1)} %maximum_bitcast_fusion.x_ref, bf16[3,3,256,512]{3,2,1,0:T(8,128)(2,1)} %w_ref.2), custom_call_target="tpu_custom_call" | custom-call | tf_op jit(solution)/shard_map/pallas_call | solution.py:68
  31.9 0.5 broadcast.59
  32.4 1.2 reduce.11
  33.6 0.1 reshape.80
  33.7 1.2 reduce.10
  35.0 0.1 reshape.81
  35.0 0.1 reduce_sum.46
  35.1 0.1 reduce_sum.47
  35.3 0.1 fusion.3
  35.4 0.1 subtract_convert_fusion
  35.4 0.1 fusion.2
  35.5 0.7 broadcast_dynamic-update-slice_fusion
  36.2 0.0 copy-start.1
  36.2 135.9 %all_to_all.12 = bf16[1,32,161,512]{3,2,0,1:T(8,128)(2,1)S(1)} all-to-all(bf16[1,32,161,512]{3,2,0,1:T(8,128)(2,1)} %bitcast.18), channel_id=1, replica_groups=mesh['dp'=4,'tm'=32,'height'=2] {'tm'}, dimensions={1} | all-to-all | bytes 10551296 | tf_op jit(solution)/shard_map/all_to_all | solution.py:221
  172.1 0.0 copy-start
  172.1 2.4 %copy-done = bf16[1,32,161,512]{3,2,0,1:T(8,128)(2,1)} copy-done((bf16[1,32,161,512]{3,2,0,1:T(8,128)(2,1)}, bf16[1,32,161,512]{3,2,0,1:T(8,128)(2,1)S(1)}, u32[]{:S(2)}) %copy-start) | copy-done | bytes 5275672
  174.5 0.1 slice_reduce_fusion
  174.6 0.7 collective-permute-start.2
  175.3 0.0 copy-done.1
  175.3 0.6 select_reduce_fusion.slots_ref
  175.9 0.2 collective-permute-done.2
  176.1 0.1 add_rsqrt_fusion
  176.2 0.1 broadcast_in_dim.33
  176.3 0.7 reshape_reshape.10.scale_ref
  176.9 0.1 broadcast_in_dim.32
  177.0 0.7 reshape_reshape.9.mean_ref
  177.7 10.6 %shard_map.74 = bf16[9,160,512]{2,1,0:T(8,128)(2,1)} custom-call(s32[17]{0:T(128)} %select_reduce_fusion.slots_ref, bf16[32,161,512]{2,1,0:T(8,128)(2,1)} %bitcast.15, bf16[32,161,512]{2,1,0:T(8,128)(2,1)} %bitcast.16, bf16[3,512,512]{2,1,0:T(8,128)(2,1)} %w_ref.3, f32[1,512]{1,0:T(1,128)} %reshape_reshape.9.mean_ref, f32[1,512]{1,0:T(1,128)} %reshape_reshape.10.scale_ref, ...), custom_call_target="tpu_custom_call" | custom-call | tf_op jit(solution)/shard_map/pallas_call | solution.py:133
  (4 shorter events, 0.0 us)
Async XLA Ops:
  0.9 8.3 %collective-permute-start = (bf16[1,1,160,256]{3,2,1,0:T(8,128)(2,1)S(1)}, bf16[1,1,160,256]{3,2,1,0:T(8,128)(2,1)S(1)}, u32[]{:S(2)}, u32[]{:S(2)}) collective-permute-start(bf16[1,1,160,256]{3,2,1,0:T(8,128)(2,1)S(1)} %get-tuple-element.37), channel_id=1, source_target_pairs={{0,1},{2,3},{4,5},{6,7},{8,9},{10,11},{12,13},{14,15},{16,17},{18,... | collective-permute-start | bytes 245768 | tf_op jit(solution)/shard_map/ppermute | solution.py:19
  2.2 7.0 %collective-permute-start.1 = (bf16[1,1,160,256]{3,2,1,0:T(8,128)(2,1)S(1)}, bf16[1,1,160,256]{3,2,1,0:T(8,128)(2,1)S(1)}, u32[]{:S(2)}, u32[]{:S(2)}) collective-permute-start(bf16[1,1,160,256]{3,2,1,0:T(8,128)(2,1)S(1)} %get-tuple-element.38), channel_id=1, source_target_pairs={{1,0},{3,2},{5,4},{7,6},{9,8},{11,10},{13,12},{15,14},{17,16},{19,... | collective-permute-start | bytes 245768 | tf_op jit(solution)/shard_map/ppermute | solution.py:22
  36.2 139.1 %copy-start.1 = (s32[32]{0:T(128)S(1)}, s32[32]{0:T(128)}, u32[]{:S(2)}) copy-start(s32[32]{0:T(128)} %param.12) | copy-start | bytes 388
  172.1 2.4 %copy-start = (bf16[1,32,161,512]{3,2,0,1:T(8,128)(2,1)}, bf16[1,32,161,512]{3,2,0,1:T(8,128)(2,1)S(1)}, u32[]{:S(2)}) copy-start(bf16[1,32,161,512]{3,2,0,1:T(8,128)(2,1)S(1)} %all_to_all.12) | copy-start | bytes 15826948
  174.6 1.5 collective-permute-start.2

commit v7 on v5

--- a/solution.py
+++ b/solution.py
@@ -86,49 +86,46 @@
     )(x, w)
 
 
-def latent_kernel(slots_ref, x0_ref, x1_ref, x2_ref, w_ref, mean_ref, scale_ref, gain_ref, shift_ref, bias_ref, out_ref):
-    running = bias_ref[...]
-    for time_tap, x_ref in enumerate((x0_ref, x1_ref, x2_ref)):
-        values = x_ref[0].astype(jnp.float32)
+def latent_kernel(slots_ref, x_ref, w_ref, mean_ref, scale_ref, gain_ref, shift_ref, bias_ref, out_ref, tap0_ref, tap1_ref, tap2_ref):
+    live = 2 * out_ref.shape[0] - 1
+    cols, chans = out_ref.shape[1], out_ref.shape[2]
+    for frame in range(live):
+        values = x_ref[slots_ref[frame], pl.ds(0, cols), :].astype(jnp.float32)
         normed = (values - mean_ref[...]) * scale_ref[...] * gain_ref[...] + shift_ref[...]
         activated = jax.nn.silu(normed).astype(jnp.bfloat16)
-        running = running + jnp.dot(activated, w_ref[time_tap], preferred_element_type=jnp.float32)
-    out_ref[0] = running.astype(jnp.bfloat16)
-
-
-def tap_spec(time_tap, cols, chans):
-    def index(step, slots):
-        return (slots[jnp.maximum(2 * step + time_tap - 2, 0)], 0, 0)
-
-    return pl.BlockSpec((1, cols, chans), index)
+        if frame == 0:
+            tap0_ref[0] = activated
+            tap1_ref[0] = activated
+        if frame % 2 == 0:
+            tap2_ref[frame // 2] = activated
+            if frame // 2 + 1 < out_ref.shape[0]:
+                tap0_ref[frame // 2 + 1] = activated
+        else:
+            tap1_ref[(frame + 1) // 2] = activated
+    rows = out_ref.shape[0] * cols
+    running = bias_ref[...]
+    for time_tap, tap_ref in enumerate((tap0_ref, tap1_ref, tap2_ref)):
+        block = tap_ref[...].reshape(rows, chans)
+        running = running + jnp.dot(block, w_ref[time_tap], preferred_element_type=jnp.float32)
+    out_ref[...] = running.astype(jnp.bfloat16).reshape(out_ref.shape)
 
 
 def latent_call(frame_slots, received, w_time, mean_chan, scale_chan, norm_gain, norm_shift, time_bias, out_frames, cols):
     chans = received.shape[-1]
-    vec = pl.BlockSpec((1, chans), lambda step, slots: (0, 0))
-    grid_spec = pltpu.PrefetchScalarGridSpec(
-        num_scalar_prefetch=1,
-        grid=(out_frames,),
-        in_specs=[
-            tap_spec(0, cols, chans),
-            tap_spec(1, cols, chans),
-            tap_spec(2, cols, chans),
-            pl.BlockSpec(w_time.shape, lambda step, slots: (0, 0, 0)),
-            vec, vec, vec, vec, vec,
-        ],
-        out_specs=pl.BlockSpec((1, cols, chans), lambda step, slots: (step, 0, 0)),
-    )
+    vmem = pltpu.MemorySpace.VMEM if hasattr(pltpu, "MemorySpace") else pltpu.TPUMemorySpace.VMEM
+    smem = pltpu.MemorySpace.SMEM if hasattr(pltpu, "MemorySpace") else pltpu.TPUMemorySpace.SMEM
     row = lambda v: v.reshape(1, chans).astype(jnp.float32)
+    tap = pltpu.VMEM((out_frames, cols, chans), jnp.bfloat16)
     return pl.pallas_call(
         latent_kernel,
-        grid_spec=grid_spec,
+        in_specs=[pl.BlockSpec(memory_space=smem)] + [pl.BlockSpec(memory_space=vmem)] * 7,
+        out_specs=pl.BlockSpec(memory_space=vmem),
         out_shape=jax.ShapeDtypeStruct((out_frames, cols, chans), jnp.bfloat16),
-        compiler_params=pltpu.CompilerParams(dimension_semantics=("arbitrary",)),
+        scratch_shapes=[tap, tap, tap],
     )(
-        frame_slots, received, received, received, w_time,
+        frame_slots, received, w_time,
         row(mean_chan), row(scale_chan), row(norm_gain), row(norm_shift), row(time_bias),
     )
-
 
 def spatial_conv(row_padded, w_spatial):
     out = lax.conv_general_dilated(
@@ -218,7 +215,7 @@
     inv_scale = lax.rsqrt(group_var + 1e-06)
     latent = latent_call(
         frame_slots.astype(jnp.int32),
-        received[0] if received.ndim == 3 else received.reshape(received.shape[0], cols + 1, -1),
+        received.reshape(received.shape[0], cols + 1, -1),
         w_time,
         jnp.repeat(group_mean, per_group),
         jnp.repeat(inv_scale, per_group),

time: 188 us -> 185 us (0.984)
  Pallas kernels: 29.1 us -> 25.9 us
    pallas_call x1, Pallas kernels: 10.1 us -> 6.85 us  [latent_call(): pl.pallas_call(latent_kernel, in_specs=[pl.BlockSpec(memory_space=smem)]...]
where the time goes in v7:
time: 185 us
  blocking collectives  136 us (74%)
  Pallas kernels  25.9 us (14%)
  other arithmetic  7.4 us (4%)
  local copies, waits for them, and re-layouts  7.38 us (4%)
  starting transfers between devices  7.06 us (4%)
    all_to_all x1, blocking collectives, shards(): lax.all_to_all(payload[None], 'tm', split_axis=1, concat_axis=0, tiled=True)  136 us
    pallas_call x1, Pallas kernels, conv_call(): pl.pallas_call(functools.partial(conv_kernel, chunk=chunk, cols=cols), gr...  19 us
    pallas_call x1, Pallas kernels, latent_call(): pl.pallas_call(latent_kernel, in_specs=[pl.BlockSpec(memory_space=smem)]...  6.85 us
    ppermute x1, starting transfers between devices, with_halo(): lax.ppermute(lax.slice_in_dim(block, 0, width, axis=dim), axis, backward)  5.11 us
  transfers between devices with their start and end apart: 3, of which 1 were waited for; matrix products, arithmetic and copies ran while one was open for 1% of the time, Pallas kernels for 0%

profile of v7, /device:TPU:1, one launch (start us, length us, event | category | flops | bytes accessed | tf_op | source)
XLA Modules:
  0.0 184.5 jit_solution(16143811844607535704)
XLA Ops:
  0.0 0.9 fusion.4
  0.9 1.3 collective-permute-start
  2.2 5.1 %collective-permute-start.1 = (bf16[1,1,160,256]{3,2,1,0:T(8,128)(2,1)S(1)}, bf16[1,1,160,256]{3,2,1,0:T(8,128)(2,1)S(1)}, u32[]{:S(2)}, u32[]{:S(2)}) collective-permute-start(bf16[1,1,160,256]{3,2,1,0:T(8,128)(2,1)S(1)} %get-tuple-element.38), channel_id=1, source_target_pairs={{1,0},{3,2},{5,4},{7,6},{9,8},{11,10},{13,12},{15,14},{17,16},{19,... | collective-permute-start | bytes 245768 | tf_op jit(solution)/shard_map/ppermute | solution.py:22
  7.4 1.2 dynamic_slice.4
  9.3 0.0 collective-permute-done
  9.3 0.0 collective-permute-done.1
  9.3 3.6 %maximum_bitcast_fusion.x_ref = bf16[34,160,256]{2,1,0:T(8,128)(2,1)} fusion(bf16[1,1,160,256]{3,2,1,0:T(8,128)(2,1)S(1)} %collective-permute-done.1, bf16[1,32,160,256]{3,2,1,0:T(8,128)(2,1)} %param.11, bf16[1,1,160,256]{3,2,1,0:T(8,128)(2,1)S(1)} %collective-permute-done), kind=kLoop, calls=%fused_computation | loop fusion | flops 2785280 | bytes 5570560 | tf_op jit(solution)/shard_map/squeeze | solution.py:197
  12.9 19.0 %shard_map.73 = (bf16[32,161,512]{2,1,0:T(8,128)(2,1)}, f32[1,512]{1,0:T(1,128)}, f32[1,512]{1,0:T(1,128)}) custom-call(bf16[34,160,256]{2,1,0:T(8,128)(2,1)} %maximum_bitcast_fusion.x_ref, bf16[3,3,256,512]{3,2,1,0:T(8,128)(2,1)} %w_ref.2), custom_call_target="tpu_custom_call" | custom-call | tf_op jit(solution)/shard_map/pallas_call | solution.py:68
  31.9 0.5 broadcast.59
  32.4 1.2 reduce.11
  33.6 0.1 reshape.80
  33.7 1.2 reduce.10
  35.0 0.1 reshape.81
  35.0 0.1 reduce_sum.46
  35.1 0.1 reduce_sum.47
  35.3 0.1 fusion.3
  35.4 0.1 subtract_convert_fusion
  35.4 0.1 fusion.2
  35.5 0.7 broadcast_dynamic-update-slice_fusion
  36.2 0.0 copy-start.1
  36.2 135.9 %all_to_all.12 = bf16[1,32,161,512]{3,2,0,1:T(8,128)(2,1)S(1)} all-to-all(bf16[1,32,161,512]{3,2,0,1:T(8,128)(2,1)} %bitcast.17), channel_id=1, replica_groups=mesh['dp'=4,'tm'=32,'height'=2] {'tm'}, dimensions={1} | all-to-all | bytes 10551296 | tf_op jit(solution)/shard_map/all_to_all | solution.py:207
  172.1 0.0 copy-start
  172.1 2.4 %copy-done = bf16[1,32,161,512]{3,2,0,1:T(8,128)(2,1)} copy-done((bf16[1,32,161,512]{3,2,0,1:T(8,128)(2,1)}, bf16[1,32,161,512]{3,2,0,1:T(8,128)(2,1)S(1)}, u32[]{:S(2)}) %copy-start) | copy-done | bytes 5275672
  174.5 0.1 slice_reduce_fusion
  174.6 0.7 collective-permute-start.2
  175.3 0.0 copy-done.1
  175.3 0.6 select_reduce_fusion.slots_ref
  175.9 0.2 collective-permute-done.2
  176.1 0.1 add_rsqrt_fusion
  176.2 0.1 broadcast_in_dim.33
  176.3 0.7 reshape_reshape.10.scale_ref
  176.9 0.1 broadcast_in_dim.32
  177.0 0.7 reshape_reshape.9.mean_ref
  177.7 6.8 %shard_map.74 = bf16[9,160,512]{2,1,0:T(8,128)(2,1)} custom-call(s32[17]{0:T(128)} %select_reduce_fusion.slots_ref, bf16[32,161,512]{2,1,0:T(8,128)(2,1)} %bitcast.15, bf16[3,512,512]{2,1,0:T(8,128)(2,1)} %w_ref.3, f32[1,512]{1,0:T(1,128)} %reshape_reshape.9.mean_ref, f32[1,512]{1,0:T(1,128)} %reshape_reshape.10.scale_ref, f32[1,512]{1,0:T(1,128)} %bitcast.19, ...), custom_call_target="tpu_custom_call" | custom-call | tf_op jit(solution)/shard_map/pallas_call | solution.py:119
  (4 shorter events, 0.0 us)
Async XLA Ops:
  0.9 8.3 %collective-permute-start = (bf16[1,1,160,256]{3,2,1,0:T(8,128)(2,1)S(1)}, bf16[1,1,160,256]{3,2,1,0:T(8,128)(2,1)S(1)}, u32[]{:S(2)}, u32[]{:S(2)}) collective-permute-start(bf16[1,1,160,256]{3,2,1,0:T(8,128)(2,1)S(1)} %get-tuple-element.37), channel_id=1, source_target_pairs={{0,1},{2,3},{4,5},{6,7},{8,9},{10,11},{12,13},{14,15},{16,17},{18,... | collective-permute-start | bytes 245768 | tf_op jit(solution)/shard_map/ppermute | solution.py:19
  2.2 7.0 %collective-permute-start.1 = (bf16[1,1,160,256]{3,2,1,0:T(8,128)(2,1)S(1)}, bf16[1,1,160,256]{3,2,1,0:T(8,128)(2,1)S(1)}, u32[]{:S(2)}, u32[]{:S(2)}) collective-permute-start(bf16[1,1,160,256]{3,2,1,0:T(8,128)(2,1)S(1)} %get-tuple-element.38), channel_id=1, source_target_pairs={{1,0},{3,2},{5,4},{7,6},{9,8},{11,10},{13,12},{15,14},{17,16},{19,... | collective-permute-start | bytes 245768 | tf_op jit(solution)/shard_map/ppermute | solution.py:22
  36.2 139.1 %copy-start.1 = (s32[32]{0:T(128)S(1)}, s32[32]{0:T(128)}, u32[]{:S(2)}) copy-start(s32[32]{0:T(128)} %param.12) | copy-start | bytes 388
  172.1 2.4 %copy-start = (bf16[1,32,161,512]{3,2,0,1:T(8,128)(2,1)}, bf16[1,32,161,512]{3,2,0,1:T(8,128)(2,1)S(1)}, u32[]{:S(2)}) copy-start(bf16[1,32,161,512]{3,2,0,1:T(8,128)(2,1)S(1)} %all_to_all.12) | copy-start | bytes 15826948
  174.6 1.5 collective-permute-start.2

commit v8 on v7

--- a/solution.py
+++ b/solution.py
@@ -48,8 +48,12 @@
     right = jnp.where(col == cols - 1, 0.0, pltpu.roll(parts[2], m - 1, 0))
     total = (left + parts[1]) + right
     rounded = total.astype(jnp.bfloat16)
-    out_ref[:, 0:cols, :] = rounded.reshape(chunk, cols, -1)
-    out_ref[:, cols:cols + 1, :] = jnp.zeros((chunk, 1, out_ref.shape[-1]), jnp.bfloat16)
+    lanes = out_ref.shape[-1]
+    for quarter in range(rounded.shape[-1] // lanes):
+        piece = rounded[:, quarter * lanes : (quarter + 1) * lanes]
+        out_ref[:, quarter * cols : (quarter + 1) * cols, :] = piece.reshape(chunk, cols, lanes)
+    tail = out_ref.shape[1] - 1
+    out_ref[:, tail : tail + 1, :] = jnp.zeros((chunk, 1, lanes), jnp.bfloat16)
     values = rounded.astype(jnp.float32)
 
     @pl.when(step == 0)
@@ -60,11 +64,12 @@
     sum_ref[...] += jnp.sum(values, axis=0, keepdims=True)
     sq_ref[...] += jnp.sum(values * values, axis=0, keepdims=True)
 
-def conv_call(x, w, chunk=8):
+def conv_call(x, w, chunk=8, lanes=128):
     rows = x.shape[0] - 2
     cols = x.shape[1]
     cin = x.shape[2]
     cout = w.shape[-1]
+    stacked = cols * (cout // lanes) + 1
     return pl.pallas_call(
         functools.partial(conv_kernel, chunk=chunk, cols=cols),
         grid=(rows // chunk,),
@@ -73,12 +78,12 @@
             pl.BlockSpec((3, 3, cin, cout), lambda i: (0, 0, 0, 0)),
         ],
         out_specs=[
-            pl.BlockSpec((chunk, cols + 1, cout), lambda i: (i, 0, 0)),
+            pl.BlockSpec((chunk, stacked, lanes), lambda i: (i, 0, 0)),
             pl.BlockSpec((1, cout), lambda i: (0, 0)),
             pl.BlockSpec((1, cout), lambda i: (0, 0)),
         ],
         out_shape=[
-            jax.ShapeDtypeStruct((rows, cols + 1, cout), jnp.bfloat16),
+            jax.ShapeDtypeStruct((rows, stacked, lanes), jnp.bfloat16),
             jax.ShapeDtypeStruct((1, cout), jnp.float32),
             jax.ShapeDtypeStruct((1, cout), jnp.float32),
         ],
@@ -90,7 +95,10 @@
     live = 2 * out_ref.shape[0] - 1
     cols, chans = out_ref.shape[1], out_ref.shape[2]
     for frame in range(live):
-        values = x_ref[slots_ref[frame], pl.ds(0, cols), :].astype(jnp.float32)
+        slot = slots_ref[frame]
+        lanes = x_ref.shape[-1]
+        pieces = [x_ref[slot, pl.ds(q * cols, cols), :] for q in range(chans // lanes)]
+        values = jnp.concatenate(pieces, axis=-1).astype(jnp.float32)
         normed = (values - mean_ref[...]) * scale_ref[...] * gain_ref[...] + shift_ref[...]
         activated = jax.nn.silu(normed).astype(jnp.bfloat16)
         if frame == 0:
@@ -111,7 +119,7 @@
 
 
 def latent_call(frame_slots, received, w_time, mean_chan, scale_chan, norm_gain, norm_shift, time_bias, out_frames, cols):
-    chans = received.shape[-1]
+    chans = w_time.shape[-1]
     vmem = pltpu.MemorySpace.VMEM if hasattr(pltpu, "MemorySpace") else pltpu.TPUMemorySpace.VMEM
     smem = pltpu.MemorySpace.SMEM if hasattr(pltpu, "MemorySpace") else pltpu.TPUMemorySpace.SMEM
     row = lambda v: v.reshape(1, chans).astype(jnp.float32)
@@ -195,17 +203,18 @@
     frame_slots = slot_lookup(frame_of_slot, live_frames)
     padded = with_halo(clip_frames, (("height", 1),), 1)
     staged, chan_sums, chan_squares = conv_call(padded[0], w_spatial)
-    cols = staged.shape[1] - 1
+    cols = padded.shape[2]
+    tail = staged.shape[1] - 1
     own_frame = lax.dynamic_index_in_dim(frame_of_slot, lax.axis_index("tm"), 0, keepdims=False)
     weight = jnp.where(own_frame >= 0, 1.0, 0.0).astype(jnp.float32)
-    per_group = staged.shape[-1] // GROUPS
+    per_group = w_spatial.shape[-1] // GROUPS
     sums = chan_sums.reshape(GROUPS, per_group).sum(axis=1) * weight
     squares = chan_squares.reshape(GROUPS, per_group).sum(axis=1) * weight
     coded = encode_stats(jnp.concatenate([sums, squares]))
     column = jnp.zeros((staged.shape[-1],), jnp.bfloat16).at[: coded.shape[0]].set(coded)
-    payload = staged.at[:, cols, :].set(jnp.broadcast_to(column, (staged.shape[0], column.shape[0])))
+    payload = staged.at[:, tail, :].set(jnp.broadcast_to(column, (staged.shape[0], column.shape[0])))
     received = lax.all_to_all(payload[None], "tm", split_axis=1, concat_axis=0, tiled=True)
-    partial = decode_stats(received[:, 0, cols, : coded.shape[0]], 2 * GROUPS)
+    partial = decode_stats(received[:, 0, tail, : coded.shape[0]], 2 * GROUPS)
     other = lax.ppermute(partial, "height", [(0, 1), (1, 0)])
     totals = partial + other
     sums, squares = totals[:GROUPS], totals[GROUPS:]
@@ -215,7 +224,7 @@
     inv_scale = lax.rsqrt(group_var + 1e-06)
     latent = latent_call(
         frame_slots.astype(jnp.int32),
-        received.reshape(received.shape[0], cols + 1, -1),
+        received.reshape(received.shape[0], tail + 1, -1),
         w_time,
         jnp.repeat(group_mean, per_group),
         jnp.repeat(inv_scale, per_group),

time: 185 us -> 181 us (0.978)
  blocking collectives: 136 us -> 132 us
    all_to_all x1, blocking collectives: 136 us -> 132 us  [shards(): lax.all_to_all(payload[None], 'tm', split_axis=1, concat_axis=0, tiled=True)]
where the time goes in v8:
time: 181 us
  blocking collectives  132 us (73%)
  Pallas kernels  25.7 us (14%)
  other arithmetic  7.51 us (4%)
  local copies, waits for them, and re-layouts  7.28 us (4%)
  starting transfers between devices  6.89 us (4%)
    all_to_all x1, blocking collectives, shards(): lax.all_to_all(payload[None], 'tm', split_axis=1, concat_axis=0, tiled=True)  132 us
    pallas_call x1, Pallas kernels, conv_call(): pl.pallas_call(functools.partial(conv_kernel, chunk=chunk, cols=cols), gr...  18.9 us
    pallas_call x1, Pallas kernels, latent_call(): pl.pallas_call(latent_kernel, in_specs=[pl.BlockSpec(memory_space=smem)]...  6.79 us
    ppermute x1, starting transfers between devices, with_halo(): lax.ppermute(lax.slice_in_dim(block, 0, width, axis=dim), axis, backward)  5.11 us
    squeeze x1, other arithmetic, shards(): staged, chan_sums, chan_squares = conv_call(padded[0], w_spatial)  3.62 us
  transfers between devices with their start and end apart: 3, of which 1 were waited for; matrix products, arithmetic and copies ran while one was open for 1% of the time, Pallas kernels for 0%

profile of v8, /device:TPU:1, one launch (start us, length us, event | category | flops | bytes accessed | tf_op | source)
XLA Modules:
  0.0 180.8 jit_solution(4883242625206770879)
XLA Ops:
  0.0 0.9 fusion.1
  0.9 1.3 collective-permute-start
  2.2 5.1 %collective-permute-start.1 = (bf16[1,1,160,256]{3,2,1,0:T(8,128)(2,1)S(1)}, bf16[1,1,160,256]{3,2,1,0:T(8,128)(2,1)S(1)}, u32[]{:S(2)}, u32[]{:S(2)}) collective-permute-start(bf16[1,1,160,256]{3,2,1,0:T(8,128)(2,1)S(1)} %get-tuple-element.46), channel_id=1, source_target_pairs={{1,0},{3,2},{5,4},{7,6},{9,8},{11,10},{13,12},{15,14},{17,16},{19,... | collective-permute-start | bytes 245768 | tf_op jit(solution)/shard_map/ppermute | solution.py:22
  7.4 1.2 dynamic_slice.4
  9.3 0.0 collective-permute-done
  9.3 0.0 collective-permute-done.1
  9.3 3.6 %maximum_bitcast_fusion.x_ref = bf16[34,160,256]{2,1,0:T(8,128)(2,1)} fusion(bf16[1,1,160,256]{3,2,1,0:T(8,128)(2,1)S(1)} %collective-permute-done.1, bf16[1,32,160,256]{3,2,1,0:T(8,128)(2,1)} %param.13, bf16[1,1,160,256]{3,2,1,0:T(8,128)(2,1)S(1)} %collective-permute-done), kind=kLoop, calls=%fused_computation | loop fusion | flops 2785280 | bytes 5570560 | tf_op jit(solution)/shard_map/squeeze | solution.py:205
  12.9 18.9 %shard_map.78 = (bf16[32,641,128]{2,1,0:T(8,128)(2,1)}, f32[1,512]{1,0:T(1,128)}, f32[1,512]{1,0:T(1,128)}) custom-call(bf16[34,160,256]{2,1,0:T(8,128)(2,1)} %maximum_bitcast_fusion.x_ref, bf16[3,3,256,512]{3,2,1,0:T(8,128)(2,1)} %w_ref.2), custom_call_target="tpu_custom_call" | custom-call | tf_op jit(solution)/shard_map/pallas_call | solution.py:73
  31.8 0.5 broadcast.52
  32.4 1.3 reduce.11
  33.7 0.1 reshape.84
  33.8 1.3 reduce.10
  35.0 0.1 reshape.85
  35.1 0.1 reduce_sum.46
  35.2 0.1 reduce_sum.47
  35.4 0.1 fusion
  35.5 0.1 subtract_convert_fusion
  35.5 0.1 pad_maximum_fusion.1
  35.6 0.6 broadcast_dynamic-update-slice_fusion
  36.2 0.0 copy-start.1
  36.2 132.5 %all_to_all.12 = bf16[1,32,641,128]{3,2,0,1:T(8,128)(2,1)S(1)} all-to-all(bf16[1,32,641,128]{3,2,0,1:T(8,128)(2,1)} %bitcast.17), channel_id=1, replica_groups=mesh['dp'=4,'tm'=32,'height'=2] {'tm'}, dimensions={1} | all-to-all | bytes 10502144 | tf_op jit(solution)/shard_map/all_to_all | solution.py:216
  168.7 0.0 copy-start
  168.7 2.3 %copy-done = bf16[1,32,641,128]{3,2,0,1:T(8,128)(2,1)} copy-done((bf16[1,32,641,128]{3,2,0,1:T(8,128)(2,1)}, bf16[1,32,641,128]{3,2,0,1:T(8,128)(2,1)S(1)}, u32[]{:S(2)}) %copy-start) | copy-done | bytes 5251096
  171.1 0.1 slice_reduce_fusion
  171.2 0.5 collective-permute-start.2
  171.6 0.0 copy-done.1
  171.6 0.6 select_reduce_fusion.slots_ref
  172.3 0.2 collective-permute-done.2
  172.5 0.1 add_rsqrt_fusion
  172.5 0.1 broadcast_in_dim.33
  172.6 0.7 reshape_reshape.10.scale_ref
  173.3 0.1 broadcast_in_dim.32
  173.4 0.6 reshape_reshape.9.mean_ref
  174.0 6.8 %shard_map.79 = bf16[9,160,512]{2,1,0:T(8,128)(2,1)} custom-call(s32[17]{0:T(128)} %select_reduce_fusion.slots_ref, bf16[32,641,128]{2,1,0:T(8,128)(2,1)} %bitcast.15, bf16[3,512,512]{2,1,0:T(8,128)(2,1)} %w_ref.3, f32[1,512]{1,0:T(1,128)} %reshape_reshape.9.mean_ref, f32[1,512]{1,0:T(1,128)} %reshape_reshape.10.scale_ref, f32[1,512]{1,0:T(1,128)} %bitcast.19, ...), custom_call_target="tpu_custom_call" | custom-call | tf_op jit(solution)/shard_map/pallas_call | solution.py:127
  (4 shorter events, 0.0 us)
Async XLA Ops:
  0.9 8.3 %collective-permute-start = (bf16[1,1,160,256]{3,2,1,0:T(8,128)(2,1)S(1)}, bf16[1,1,160,256]{3,2,1,0:T(8,128)(2,1)S(1)}, u32[]{:S(2)}, u32[]{:S(2)}) collective-permute-start(bf16[1,1,160,256]{3,2,1,0:T(8,128)(2,1)S(1)} %get-tuple-element.45), channel_id=1, source_target_pairs={{0,1},{2,3},{4,5},{6,7},{8,9},{10,11},{12,13},{14,15},{16,17},{18,... | collective-permute-start | bytes 245768 | tf_op jit(solution)/shard_map/ppermute | solution.py:19
  2.2 7.0 %collective-permute-start.1 = (bf16[1,1,160,256]{3,2,1,0:T(8,128)(2,1)S(1)}, bf16[1,1,160,256]{3,2,1,0:T(8,128)(2,1)S(1)}, u32[]{:S(2)}, u32[]{:S(2)}) collective-permute-start(bf16[1,1,160,256]{3,2,1,0:T(8,128)(2,1)S(1)} %get-tuple-element.46), channel_id=1, source_target_pairs={{1,0},{3,2},{5,4},{7,6},{9,8},{11,10},{13,12},{15,14},{17,16},{19,... | collective-permute-start | bytes 245768 | tf_op jit(solution)/shard_map/ppermute | solution.py:22
  36.2 135.4 %copy-start.1 = (s32[32]{0:T(128)S(1)}, s32[32]{0:T(128)}, u32[]{:S(2)}) copy-start(s32[32]{0:T(128)} %param.14) | copy-start | bytes 388
  168.7 2.3 %copy-start = (bf16[1,32,641,128]{3,2,0,1:T(8,128)(2,1)}, bf16[1,32,641,128]{3,2,0,1:T(8,128)(2,1)S(1)}, u32[]{:S(2)}) copy-start(bf16[1,32,641,128]{3,2,0,1:T(8,128)(2,1)S(1)} %all_to_all.12) | copy-start | bytes 15753220
  171.2 1.3 collective-permute-start.2

commit v9 on v8

--- a/solution.py
+++ b/solution.py
@@ -31,8 +31,18 @@
     return jnp.sum(jnp.where(matches, places, 0), axis=1)
 
 
-def conv_kernel(x_ref, w_ref, out_ref, sum_ref, sq_ref, *, chunk, cols):
+def conv_kernel(low_ref, high_ref, block_ref, w_ref, out_ref, sum_ref, sq_ref, x_ref, sem, *, chunk, cols):
     step = pl.program_id(0)
+    rows = block_ref.shape[0]
+
+    @pl.when(step == 0)
+    def _():
+        fetch = pltpu.make_async_copy(block_ref, x_ref.at[pl.ds(1, rows)], sem)
+        fetch.start()
+        x_ref[0:1] = low_ref[...]
+        x_ref[rows + 1 : rows + 2] = high_ref[...]
+        fetch.wait()
+
     base = step * chunk
     m = chunk * cols
     parts = []
@@ -64,17 +74,18 @@
     sum_ref[...] += jnp.sum(values, axis=0, keepdims=True)
     sq_ref[...] += jnp.sum(values * values, axis=0, keepdims=True)
 
-def conv_call(x, w, chunk=8, lanes=128):
-    rows = x.shape[0] - 2
-    cols = x.shape[1]
-    cin = x.shape[2]
+def conv_call(low, high, block, w, chunk=8, lanes=128):
+    rows, cols, cin = block.shape
     cout = w.shape[-1]
     stacked = cols * (cout // lanes) + 1
+    halo = pl.BlockSpec((1, cols, cin), lambda i: (0, 0, 0))
     return pl.pallas_call(
         functools.partial(conv_kernel, chunk=chunk, cols=cols),
         grid=(rows // chunk,),
         in_specs=[
-            pl.BlockSpec((rows + 2, cols, cin), lambda i: (0, 0, 0)),
+            halo,
+            halo,
+            pl.BlockSpec(memory_space=pl.ANY),
             pl.BlockSpec((3, 3, cin, cout), lambda i: (0, 0, 0, 0)),
         ],
         out_specs=[
@@ -87,9 +98,9 @@
             jax.ShapeDtypeStruct((1, cout), jnp.float32),
             jax.ShapeDtypeStruct((1, cout), jnp.float32),
         ],
+        scratch_shapes=[pltpu.VMEM((rows + 2, cols, cin), block.dtype), pltpu.SemaphoreType.DMA(())],
         compiler_params=pltpu.CompilerParams(dimension_semantics=("arbitrary",)),
-    )(x, w)
-
+    )(low, high, block, w)
 
 def latent_kernel(slots_ref, x_ref, w_ref, mean_ref, scale_ref, gain_ref, shift_ref, bias_ref, out_ref, tap0_ref, tap1_ref, tap2_ref):
     live = 2 * out_ref.shape[0] - 1
@@ -201,9 +212,13 @@
     live_frames = tm_count // 2 + 1
     out_frames = (live_frames - 1) // 2 + 1
     frame_slots = slot_lookup(frame_of_slot, live_frames)
-    padded = with_halo(clip_frames, (("height", 1),), 1)
-    staged, chan_sums, chan_squares = conv_call(padded[0], w_spatial)
-    cols = padded.shape[2]
+    count = lax.axis_size("height")
+    forward = [(i, i + 1) for i in range(count - 1)]
+    backward = [(target, source) for source, target in forward]
+    low = lax.ppermute(clip_frames[0, -1:], "height", forward)
+    high = lax.ppermute(clip_frames[0, :1], "height", backward)
+    staged, chan_sums, chan_squares = conv_call(low, high, clip_frames[0], w_spatial)
+    cols = clip_frames.shape[2]
     tail = staged.shape[1] - 1
     own_frame = lax.dynamic_index_in_dim(frame_of_slot, lax.axis_index("tm"), 0, keepdims=False)
     weight = jnp.where(own_frame >= 0, 1.0, 0.0).astype(jnp.float32)

time: 181 us -> 179 us (0.989)
  other arithmetic: 7.51 us -> 3.99 us
    squeeze x1 -> x0, other arithmetic: 3.62 us -> none  [shards(): staged, chan_sums, chan_squares = conv_call(padded[0], w_spatial)]
where the time goes in v9:
time: 179 us
  blocking collectives  133 us (74%)
  Pallas kernels  26.7 us (15%)
  local copies, waits for them, and re-layouts  7.89 us (4%)
  starting transfers between devices  6.89 us (4%)
  other arithmetic  3.99 us (2%)
    all_to_all x1, blocking collectives, shards(): lax.all_to_all(payload[None], 'tm', split_axis=1, concat_axis=0, tiled=True)  133 us
    pallas_call x1, Pallas kernels, conv_call(): pl.pallas_call(functools.partial(conv_kernel, chunk=chunk, cols=cols), gr...  20 us
    pallas_call x1, Pallas kernels, latent_call(): pl.pallas_call(latent_kernel, in_specs=[pl.BlockSpec(memory_space=smem)]...  6.79 us
    ppermute x1, starting transfers between devices, shards(): high = lax.ppermute(clip_frames[0, :1], 'height', backward)  5.11 us
  transfers between devices with their start and end apart: 3, of which 1 were waited for; matrix products, arithmetic and copies ran while one was open for 1% of the time, Pallas kernels for 0%

profile of v9, /device:TPU:1, one launch (start us, length us, event | category | flops | bytes accessed | tf_op | source)
XLA Modules:
  0.0 179.0 jit_solution(17983706934751177820)
XLA Ops:
  0.0 0.9 slice_bitcast_fusion
  0.9 1.3 collective-permute-start
  2.2 5.1 %collective-permute-start.1 = (bf16[1,160,256]{2,1,0:T(8,128)(2,1)S(1)}, bf16[1,160,256]{2,1,0:T(8,128)(2,1)S(1)}, u32[]{:S(2)}, u32[]{:S(2)}) collective-permute-start(bf16[1,160,256]{2,1,0:T(8,128)(2,1)S(1)} %get-tuple-element.45), channel_id=1, source_target_pairs={{1,0},{3,2},{5,4},{7,6},{9,8},{11,10},{13,12},{15,14},{17,16},{19,... | collective-permute-start | bytes 245768 | tf_op jit(solution)/shard_map/ppermute | solution.py:219
  7.4 1.2 dynamic_slice.4
  9.3 0.0 collective-permute-done.low_ref
  9.3 0.0 copy-start.1
  9.3 0.0 collective-permute-done.1.high_ref
  9.3 0.0 copy-start.2
  9.3 0.6 copy-done.1
  9.9 0.0 copy-done.2
  9.9 20.0 %shard_map.78 = (bf16[32,641,128]{2,1,0:T(8,128)(2,1)}, f32[1,512]{1,0:T(1,128)}, f32[1,512]{1,0:T(1,128)}) custom-call(bf16[1,160,256]{2,1,0:T(8,128)(2,1)} %copy-done.1, bf16[1,160,256]{2,1,0:T(8,128)(2,1)} %copy-done.2, bf16[32,160,256]{2,1,0:T(8,128)(2,1)} %bitcast.21, bf16[3,3,256,512]{3,2,1,0:T(8,128)(2,1)} %w_ref.2), custom_call_target="tpu_custom_call" | custom-call | tf_op jit(solution)/shard_map/pallas_call | solution.py:82
  29.9 0.5 broadcast.52
  30.4 1.3 reduce.11
  31.8 0.1 reshape.84
  31.8 1.3 reduce.10
  33.2 0.1 reshape.85
  33.3 0.1 reduce_sum.46
  33.4 0.1 reduce_sum.47
  33.5 0.1 fusion
  33.6 0.1 subtract_convert_fusion
  33.7 0.1 pad_maximum_fusion.1
  33.8 0.6 broadcast_dynamic-update-slice_fusion
  34.4 0.0 copy-start.3
  34.4 132.6 %all_to_all.12 = bf16[1,32,641,128]{3,2,0,1:T(8,128)(2,1)S(1)} all-to-all(bf16[1,32,641,128]{3,2,0,1:T(8,128)(2,1)} %bitcast.20), channel_id=1, replica_groups=mesh['dp'=4,'tm'=32,'height'=2] {'tm'}, dimensions={1} | all-to-all | bytes 10502144 | tf_op jit(solution)/shard_map/all_to_all | solution.py:231
  167.0 0.0 copy-start
  167.0 2.3 %copy-done = bf16[1,32,641,128]{3,2,0,1:T(8,128)(2,1)} copy-done((bf16[1,32,641,128]{3,2,0,1:T(8,128)(2,1)}, bf16[1,32,641,128]{3,2,0,1:T(8,128)(2,1)S(1)}, u32[]{:S(2)}) %copy-start) | copy-done | bytes 5251096
  169.3 0.1 slice_reduce_fusion
  169.4 0.5 collective-permute-start.2
  169.9 0.0 copy-done.3
  169.9 0.6 select_reduce_fusion.slots_ref
  170.5 0.2 collective-permute-done.2
  170.7 0.1 add_rsqrt_fusion
  170.8 0.1 broadcast_in_dim.33
  170.8 0.7 reshape_reshape.10.scale_ref
  171.5 0.1 broadcast_in_dim.32
  171.6 0.6 reshape_reshape.9.mean_ref
  172.2 6.8 %shard_map.79 = bf16[9,160,512]{2,1,0:T(8,128)(2,1)} custom-call(s32[17]{0:T(128)} %select_reduce_fusion.slots_ref, bf16[32,641,128]{2,1,0:T(8,128)(2,1)} %bitcast.18, bf16[3,512,512]{2,1,0:T(8,128)(2,1)} %w_ref.3, f32[1,512]{1,0:T(1,128)} %reshape_reshape.9.mean_ref, f32[1,512]{1,0:T(1,128)} %reshape_reshape.10.scale_ref, f32[1,512]{1,0:T(1,128)} %bitcast.23, ...), custom_call_target="tpu_custom_call" | custom-call | tf_op jit(solution)/shard_map/pallas_call | solution.py:138
  (4 shorter events, 0.0 us)
Async XLA Ops:
  0.9 8.3 %collective-permute-start = (bf16[1,160,256]{2,1,0:T(8,128)(2,1)S(1)}, bf16[1,160,256]{2,1,0:T(8,128)(2,1)S(1)}, u32[]{:S(2)}, u32[]{:S(2)}) collective-permute-start(bf16[1,160,256]{2,1,0:T(8,128)(2,1)S(1)} %get-tuple-element.46), channel_id=1, source_target_pairs={{0,1},{2,3},{4,5},{6,7},{8,9},{10,11},{12,13},{14,15},{16,17},{18,... | collective-permute-start | bytes 245768 | tf_op jit(solution)/shard_map/ppermute | solution.py:218
  2.2 7.0 %collective-permute-start.1 = (bf16[1,160,256]{2,1,0:T(8,128)(2,1)S(1)}, bf16[1,160,256]{2,1,0:T(8,128)(2,1)S(1)}, u32[]{:S(2)}, u32[]{:S(2)}) collective-permute-start(bf16[1,160,256]{2,1,0:T(8,128)(2,1)S(1)} %get-tuple-element.45), channel_id=1, source_target_pairs={{1,0},{3,2},{5,4},{7,6},{9,8},{11,10},{13,12},{15,14},{17,16},{19,... | collective-permute-start | bytes 245768 | tf_op jit(solution)/shard_map/ppermute | solution.py:219
  9.3 0.6 copy-start.1
  9.3 0.6 copy-start.2
  34.4 135.5 %copy-start.3 = (s32[32]{0:T(128)S(1)}, s32[32]{0:T(128)}, u32[]{:S(2)}) copy-start(s32[32]{0:T(128)} %param.14) | copy-start | bytes 388
  167.0 2.3 %copy-start = (bf16[1,32,641,128]{3,2,0,1:T(8,128)(2,1)}, bf16[1,32,641,128]{3,2,0,1:T(8,128)(2,1)S(1)}, u32[]{:S(2)}) copy-start(bf16[1,32,641,128]{3,2,0,1:T(8,128)(2,1)S(1)} %all_to_all.12) | copy-start | bytes 15753220
  169.4 1.3 collective-permute-start.2

commit v10 on v9

--- a/solution.py
+++ b/solution.py
@@ -31,7 +31,7 @@
     return jnp.sum(jnp.where(matches, places, 0), axis=1)
 
 
-def conv_kernel(low_ref, high_ref, block_ref, w_ref, out_ref, sum_ref, sq_ref, x_ref, sem, *, chunk, cols):
+def conv_kernel(fos_ref, low_ref, high_ref, block_ref, w_ref, out_ref, sum_ref, sq_ref, code_ref, x_ref, sem, *, chunk, cols, groups):
     step = pl.program_id(0)
     rows = block_ref.shape[0]
 
@@ -74,15 +74,35 @@
     sum_ref[...] += jnp.sum(values, axis=0, keepdims=True)
     sq_ref[...] += jnp.sum(values * values, axis=0, keepdims=True)
 
-def conv_call(low, high, block, w, chunk=8, lanes=128):
+    @pl.when(step == pl.num_programs(0) - 1)
+    def _():
+        chans = sum_ref.shape[-1]
+        width = code_ref.shape[-1]
+        per_group = chans // groups
+        chan = lax.broadcasted_iota(jnp.int32, (chans, width), 0) // per_group
+        lane = lax.broadcasted_iota(jnp.int32, (chans, width), 1)
+        to_sums = jnp.where(chan == lane, 1.0, 0.0)
+        to_squares = jnp.where(chan + groups == lane, 1.0, 0.0)
+        exact = lax.Precision.HIGHEST
+        grouped = jnp.dot(sum_ref[...], to_sums, precision=exact, preferred_element_type=jnp.float32)
+        grouped = grouped + jnp.dot(sq_ref[...], to_squares, precision=exact, preferred_element_type=jnp.float32)
+        own = fos_ref[lax.axis_index("tm")]
+        grouped = grouped * jnp.where(own >= 0, 1.0, 0.0)
+        high = grouped.astype(jnp.bfloat16).astype(jnp.float32)
+        low = pltpu.roll(grouped - high, 2 * groups, 1)
+        out_lane = lax.broadcasted_iota(jnp.int32, (1, width), 1)
+        code_ref[...] = jnp.where(out_lane < 2 * groups, high, low).astype(jnp.bfloat16)
+
+def conv_call(frame_of_slot, low, high, block, w, chunk=8, lanes=128):
     rows, cols, cin = block.shape
     cout = w.shape[-1]
     stacked = cols * (cout // lanes) + 1
     halo = pl.BlockSpec((1, cols, cin), lambda i: (0, 0, 0))
     return pl.pallas_call(
-        functools.partial(conv_kernel, chunk=chunk, cols=cols),
+        functools.partial(conv_kernel, chunk=chunk, cols=cols, groups=GROUPS),
         grid=(rows // chunk,),
         in_specs=[
+            pl.BlockSpec(memory_space=pltpu.SMEM),
             halo,
             halo,
             pl.BlockSpec(memory_space=pl.ANY),
@@ -92,15 +112,17 @@
             pl.BlockSpec((chunk, stacked, lanes), lambda i: (i, 0, 0)),
             pl.BlockSpec((1, cout), lambda i: (0, 0)),
             pl.BlockSpec((1, cout), lambda i: (0, 0)),
+            pl.BlockSpec((1, lanes), lambda i: (0, 0)),
         ],
         out_shape=[
             jax.ShapeDtypeStruct((rows, stacked, lanes), jnp.bfloat16),
             jax.ShapeDtypeStruct((1, cout), jnp.float32),
             jax.ShapeDtypeStruct((1, cout), jnp.float32),
+            jax.ShapeDtypeStruct((1, lanes), jnp.bfloat16),
         ],
         scratch_shapes=[pltpu.VMEM((rows + 2, cols, cin), block.dtype), pltpu.SemaphoreType.DMA(())],
         compiler_params=pltpu.CompilerParams(dimension_semantics=("arbitrary",)),
-    )(low, high, block, w)
+    )(frame_of_slot, low, high, block, w)
 
 def latent_kernel(slots_ref, x_ref, w_ref, mean_ref, scale_ref, gain_ref, shift_ref, bias_ref, out_ref, tap0_ref, tap1_ref, tap2_ref):
     live = 2 * out_ref.shape[0] - 1
@@ -217,19 +239,14 @@
     backward = [(target, source) for source, target in forward]
     low = lax.ppermute(clip_frames[0, -1:], "height", forward)
     high = lax.ppermute(clip_frames[0, :1], "height", backward)
-    staged, chan_sums, chan_squares = conv_call(low, high, clip_frames[0], w_spatial)
+    staged, _, _, coded = conv_call(frame_of_slot, low, high, clip_frames[0], w_spatial)
     cols = clip_frames.shape[2]
     tail = staged.shape[1] - 1
-    own_frame = lax.dynamic_index_in_dim(frame_of_slot, lax.axis_index("tm"), 0, keepdims=False)
-    weight = jnp.where(own_frame >= 0, 1.0, 0.0).astype(jnp.float32)
     per_group = w_spatial.shape[-1] // GROUPS
-    sums = chan_sums.reshape(GROUPS, per_group).sum(axis=1) * weight
-    squares = chan_squares.reshape(GROUPS, per_group).sum(axis=1) * weight
-    coded = encode_stats(jnp.concatenate([sums, squares]))
-    column = jnp.zeros((staged.shape[-1],), jnp.bfloat16).at[: coded.shape[0]].set(coded)
+    column = coded[0]
     payload = staged.at[:, tail, :].set(jnp.broadcast_to(column, (staged.shape[0], column.shape[0])))
     received = lax.all_to_all(payload[None], "tm", split_axis=1, concat_axis=0, tiled=True)
-    partial = decode_stats(received[:, 0, tail, : coded.shape[0]], 2 * GROUPS)
+    partial = decode_stats(received[:, 0, tail, :], 2 * GROUPS)
     other = lax.ppermute(partial, "height", [(0, 1), (1, 0)])
     totals = partial + other
     sums, squares = totals[:GROUPS], totals[GROUPS:]

time: 179 us -> 176 us (0.983)
  other arithmetic: 3.99 us -> 0.9 us
  blocking collectives: 133 us -> 131 us
    pallas_call x2 -> x0, other arithmetic: 2.7 us -> none  [conv_call(): pl.pallas_call(functools.partial(conv_kernel, chunk=chunk, cols=cols), gr...]
    all_to_all x1, blocking collectives: 133 us -> 131 us  [shards(): lax.all_to_all(payload[None], 'tm', split_axis=1, concat_axis=0, tiled=True)]
  transfers between devices with their start and end apart: 3 -> 3, of which waited for: 1 -> 2; matrix products, arithmetic and copies ran while one was open for 1% -> 0% of each run, Pallas kernels for 0% -> 0%
where the time goes in v10:
time: 176 us; the launch traced here: 175 us
  blocking collectives  131 us (74%)
  Pallas kernels  27.6 us (16%)
  starting transfers between devices  8.57 us (5%)
  local copies, waits for them, and re-layouts  6.65 us (4%)
    all_to_all x1, blocking collectives, shards(): lax.all_to_all(payload[None], 'tm', split_axis=1, concat_axis=0, tiled=True)  131 us
    pallas_call x1, Pallas kernels, conv_call(): pl.pallas_call(functools.partial(conv_kernel, chunk=chunk, cols=cols, gro...  20.8 us
    pallas_call x1, Pallas kernels, latent_call(): pl.pallas_call(latent_kernel, in_specs=[pl.BlockSpec(memory_space=smem)]...  6.77 us
    ppermute x1, starting transfers between devices, shards(): high = lax.ppermute(clip_frames[0, :1], 'height', backward)  5.11 us
  transfers between devices with their start and end apart: 3, of which 2 were waited for; matrix products, arithmetic and copies ran while one was open for 0% of the time, Pallas kernels for 0%

profile of v10, /device:TPU:1, one launch (start us, length us, event | category | flops | bytes accessed | tf_op | source)
XLA Modules:
  0.0 175.3 jit_solution(3245705841877841674)
XLA Ops:
  0.0 0.9 slice_bitcast_fusion
  0.9 1.3 collective-permute-start
  2.2 5.1 %collective-permute-start.1 = (bf16[1,160,256]{2,1,0:T(8,128)(2,1)S(1)}, bf16[1,160,256]{2,1,0:T(8,128)(2,1)S(1)}, u32[]{:S(2)}, u32[]{:S(2)}) collective-permute-start(bf16[1,160,256]{2,1,0:T(8,128)(2,1)S(1)} %get-tuple-element.23), channel_id=1, source_target_pairs={{1,0},{3,2},{5,4},{7,6},{9,8},{11,10},{13,12},{15,14},{17,16},{19,... | collective-permute-start | bytes 245768 | tf_op jit(solution)/shard_map/ppermute | solution.py:241
  7.4 0.0 collective-permute-done.low_ref
  7.4 0.0 copy-start.1
  7.4 0.9 collective-permute-done.1.high_ref
  8.3 0.0 copy-start.2
  8.3 0.0 copy-done.1
  8.3 0.6 copy-done.2
  8.9 20.8 %shard_map.73 = (bf16[32,641,128]{2,1,0:T(8,128)(2,1)}, f32[1,512]{1,0:T(1,128)}, f32[1,512]{1,0:T(1,128)}, bf16[1,128]{1,0:T(2,128)(2,1)}) custom-call(s32[32]{0:T(128)} %fos_ref.1, bf16[1,160,256]{2,1,0:T(8,128)(2,1)} %copy-done.1, bf16[1,160,256]{2,1,0:T(8,128)(2,1)} %copy-done.2, bf16[32,160,256]{2,1,0:T(8,128)(2,1)} %bitcast.21, ...), custom_call_target="tpu_custom_call" | custom-call | tf_op jit(solution)/shard_map/pallas_call | solution.py:101
  29.7 1.3 broadcast_dynamic-update-slice_fusion
  30.9 0.0 copy-start.3
  30.9 130.6 %all_to_all.12 = bf16[1,32,641,128]{3,2,0,1:T(8,128)(2,1)S(1)} all-to-all(bf16[1,32,641,128]{3,2,0,1:T(8,128)(2,1)} %bitcast.20), channel_id=1, replica_groups=mesh['dp'=4,'tm'=32,'height'=2] {'tm'}, dimensions={1} | all-to-all | bytes 10502144 | tf_op jit(solution)/shard_map/all_to_all | solution.py:248
  161.5 0.0 copy-start
  161.5 2.3 %copy-done = bf16[1,32,641,128]{3,2,0,1:T(8,128)(2,1)} copy-done((bf16[1,32,641,128]{3,2,0,1:T(8,128)(2,1)}, bf16[1,32,641,128]{3,2,0,1:T(8,128)(2,1)S(1)}, u32[]{:S(2)}) %copy-start) | copy-done | bytes 5251096
  163.9 0.1 slice_reduce_fusion
  164.0 2.2 %collective-permute-start.2 = (f32[64]{0:T(128)S(1)}, f32[64]{0:T(128)S(1)}, u32[]{:S(2)}, u32[]{:S(2)}) collective-permute-start(f32[64]{0:T(128)S(1)} %add.14), channel_id=1, source_target_pairs={{0,1},{1,0},{2,3},{3,2},{4,5},{5,4},{6,7},{7,6},{8,9},{9,8},{10,11... | collective-permute-start | bytes 776 | tf_op jit(solution)/shard_map/ppermute | solution.py:250
  166.1 0.0 copy-done.3
  166.1 0.7 select_reduce_fusion.slots_ref
  166.8 0.1 collective-permute-done.2
  166.9 0.1 add_rsqrt_fusion
  167.0 0.1 broadcast_in_dim.32
  167.1 0.7 reshape_reshape.10.scale_ref
  167.8 0.1 broadcast_in_dim.31
  167.8 0.7 reshape_reshape.9.mean_ref
  168.5 6.8 %shard_map.74 = bf16[9,160,512]{2,1,0:T(8,128)(2,1)} custom-call(s32[17]{0:T(128)} %select_reduce_fusion.slots_ref, bf16[32,641,128]{2,1,0:T(8,128)(2,1)} %bitcast.18, bf16[3,512,512]{2,1,0:T(8,128)(2,1)} %w_ref.3, f32[1,512]{1,0:T(1,128)} %reshape_reshape.9.mean_ref, f32[1,512]{1,0:T(1,128)} %reshape_reshape.10.scale_ref, f32[1,512]{1,0:T(1,128)} %bitcast.23, ...), custom_call_target="tpu_custom_call" | custom-call | tf_op jit(solution)/shard_map/pallas_call | solution.py:160
  (3 shorter events, 0.0 us)
Async XLA Ops:
  0.9 6.4 %collective-permute-start = (bf16[1,160,256]{2,1,0:T(8,128)(2,1)S(1)}, bf16[1,160,256]{2,1,0:T(8,128)(2,1)S(1)}, u32[]{:S(2)}, u32[]{:S(2)}) collective-permute-start(bf16[1,160,256]{2,1,0:T(8,128)(2,1)S(1)} %get-tuple-element.24), channel_id=1, source_target_pairs={{0,1},{2,3},{4,5},{6,7},{8,9},{10,11},{12,13},{14,15},{16,17},{18,... | collective-permute-start | bytes 245768 | tf_op jit(solution)/shard_map/ppermute | solution.py:240
  2.2 6.0 %collective-permute-start.1 = (bf16[1,160,256]{2,1,0:T(8,128)(2,1)S(1)}, bf16[1,160,256]{2,1,0:T(8,128)(2,1)S(1)}, u32[]{:S(2)}, u32[]{:S(2)}) collective-permute-start(bf16[1,160,256]{2,1,0:T(8,128)(2,1)S(1)} %get-tuple-element.23), channel_id=1, source_target_pairs={{1,0},{3,2},{5,4},{7,6},{9,8},{11,10},{13,12},{15,14},{17,16},{19,... | collective-permute-start | bytes 245768 | tf_op jit(solution)/shard_map/ppermute | solution.py:241
  7.4 0.9 copy-start.1
  8.3 0.6 copy-start.2
  30.9 135.2 %copy-start.3 = (s32[32]{0:T(128)S(1)}, s32[32]{0:T(128)}, u32[]{:S(2)}) copy-start(s32[32]{0:T(128)} %fos_ref.1) | copy-start | bytes 388
  161.5 2.3 %copy-start = (bf16[1,32,641,128]{3,2,0,1:T(8,128)(2,1)}, bf16[1,32,641,128]{3,2,0,1:T(8,128)(2,1)S(1)}, u32[]{:S(2)}) copy-start(bf16[1,32,641,128]{3,2,0,1:T(8,128)(2,1)S(1)} %all_to_all.12) | copy-start | bytes 15753220
  164.0 3.0 %collective-permute-start.2 = (f32[64]{0:T(128)S(1)}, f32[64]{0:T(128)S(1)}, u32[]{:S(2)}, u32[]{:S(2)}) collective-permute-start(f32[64]{0:T(128)S(1)} %add.14), channel_id=1, source_target_pairs={{0,1},{1,0},{2,3},{3,2},{4,5},{5,4},{6,7},{7,6},{8,9},{9,8},{10,11... | collective-permute-start | bytes 776 | tf_op jit(solution)/shard_map/ppermute | solution.py:250

commit v11 on v10

--- a/solution.py
+++ b/solution.py
@@ -124,15 +124,28 @@
         compiler_params=pltpu.CompilerParams(dimension_semantics=("arbitrary",)),
     )(frame_of_slot, low, high, block, w)
 
-def latent_kernel(slots_ref, x_ref, w_ref, mean_ref, scale_ref, gain_ref, shift_ref, bias_ref, out_ref, tap0_ref, tap1_ref, tap2_ref):
+def latent_kernel(slots_ref, x_ref, w_ref, totals_ref, gain_ref, shift_ref, bias_ref, out_ref, tap0_ref, tap1_ref, tap2_ref, *, cell_count, groups):
     live = 2 * out_ref.shape[0] - 1
     cols, chans = out_ref.shape[1], out_ref.shape[2]
+    width = totals_ref.shape[-1]
+    totals = totals_ref[...]
+    lane = lax.broadcasted_iota(jnp.int32, (1, width), 1)
+    group_mean = totals / cell_count
+    group_var = pltpu.roll(totals, width - groups, 1) / cell_count - group_mean * group_mean
+    inv_scale = lax.rsqrt(group_var + 1e-06)
+    group_mean = jnp.where(lane < groups, group_mean, 0.0)
+    inv_scale = jnp.where(lane < groups, inv_scale, 0.0)
+    owner = lax.broadcasted_iota(jnp.int32, (width, chans), 1) // (chans // groups)
+    expand = jnp.where(owner == lax.broadcasted_iota(jnp.int32, (width, chans), 0), 1.0, 0.0)
+    exact = lax.Precision.HIGHEST
+    mean_chan = jnp.dot(group_mean, expand, precision=exact, preferred_element_type=jnp.float32)
+    scale_chan = jnp.dot(inv_scale, expand, precision=exact, preferred_element_type=jnp.float32)
     for frame in range(live):
         slot = slots_ref[frame]
         lanes = x_ref.shape[-1]
         pieces = [x_ref[slot, pl.ds(q * cols, cols), :] for q in range(chans // lanes)]
         values = jnp.concatenate(pieces, axis=-1).astype(jnp.float32)
-        normed = (values - mean_ref[...]) * scale_ref[...] * gain_ref[...] + shift_ref[...]
+        normed = (values - mean_chan) * scale_chan * gain_ref[...] + shift_ref[...]
         activated = jax.nn.silu(normed).astype(jnp.bfloat16)
         if frame == 0:
             tap0_ref[0] = activated
@@ -151,21 +164,21 @@
     out_ref[...] = running.astype(jnp.bfloat16).reshape(out_ref.shape)
 
 
-def latent_call(frame_slots, received, w_time, mean_chan, scale_chan, norm_gain, norm_shift, time_bias, out_frames, cols):
+def latent_call(frame_slots, received, w_time, totals, cell_count, norm_gain, norm_shift, time_bias, out_frames, cols):
     chans = w_time.shape[-1]
     vmem = pltpu.MemorySpace.VMEM if hasattr(pltpu, "MemorySpace") else pltpu.TPUMemorySpace.VMEM
     smem = pltpu.MemorySpace.SMEM if hasattr(pltpu, "MemorySpace") else pltpu.TPUMemorySpace.SMEM
     row = lambda v: v.reshape(1, chans).astype(jnp.float32)
     tap = pltpu.VMEM((out_frames, cols, chans), jnp.bfloat16)
     return pl.pallas_call(
-        latent_kernel,
-        in_specs=[pl.BlockSpec(memory_space=smem)] + [pl.BlockSpec(memory_space=vmem)] * 7,
+        functools.partial(latent_kernel, cell_count=cell_count, groups=GROUPS),
+        in_specs=[pl.BlockSpec(memory_space=smem)] + [pl.BlockSpec(memory_space=vmem)] * 6,
         out_specs=pl.BlockSpec(memory_space=vmem),
         out_shape=jax.ShapeDtypeStruct((out_frames, cols, chans), jnp.bfloat16),
         scratch_shapes=[tap, tap, tap],
     )(
         frame_slots, received, w_time,
-        row(mean_chan), row(scale_chan), row(norm_gain), row(norm_shift), row(time_bias),
+        totals, row(norm_gain), row(norm_shift), row(time_bias),
     )
 
 def spatial_conv(row_padded, w_spatial):
@@ -245,21 +258,19 @@
     per_group = w_spatial.shape[-1] // GROUPS
     column = coded[0]
     payload = staged.at[:, tail, :].set(jnp.broadcast_to(column, (staged.shape[0], column.shape[0])))
+    payload, frame_slots = lax.optimization_barrier((payload, frame_slots))
     received = lax.all_to_all(payload[None], "tm", split_axis=1, concat_axis=0, tiled=True)
     partial = decode_stats(received[:, 0, tail, :], 2 * GROUPS)
     other = lax.ppermute(partial, "height", [(0, 1), (1, 0)])
     totals = partial + other
-    sums, squares = totals[:GROUPS], totals[GROUPS:]
     cell_count = float(live_frames * clip_frames.shape[1] * height_count * cols * per_group)
-    group_mean = sums / cell_count
-    group_var = squares / cell_count - group_mean * group_mean
-    inv_scale = lax.rsqrt(group_var + 1e-06)
+    padded_totals = jnp.zeros((1, 128), jnp.float32).at[0, : totals.shape[0]].set(totals)
     latent = latent_call(
         frame_slots.astype(jnp.int32),
         received.reshape(received.shape[0], tail + 1, -1),
         w_time,
-        jnp.repeat(group_mean, per_group),
-        jnp.repeat(inv_scale, per_group),
+        padded_totals,
+        cell_count,
         norm_gain,
         norm_shift,
         time_bias,

time: 176 us -> 176 us (level)
  other arithmetic: 0.9 us -> 2.74 us
  transfers between devices with their start and end apart: 3 -> 3, of which waited for: 2 -> 1; matrix products, arithmetic and copies ran while one was open for 0% -> 1% of each run, Pallas kernels for 0% -> 0%
where the time goes in v11:
time: 176 us
  blocking collectives  131 us (74%)
  Pallas kernels  27.8 us (16%)
  starting transfers between devices  7.57 us (4%)
  local copies, waits for them, and re-layouts  5.74 us (3%)
  other arithmetic  2.74 us (2%)
    all_to_all x1, blocking collectives, shards(): lax.all_to_all(payload[None], 'tm', split_axis=1, concat_axis=0, tiled=True)  131 us
    pallas_call x1, Pallas kernels, conv_call(): pl.pallas_call(functools.partial(conv_kernel, chunk=chunk, cols=cols, gro...  20.8 us
    pallas_call x1, Pallas kernels, latent_call(): pl.pallas_call(functools.partial(latent_kernel, cell_count=cell_count, gr...  7 us
    ppermute x1, starting transfers between devices, shards(): high = lax.ppermute(clip_frames[0, :1], 'height', backward)  5.11 us
  transfers between devices with their start and end apart: 3, of which 1 were waited for; matrix products, arithmetic and copies ran while one was open for 1% of the time, Pallas kernels for 0%

profile of v11, /device:TPU:1, one launch (start us, length us, event | category | flops | bytes accessed | tf_op | source)
XLA Modules:
  0.0 175.5 jit_solution(1425594595954309149)
XLA Ops:
  0.0 0.9 slice_bitcast_fusion
  0.9 1.3 collective-permute-start
  2.2 5.1 %collective-permute-start.1 = (bf16[1,160,256]{2,1,0:T(8,128)(2,1)S(1)}, bf16[1,160,256]{2,1,0:T(8,128)(2,1)S(1)}, u32[]{:S(2)}, u32[]{:S(2)}) collective-permute-start(bf16[1,160,256]{2,1,0:T(8,128)(2,1)S(1)} %get-tuple-element.39), channel_id=1, source_target_pairs={{1,0},{3,2},{5,4},{7,6},{9,8},{11,10},{13,12},{15,14},{17,16},{19,... | collective-permute-start | bytes 245768 | tf_op jit(solution)/shard_map/ppermute | solution.py:254
  7.4 1.3 select_reduce_fusion.slots_ref
  8.7 0.0 collective-permute-done.low_ref
  8.7 0.0 copy-start.1
  8.7 0.0 collective-permute-done.1.high_ref
  8.7 0.0 copy-start.2
  8.7 0.6 copy-done.1
  9.3 0.0 copy-done.2
  9.4 20.8 %shard_map.73 = (bf16[32,641,128]{2,1,0:T(8,128)(2,1)}, f32[1,512]{1,0:T(1,128)}, f32[1,512]{1,0:T(1,128)}, bf16[1,128]{1,0:T(2,128)(2,1)}) custom-call(s32[32]{0:T(128)} %fos_ref.1, bf16[1,160,256]{2,1,0:T(8,128)(2,1)} %copy-done.1, bf16[1,160,256]{2,1,0:T(8,128)(2,1)} %copy-done.2, bf16[32,160,256]{2,1,0:T(8,128)(2,1)} %bitcast.23, ...), custom_call_target="tpu_custom_call" | custom-call | tf_op jit(solution)/shard_map/pallas_call | solution.py:101
  30.2 1.3 broadcast_dynamic-update-slice_fusion
  31.5 131.4 %all_to_all.12 = bf16[1,32,641,128]{3,2,0,1:T(8,128)(2,1)S(1)} all-to-all(bf16[1,32,641,128]{3,2,0,1:T(8,128)(2,1)} %bitcast.22), channel_id=1, replica_groups=mesh['dp'=4,'tm'=32,'height'=2] {'tm'}, dimensions={1} | all-to-all | bytes 10502144 | tf_op jit(solution)/shard_map/all_to_all | solution.py:262
  162.9 0.0 copy-start
  162.9 2.3 %copy-done = bf16[1,32,641,128]{3,2,0,1:T(8,128)(2,1)} copy-done((bf16[1,32,641,128]{3,2,0,1:T(8,128)(2,1)}, bf16[1,32,641,128]{3,2,0,1:T(8,128)(2,1)S(1)}, u32[]{:S(2)}) %copy-start) | copy-done | bytes 5251096
  165.2 0.1 slice_reduce_fusion
  165.3 1.2 collective-permute-start.2
  166.5 0.6 compare_reduce_fusion
  167.1 0.2 collective-permute-done.2
  167.3 0.6 fusion
  168.0 0.5 scatter.9.totals_ref
  168.5 7.0 %shard_map.74 = bf16[9,160,512]{2,1,0:T(8,128)(2,1)} custom-call(s32[17]{0:T(128)} %select_reduce_fusion.slots_ref, bf16[32,641,128]{2,1,0:T(8,128)(2,1)} %bitcast.21, bf16[3,512,512]{2,1,0:T(8,128)(2,1)} %w_ref.3, f32[1,128]{1,0:T(1,128)} %scatter.9.totals_ref, f32[1,512]{1,0:T(1,128)} %bitcast.25, f32[1,512]{1,0:T(1,128)} %bitcast.26, f32[1,512]{1,0:T(1,128)} %bitcast.27), custom_call_target="tpu_custom_call" | custom-call | tf_op jit(solution)/shard_map/pallas_call | solution.py:173
  (2 shorter events, 0.0 us)
Async XLA Ops:
  0.9 7.8 %collective-permute-start = (bf16[1,160,256]{2,1,0:T(8,128)(2,1)S(1)}, bf16[1,160,256]{2,1,0:T(8,128)(2,1)S(1)}, u32[]{:S(2)}, u32[]{:S(2)}) collective-permute-start(bf16[1,160,256]{2,1,0:T(8,128)(2,1)S(1)} %get-tuple-element.40), channel_id=1, source_target_pairs={{0,1},{2,3},{4,5},{6,7},{8,9},{10,11},{12,13},{14,15},{16,17},{18,... | collective-permute-start | bytes 245768 | tf_op jit(solution)/shard_map/ppermute | solution.py:253
  2.2 6.5 %collective-permute-start.1 = (bf16[1,160,256]{2,1,0:T(8,128)(2,1)S(1)}, bf16[1,160,256]{2,1,0:T(8,128)(2,1)S(1)}, u32[]{:S(2)}, u32[]{:S(2)}) collective-permute-start(bf16[1,160,256]{2,1,0:T(8,128)(2,1)S(1)} %get-tuple-element.39), channel_id=1, source_target_pairs={{1,0},{3,2},{5,4},{7,6},{9,8},{11,10},{13,12},{15,14},{17,16},{19,... | collective-permute-start | bytes 245768 | tf_op jit(solution)/shard_map/ppermute | solution.py:254
  8.7 0.6 copy-start.1
  8.7 0.7 copy-start.2
  162.9 2.3 %copy-start = (bf16[1,32,641,128]{3,2,0,1:T(8,128)(2,1)}, bf16[1,32,641,128]{3,2,0,1:T(8,128)(2,1)S(1)}, u32[]{:S(2)}) copy-start(bf16[1,32,641,128]{3,2,0,1:T(8,128)(2,1)S(1)} %all_to_all.12) | copy-start | bytes 15753220
  165.3 2.0 %collective-permute-start.2 = (f32[64]{0:T(128)S(1)}, f32[64]{0:T(128)S(1)}, u32[]{:S(2)}, u32[]{:S(2)}) collective-permute-start(f32[64]{0:T(128)S(1)} %add.12), channel_id=1, source_target_pairs={{0,1},{1,0},{2,3},{3,2},{4,5},{5,4},{6,7},{7,6},{8,9},{9,8},{10,11... | collective-permute-start | bytes 776 | tf_op jit(solution)/shard_map/ppermute | solution.py:264

commit v12 on v11

--- a/solution.py
+++ b/solution.py
@@ -93,7 +93,7 @@
         out_lane = lax.broadcasted_iota(jnp.int32, (1, width), 1)
         code_ref[...] = jnp.where(out_lane < 2 * groups, high, low).astype(jnp.bfloat16)
 
-def conv_call(frame_of_slot, low, high, block, w, chunk=8, lanes=128):
+def conv_call(frame_of_slot, low, high, block, w, chunk=16, lanes=128):
     rows, cols, cin = block.shape
     cout = w.shape[-1]
     stacked = cols * (cout // lanes) + 1

time: 176 us -> 176 us (level)
  no operation moved by 1% of the time
where the time goes in v12:
time: 176 us
  blocking collectives  131 us (74%)
  Pallas kernels  28.3 us (16%)
  starting transfers between devices  7.59 us (4%)
  local copies, waits for them, and re-layouts  5.74 us (3%)
  other arithmetic  2.74 us (2%)
    all_to_all x1, blocking collectives, shards(): lax.all_to_all(payload[None], 'tm', split_axis=1, concat_axis=0, tiled=True)  131 us
    pallas_call x1, Pallas kernels, conv_call(): pl.pallas_call(functools.partial(conv_kernel, chunk=chunk, cols=cols, gro...  21.3 us
    pallas_call x1, Pallas kernels, latent_call(): pl.pallas_call(functools.partial(latent_kernel, cell_count=cell_count, gr...  7 us
    ppermute x1, starting transfers between devices, shards(): high = lax.ppermute(clip_frames[0, :1], 'height', backward)  5.11 us
  transfers between devices with their start and end apart: 3, of which 1 were waited for; matrix products, arithmetic and copies ran while one was open for 1% of the time, Pallas kernels for 0%

profile of v12, /device:TPU:1, one launch (start us, length us, event | category | flops | bytes accessed | tf_op | source)
XLA Modules:
  0.0 176.0 jit_solution(14774576879368014128)
XLA Ops:
  0.0 0.9 slice_bitcast_fusion
  0.9 1.3 collective-permute-start
  2.2 5.1 %collective-permute-start.1 = (bf16[1,160,256]{2,1,0:T(8,128)(2,1)S(1)}, bf16[1,160,256]{2,1,0:T(8,128)(2,1)S(1)}, u32[]{:S(2)}, u32[]{:S(2)}) collective-permute-start(bf16[1,160,256]{2,1,0:T(8,128)(2,1)S(1)} %get-tuple-element.39), channel_id=1, source_target_pairs={{1,0},{3,2},{5,4},{7,6},{9,8},{11,10},{13,12},{15,14},{17,16},{19,... | collective-permute-start | bytes 245768 | tf_op jit(solution)/shard_map/ppermute | solution.py:254
  7.4 1.3 select_reduce_fusion.slots_ref
  8.7 0.0 collective-permute-done.low_ref
  8.7 0.0 copy-start.1
  8.7 0.0 collective-permute-done.1.high_ref
  8.7 0.0 copy-start.2
  8.7 0.6 copy-done.1
  9.3 0.0 copy-done.2
  9.4 21.3 %shard_map.73 = (bf16[32,641,128]{2,1,0:T(8,128)(2,1)}, f32[1,512]{1,0:T(1,128)}, f32[1,512]{1,0:T(1,128)}, bf16[1,128]{1,0:T(2,128)(2,1)}) custom-call(s32[32]{0:T(128)} %fos_ref.1, bf16[1,160,256]{2,1,0:T(8,128)(2,1)} %copy-done.1, bf16[1,160,256]{2,1,0:T(8,128)(2,1)} %copy-done.2, bf16[32,160,256]{2,1,0:T(8,128)(2,1)} %bitcast.23, ...), custom_call_target="tpu_custom_call" | custom-call | tf_op jit(solution)/shard_map/pallas_call | solution.py:101
  30.7 1.3 broadcast_dynamic-update-slice_fusion
  32.0 131.4 %all_to_all.12 = bf16[1,32,641,128]{3,2,0,1:T(8,128)(2,1)S(1)} all-to-all(bf16[1,32,641,128]{3,2,0,1:T(8,128)(2,1)} %bitcast.22), channel_id=1, replica_groups=mesh['dp'=4,'tm'=32,'height'=2] {'tm'}, dimensions={1} | all-to-all | bytes 10502144 | tf_op jit(solution)/shard_map/all_to_all | solution.py:262
  163.4 0.0 copy-start
  163.4 2.3 %copy-done = bf16[1,32,641,128]{3,2,0,1:T(8,128)(2,1)} copy-done((bf16[1,32,641,128]{3,2,0,1:T(8,128)(2,1)}, bf16[1,32,641,128]{3,2,0,1:T(8,128)(2,1)S(1)}, u32[]{:S(2)}) %copy-start) | copy-done | bytes 5251096
  165.7 0.1 slice_reduce_fusion
  165.8 1.2 collective-permute-start.2
  167.0 0.6 compare_reduce_fusion
  167.6 0.2 collective-permute-done.2
  167.8 0.6 fusion
  168.5 0.5 scatter.9.totals_ref
  169.0 7.0 %shard_map.74 = bf16[9,160,512]{2,1,0:T(8,128)(2,1)} custom-call(s32[17]{0:T(128)} %select_reduce_fusion.slots_ref, bf16[32,641,128]{2,1,0:T(8,128)(2,1)} %bitcast.21, bf16[3,512,512]{2,1,0:T(8,128)(2,1)} %w_ref.3, f32[1,128]{1,0:T(1,128)} %scatter.9.totals_ref, f32[1,512]{1,0:T(1,128)} %bitcast.25, f32[1,512]{1,0:T(1,128)} %bitcast.26, f32[1,512]{1,0:T(1,128)} %bitcast.27), custom_call_target="tpu_custom_call" | custom-call | tf_op jit(solution)/shard_map/pallas_call | solution.py:173
  (2 shorter events, 0.0 us)
Async XLA Ops:
  0.9 7.8 %collective-permute-start = (bf16[1,160,256]{2,1,0:T(8,128)(2,1)S(1)}, bf16[1,160,256]{2,1,0:T(8,128)(2,1)S(1)}, u32[]{:S(2)}, u32[]{:S(2)}) collective-permute-start(bf16[1,160,256]{2,1,0:T(8,128)(2,1)S(1)} %get-tuple-element.40), channel_id=1, source_target_pairs={{0,1},{2,3},{4,5},{6,7},{8,9},{10,11},{12,13},{14,15},{16,17},{18,... | collective-permute-start | bytes 245768 | tf_op jit(solution)/shard_map/ppermute | solution.py:253
  2.2 6.5 %collective-permute-start.1 = (bf16[1,160,256]{2,1,0:T(8,128)(2,1)S(1)}, bf16[1,160,256]{2,1,0:T(8,128)(2,1)S(1)}, u32[]{:S(2)}, u32[]{:S(2)}) collective-permute-start(bf16[1,160,256]{2,1,0:T(8,128)(2,1)S(1)} %get-tuple-element.39), channel_id=1, source_target_pairs={{1,0},{3,2},{5,4},{7,6},{9,8},{11,10},{13,12},{15,14},{17,16},{19,... | collective-permute-start | bytes 245768 | tf_op jit(solution)/shard_map/ppermute | solution.py:254
  8.7 0.6 copy-start.1
  8.7 0.7 copy-start.2
  163.4 2.3 %copy-start = (bf16[1,32,641,128]{3,2,0,1:T(8,128)(2,1)}, bf16[1,32,641,128]{3,2,0,1:T(8,128)(2,1)S(1)}, u32[]{:S(2)}) copy-start(bf16[1,32,641,128]{3,2,0,1:T(8,128)(2,1)S(1)} %all_to_all.12) | copy-start | bytes 15753220
  165.8 2.0 %collective-permute-start.2 = (f32[64]{0:T(128)S(1)}, f32[64]{0:T(128)S(1)}, u32[]{:S(2)}, u32[]{:S(2)}) collective-permute-start(f32[64]{0:T(128)S(1)} %add.12), channel_id=1, source_target_pairs={{0,1},{1,0},{2,3},{3,2},{4,5},{5,4},{6,7},{7,6},{8,9},{9,8},{10,11... | collective-permute-start | bytes 776 | tf_op jit(solution)/shard_map/ppermute | solution.py:264

commit v13 on v11

--- a/solution.py
+++ b/solution.py
@@ -124,9 +124,16 @@
         compiler_params=pltpu.CompilerParams(dimension_semantics=("arbitrary",)),
     )(frame_of_slot, low, high, block, w)
 
-def latent_kernel(slots_ref, x_ref, w_ref, totals_ref, gain_ref, shift_ref, bias_ref, out_ref, tap0_ref, tap1_ref, tap2_ref, *, cell_count, groups):
+def latent_kernel(slots_ref, src_ref, w_ref, totals_ref, gain_ref, shift_ref, bias_ref, out_ref, tap0_ref, tap1_ref, tap2_ref, x_ref, sems, *, cell_count, groups):
     live = 2 * out_ref.shape[0] - 1
     cols, chans = out_ref.shape[1], out_ref.shape[2]
+    span = x_ref.shape[1]
+    fetches = [
+        pltpu.make_async_copy(src_ref.at[slots_ref[frame], pl.ds(0, span)], x_ref.at[frame], sems.at[frame])
+        for frame in range(live)
+    ]
+    for fetch in fetches:
+        fetch.start()
     width = totals_ref.shape[-1]
     totals = totals_ref[...]
     lane = lax.broadcasted_iota(jnp.int32, (1, width), 1)
@@ -141,9 +148,9 @@
     mean_chan = jnp.dot(group_mean, expand, precision=exact, preferred_element_type=jnp.float32)
     scale_chan = jnp.dot(inv_scale, expand, precision=exact, preferred_element_type=jnp.float32)
     for frame in range(live):
-        slot = slots_ref[frame]
+        fetches[frame].wait()
         lanes = x_ref.shape[-1]
-        pieces = [x_ref[slot, pl.ds(q * cols, cols), :] for q in range(chans // lanes)]
+        pieces = [x_ref[frame, pl.ds(q * cols, cols), :] for q in range(chans // lanes)]
         values = jnp.concatenate(pieces, axis=-1).astype(jnp.float32)
         normed = (values - mean_chan) * scale_chan * gain_ref[...] + shift_ref[...]
         activated = jax.nn.silu(normed).astype(jnp.bfloat16)
@@ -172,10 +179,17 @@
     tap = pltpu.VMEM((out_frames, cols, chans), jnp.bfloat16)
     return pl.pallas_call(
         functools.partial(latent_kernel, cell_count=cell_count, groups=GROUPS),
-        in_specs=[pl.BlockSpec(memory_space=smem)] + [pl.BlockSpec(memory_space=vmem)] * 6,
+        in_specs=[pl.BlockSpec(memory_space=smem), pl.BlockSpec(memory_space=pl.ANY)]
+        + [pl.BlockSpec(memory_space=vmem)] * 5,
         out_specs=pl.BlockSpec(memory_space=vmem),
         out_shape=jax.ShapeDtypeStruct((out_frames, cols, chans), jnp.bfloat16),
-        scratch_shapes=[tap, tap, tap],
+        scratch_shapes=[
+            tap,
+            tap,
+            tap,
+            pltpu.VMEM((2 * out_frames - 1, cols * (chans // received.shape[-1]), received.shape[-1]), received.dtype),
+            pltpu.SemaphoreType.DMA((2 * out_frames - 1,)),
+        ],
     )(
         frame_slots, received, w_time,
         totals, row(norm_gain), row(norm_shift), row(time_bias),

time: 176 us -> 177 us (level)
  no operation moved by 1% of the time
where the time goes in v13:
time: 177 us; the launch traced here: 176 us
  blocking collectives  131 us (74%)
  Pallas kernels  28.5 us (16%)
  starting transfers between devices  7.57 us (4%)
  local copies, waits for them, and re-layouts  5.74 us (3%)
  other arithmetic  2.74 us (2%)
    all_to_all x1, blocking collectives, shards(): lax.all_to_all(payload[None], 'tm', split_axis=1, concat_axis=0, tiled=True)  131 us
    pallas_call x1, Pallas kernels, conv_call(): pl.pallas_call(functools.partial(conv_kernel, chunk=chunk, cols=cols, gro...  20.8 us
    pallas_call x1, Pallas kernels, latent_call(): pl.pallas_call(functools.partial(latent_kernel, cell_count=cell_count, gr...  7.68 us
    ppermute x1, starting transfers between devices, shards(): high = lax.ppermute(clip_frames[0, :1], 'height', backward)  5.11 us
  transfers between devices with their start and end apart: 3, of which 1 were waited for; matrix products, arithmetic and copies ran while one was open for 1% of the time, Pallas kernels for 0%

profile of v13, /device:TPU:1, one launch (start us, length us, event | category | flops | bytes accessed | tf_op | source)
XLA Modules:
  0.0 176.2 jit_solution(5061930449001477589)
XLA Ops:
  0.0 0.9 slice_bitcast_fusion
  0.9 1.3 collective-permute-start
  2.2 5.1 %collective-permute-start.1 = (bf16[1,160,256]{2,1,0:T(8,128)(2,1)S(1)}, bf16[1,160,256]{2,1,0:T(8,128)(2,1)S(1)}, u32[]{:S(2)}, u32[]{:S(2)}) collective-permute-start(bf16[1,160,256]{2,1,0:T(8,128)(2,1)S(1)} %get-tuple-element.39), channel_id=1, source_target_pairs={{1,0},{3,2},{5,4},{7,6},{9,8},{11,10},{13,12},{15,14},{17,16},{19,... | collective-permute-start | bytes 245768 | tf_op jit(solution)/shard_map/ppermute | solution.py:268
  7.4 1.3 select_reduce_fusion.slots_ref
  8.7 0.0 collective-permute-done.low_ref
  8.7 0.0 copy-start.1
  8.7 0.0 collective-permute-done.1.high_ref
  8.7 0.0 copy-start.2
  8.7 0.6 copy-done.1
  9.3 0.0 copy-done.2
  9.4 20.8 %shard_map.73 = (bf16[32,641,128]{2,1,0:T(8,128)(2,1)}, f32[1,512]{1,0:T(1,128)}, f32[1,512]{1,0:T(1,128)}, bf16[1,128]{1,0:T(2,128)(2,1)}) custom-call(s32[32]{0:T(128)} %fos_ref.1, bf16[1,160,256]{2,1,0:T(8,128)(2,1)} %copy-done.1, bf16[1,160,256]{2,1,0:T(8,128)(2,1)} %copy-done.2, bf16[32,160,256]{2,1,0:T(8,128)(2,1)} %bitcast.23, ...), custom_call_target="tpu_custom_call" | custom-call | tf_op jit(solution)/shard_map/pallas_call | solution.py:101
  30.2 1.3 broadcast_dynamic-update-slice_fusion
  31.5 131.4 %all_to_all.12 = bf16[1,32,641,128]{3,2,0,1:T(8,128)(2,1)S(1)} all-to-all(bf16[1,32,641,128]{3,2,0,1:T(8,128)(2,1)} %bitcast.22), channel_id=1, replica_groups=mesh['dp'=4,'tm'=32,'height'=2] {'tm'}, dimensions={1} | all-to-all | bytes 10502144 | tf_op jit(solution)/shard_map/all_to_all | solution.py:276
  162.9 0.0 copy-start
  162.9 2.3 %copy-done = bf16[1,32,641,128]{3,2,0,1:T(8,128)(2,1)} copy-done((bf16[1,32,641,128]{3,2,0,1:T(8,128)(2,1)}, bf16[1,32,641,128]{3,2,0,1:T(8,128)(2,1)S(1)}, u32[]{:S(2)}) %copy-start) | copy-done | bytes 5251096
  165.2 0.1 slice_reduce_fusion
  165.3 1.2 collective-permute-start.2
  166.5 0.6 compare_reduce_fusion
  167.1 0.2 collective-permute-done.2
  167.3 0.6 fusion
  168.0 0.5 scatter.9.totals_ref
  168.5 7.7 %shard_map.74 = bf16[9,160,512]{2,1,0:T(8,128)(2,1)} custom-call(s32[17]{0:T(128)} %select_reduce_fusion.slots_ref, bf16[32,641,128]{2,1,0:T(8,128)(2,1)} %bitcast.21, bf16[3,512,512]{2,1,0:T(8,128)(2,1)} %w_ref.3, f32[1,128]{1,0:T(1,128)} %scatter.9.totals_ref, f32[1,512]{1,0:T(1,128)} %bitcast.25, f32[1,512]{1,0:T(1,128)} %bitcast.26, f32[1,512]{1,0:T(1,128)} %bitcast.27), custom_call_target="tpu_custom_call" | custom-call | tf_op jit(solution)/shard_map/pallas_call | solution.py:180
  (2 shorter events, 0.0 us)
Async XLA Ops:
  0.9 7.8 %collective-permute-start = (bf16[1,160,256]{2,1,0:T(8,128)(2,1)S(1)}, bf16[1,160,256]{2,1,0:T(8,128)(2,1)S(1)}, u32[]{:S(2)}, u32[]{:S(2)}) collective-permute-start(bf16[1,160,256]{2,1,0:T(8,128)(2,1)S(1)} %get-tuple-element.40), channel_id=1, source_target_pairs={{0,1},{2,3},{4,5},{6,7},{8,9},{10,11},{12,13},{14,15},{16,17},{18,... | collective-permute-start | bytes 245768 | tf_op jit(solution)/shard_map/ppermute | solution.py:267
  2.2 6.5 %collective-permute-start.1 = (bf16[1,160,256]{2,1,0:T(8,128)(2,1)S(1)}, bf16[1,160,256]{2,1,0:T(8,128)(2,1)S(1)}, u32[]{:S(2)}, u32[]{:S(2)}) collective-permute-start(bf16[1,160,256]{2,1,0:T(8,128)(2,1)S(1)} %get-tuple-element.39), channel_id=1, source_target_pairs={{1,0},{3,2},{5,4},{7,6},{9,8},{11,10},{13,12},{15,14},{17,16},{19,... | collective-permute-start | bytes 245768 | tf_op jit(solution)/shard_map/ppermute | solution.py:268
  8.7 0.6 copy-start.1
  8.7 0.7 copy-start.2
  162.9 2.3 %copy-start = (bf16[1,32,641,128]{3,2,0,1:T(8,128)(2,1)}, bf16[1,32,641,128]{3,2,0,1:T(8,128)(2,1)S(1)}, u32[]{:S(2)}) copy-start(bf16[1,32,641,128]{3,2,0,1:T(8,128)(2,1)S(1)} %all_to_all.12) | copy-start | bytes 15753220
  165.3 2.0 %collective-permute-start.2 = (f32[64]{0:T(128)S(1)}, f32[64]{0:T(128)S(1)}, u32[]{:S(2)}, u32[]{:S(2)}) collective-permute-start(f32[64]{0:T(128)S(1)} %add.12), channel_id=1, source_target_pairs={{0,1},{1,0},{2,3},{3,2},{4,5},{5,4},{6,7},{7,6},{8,9},{9,8},{10,11... | collective-permute-start | bytes 776 | tf_op jit(solution)/shard_map/ppermute | solution.py:278

commit v14 on v11

--- a/solution.py
+++ b/solution.py
@@ -35,13 +35,23 @@
     step = pl.program_id(0)
     rows = block_ref.shape[0]
 
+    head = chunk + 1
+    first = pltpu.make_async_copy(block_ref.at[pl.ds(0, head)], x_ref.at[pl.ds(1, head)], sem.at[0])
+    rest = pltpu.make_async_copy(
+        block_ref.at[pl.ds(head, rows - head)], x_ref.at[pl.ds(head + 1, rows - head)], sem.at[1]
+    )
+
     @pl.when(step == 0)
     def _():
-        fetch = pltpu.make_async_copy(block_ref, x_ref.at[pl.ds(1, rows)], sem)
-        fetch.start()
+        first.start()
+        rest.start()
         x_ref[0:1] = low_ref[...]
         x_ref[rows + 1 : rows + 2] = high_ref[...]
-        fetch.wait()
+        first.wait()
+
+    @pl.when(step == 1)
+    def _():
+        rest.wait()
 
     base = step * chunk
     m = chunk * cols
@@ -120,7 +130,7 @@
             jax.ShapeDtypeStruct((1, cout), jnp.float32),
             jax.ShapeDtypeStruct((1, lanes), jnp.bfloat16),
         ],
-        scratch_shapes=[pltpu.VMEM((rows + 2, cols, cin), block.dtype), pltpu.SemaphoreType.DMA(())],
+        scratch_shapes=[pltpu.VMEM((rows + 2, cols, cin), block.dtype), pltpu.SemaphoreType.DMA((2,))],
         compiler_params=pltpu.CompilerParams(dimension_semantics=("arbitrary",)),
     )(frame_of_slot, low, high, block, w)
 

time: 176 us -> 175 us (level)
  no operation moved by 1% of the time
where the time goes in v14:
time: 175 us
  blocking collectives  131 us (75%)
  Pallas kernels  27.2 us (16%)
  starting transfers between devices  7.59 us (4%)
  local copies, waits for them, and re-layouts  5.74 us (3%)
  other arithmetic  2.74 us (2%)
    all_to_all x1, blocking collectives, shards(): lax.all_to_all(payload[None], 'tm', split_axis=1, concat_axis=0, tiled=True)  131 us
    pallas_call x1, Pallas kernels, conv_call(): pl.pallas_call(functools.partial(conv_kernel, chunk=chunk, cols=cols, gro...  20.2 us
    pallas_call x1, Pallas kernels, latent_call(): pl.pallas_call(functools.partial(latent_kernel, cell_count=cell_count, gr...  7 us
    ppermute x1, starting transfers between devices, shards(): high = lax.ppermute(clip_frames[0, :1], 'height', backward)  5.11 us
  transfers between devices with their start and end apart: 3, of which 1 were waited for; matrix products, arithmetic and copies ran while one was open for 1% of the time, Pallas kernels for 0%

profile of v14, /device:TPU:1, one launch (start us, length us, event | category | flops | bytes accessed | tf_op | source)
XLA Modules:
  0.0 174.9 jit_solution(15665692416176558974)
XLA Ops:
  0.0 0.9 slice_bitcast_fusion
  0.9 1.3 collective-permute-start
  2.2 5.1 %collective-permute-start.1 = (bf16[1,160,256]{2,1,0:T(8,128)(2,1)S(1)}, bf16[1,160,256]{2,1,0:T(8,128)(2,1)S(1)}, u32[]{:S(2)}, u32[]{:S(2)}) collective-permute-start(bf16[1,160,256]{2,1,0:T(8,128)(2,1)S(1)} %get-tuple-element.39), channel_id=1, source_target_pairs={{1,0},{3,2},{5,4},{7,6},{9,8},{11,10},{13,12},{15,14},{17,16},{19,... | collective-permute-start | bytes 245768 | tf_op jit(solution)/shard_map/ppermute | solution.py:264
  7.4 1.3 select_reduce_fusion.slots_ref
  8.7 0.0 collective-permute-done.low_ref
  8.7 0.0 copy-start.1
  8.7 0.0 collective-permute-done.1.high_ref
  8.7 0.0 copy-start.2
  8.7 0.6 copy-done.1
  9.3 0.0 copy-done.2
  9.4 20.2 %shard_map.73 = (bf16[32,641,128]{2,1,0:T(8,128)(2,1)}, f32[1,512]{1,0:T(1,128)}, f32[1,512]{1,0:T(1,128)}, bf16[1,128]{1,0:T(2,128)(2,1)}) custom-call(s32[32]{0:T(128)} %fos_ref.1, bf16[1,160,256]{2,1,0:T(8,128)(2,1)} %copy-done.1, bf16[1,160,256]{2,1,0:T(8,128)(2,1)} %copy-done.2, bf16[32,160,256]{2,1,0:T(8,128)(2,1)} %bitcast.23, ...), custom_call_target="tpu_custom_call" | custom-call | tf_op jit(solution)/shard_map/pallas_call | solution.py:111
  29.6 1.3 broadcast_dynamic-update-slice_fusion
  30.9 131.4 %all_to_all.12 = bf16[1,32,641,128]{3,2,0,1:T(8,128)(2,1)S(1)} all-to-all(bf16[1,32,641,128]{3,2,0,1:T(8,128)(2,1)} %bitcast.22), channel_id=1, replica_groups=mesh['dp'=4,'tm'=32,'height'=2] {'tm'}, dimensions={1} | all-to-all | bytes 10502144 | tf_op jit(solution)/shard_map/all_to_all | solution.py:272
  162.3 0.0 copy-start
  162.3 2.3 %copy-done = bf16[1,32,641,128]{3,2,0,1:T(8,128)(2,1)} copy-done((bf16[1,32,641,128]{3,2,0,1:T(8,128)(2,1)}, bf16[1,32,641,128]{3,2,0,1:T(8,128)(2,1)S(1)}, u32[]{:S(2)}) %copy-start) | copy-done | bytes 5251096
  164.6 0.1 slice_reduce_fusion
  164.7 1.2 collective-permute-start.2
  165.9 0.6 compare_reduce_fusion
  166.5 0.2 collective-permute-done.2
  166.7 0.6 fusion
  167.4 0.5 scatter.9.totals_ref
  167.9 7.0 %shard_map.74 = bf16[9,160,512]{2,1,0:T(8,128)(2,1)} custom-call(s32[17]{0:T(128)} %select_reduce_fusion.slots_ref, bf16[32,641,128]{2,1,0:T(8,128)(2,1)} %bitcast.21, bf16[3,512,512]{2,1,0:T(8,128)(2,1)} %w_ref.3, f32[1,128]{1,0:T(1,128)} %scatter.9.totals_ref, f32[1,512]{1,0:T(1,128)} %bitcast.25, f32[1,512]{1,0:T(1,128)} %bitcast.26, f32[1,512]{1,0:T(1,128)} %bitcast.27), custom_call_target="tpu_custom_call" | custom-call | tf_op jit(solution)/shard_map/pallas_call | solution.py:183
  (2 shorter events, 0.0 us)
Async XLA Ops:
  0.9 7.8 %collective-permute-start = (bf16[1,160,256]{2,1,0:T(8,128)(2,1)S(1)}, bf16[1,160,256]{2,1,0:T(8,128)(2,1)S(1)}, u32[]{:S(2)}, u32[]{:S(2)}) collective-permute-start(bf16[1,160,256]{2,1,0:T(8,128)(2,1)S(1)} %get-tuple-element.40), channel_id=1, source_target_pairs={{0,1},{2,3},{4,5},{6,7},{8,9},{10,11},{12,13},{14,15},{16,17},{18,... | collective-permute-start | bytes 245768 | tf_op jit(solution)/shard_map/ppermute | solution.py:263
  2.2 6.5 %collective-permute-start.1 = (bf16[1,160,256]{2,1,0:T(8,128)(2,1)S(1)}, bf16[1,160,256]{2,1,0:T(8,128)(2,1)S(1)}, u32[]{:S(2)}, u32[]{:S(2)}) collective-permute-start(bf16[1,160,256]{2,1,0:T(8,128)(2,1)S(1)} %get-tuple-element.39), channel_id=1, source_target_pairs={{1,0},{3,2},{5,4},{7,6},{9,8},{11,10},{13,12},{15,14},{17,16},{19,... | collective-permute-start | bytes 245768 | tf_op jit(solution)/shard_map/ppermute | solution.py:264
  8.7 0.6 copy-start.1
  8.7 0.7 copy-start.2
  162.3 2.3 %copy-start = (bf16[1,32,641,128]{3,2,0,1:T(8,128)(2,1)}, bf16[1,32,641,128]{3,2,0,1:T(8,128)(2,1)S(1)}, u32[]{:S(2)}) copy-start(bf16[1,32,641,128]{3,2,0,1:T(8,128)(2,1)S(1)} %all_to_all.12) | copy-start | bytes 15753220
  164.7 2.0 %collective-permute-start.2 = (f32[64]{0:T(128)S(1)}, f32[64]{0:T(128)S(1)}, u32[]{:S(2)}, u32[]{:S(2)}) collective-permute-start(f32[64]{0:T(128)S(1)} %add.12), channel_id=1, source_target_pairs={{0,1},{1,0},{2,3},{3,2},{4,5},{5,4},{6,7},{7,6},{8,9},{9,8},{10,11... | collective-permute-start | bytes 776 | tf_op jit(solution)/shard_map/ppermute | solution.py:274
